TPU v7x, 256 devices: a whole 4x4x8 slice. The times are simulated.
256 devices in a mesh: ep: 64 (over z, x, core), tp: 4 (over y).
Axes of the slice: x: 4, y: 4, z: 8, core: 2. Of those that a mesh axis runs over, the one named last changes fastest.
Arguments:
- tokens: bfloat16 [16384, 3584], P('ep', 'tp'), may hold values from -6 to 6
- grad_out: bfloat16 [16384, 3584], P('ep', 'tp'), may hold values from -6 to 6
- route_ids: int32 [16384, 2], P('ep'), may hold values from 0 to 63, all different within a row; in each aligned block of 256 rows (0 to 255, 256 to 511, ...) at most 16 rows name the same one
- route_probs: float32 [16384, 2], P('ep'), may hold values from 0.2 to 1
- w_gate: bfloat16 [64, 3584, 1024], P('ep', None, 'tp'), may hold values from -0.09375 to 0.09375
- w_up: bfloat16 [64, 3584, 1024], P('ep', None, 'tp'), may hold values from -0.09375 to 0.09375
- w_down: bfloat16 [64, 1024, 3584], P('ep', 'tp'), may hold values from -0.1875 to 0.1875
Outputs:
- grad_tokens: bfloat16 [16384, 3584], P('ep', 'tp')
- grad_gate: bfloat16 [64, 3584, 1024], P('ep', None, 'tp')
- grad_up: bfloat16 [64, 3584, 1024], P('ep', None, 'tp')
- grad_down: bfloat16 [64, 1024, 3584], P('ep', 'tp')
Inputs may be any that keep to these rules, and one draw needn't show every extreme that they name: `route_ids`: each token names 2 different experts. Among the tokens of one index of ep (aligned blocks of 256 tokens), no expert is named by more than 16 tokens, and in every draw some expert is named by exactly 16 of some block.
All inputs are finite; a program needn't handle non-finite values.
Results may differ from a plain program's by a relative error of at most 0.0065.
Values may be sent and summed in bfloat16 or wider, within the bound.
No kernel may reach another device: no remote copies, remote signals or barrier semaphores. Data moves between devices by JAX's collectives and lax.ppermute only.
A program may use at most 128 MiB of HBM per device.

v0:
```python
import jax
import jax.numpy as jnp
from jax import lax
from jax.experimental import pallas as pl
from jax.experimental.pallas import tpu as pltpu
from jax.sharding import PartitionSpec as P


TILES = 4
BF = jnp.bfloat16
F32 = jnp.float32


def mm(left, right, dims):
    return lax.dot_general(left, right, (dims, ((), ())), preferred_element_type=F32)


def rows_by_columns(left, right):
    return mm(left, right, ((1,), (0,)))


def pack_kernel(me, gate, up, down, *packed):
    n = len(packed)
    quarter, hid = gate.shape[1:]
    for k in range(n):
        out = packed[k]
        q = lax.rem(me[0] + n - k, n)

        @pl.loop(0, quarter // 128)
        def _(t):
            span = pl.ds(pl.multiple_of(t * 128, 128), 128)
            out[span, 0:hid] = gate[q, span, :]
            out[span, hid : 2 * hid] = up[q, span, :]
            start = pl.multiple_of(q * quarter + t * 128, 128)
            out[span, 2 * hid : 3 * hid] = down[:, pl.ds(start, 128)].T


def partial_kernel(me, own, after, last, gate, up, out):
    n, _, hid = gate.shape
    pieces = ((own, 0), (after, 1), (last, n - 1))
    for weight, first in ((gate, 0), (up, hid)):
        out[:, first : first + hid] = sum(
            rows_by_columns(x[...], weight[lax.rem(me[0] + k, n)]) for x, k in pieces
        )


def back_kernel(s, *refs):
    n = len(refs) // 2
    for k in range(n):
        out = refs[n + k]
        out[...] = rows_by_columns(s[...], refs[k][...]).astype(out.dtype)


def acts_kernel(me, far_a, far_b, partial, gate_w, up_w, *refs):
    hidden, grads, x = refs[-3:]
    step = pl.program_id(0)

    @pl.when(step < TILES // 2)
    def _():
        x[...] = far_a[...]

    @pl.when(step >= TILES // 2)
    def _():
        x[...] = far_b[...]

    hid = gate_w.shape[2]
    gate = partial[:, :hid] + rows_by_columns(x[...], gate_w[0])
    upper = partial[:, hid:] + rows_by_columns(x[...], up_w[0])
    back = sum(r[...].astype(F32) for r in refs[:-3])
    sigma = jax.nn.sigmoid(gate)
    active = gate * sigma
    hidden[...] = (active * upper).astype(BF)
    grads[:, :hid] = (back * upper * sigma * (1.0 + gate * (1.0 - sigma))).astype(BF)
    grads[:, hid:] = (back * active).astype(BF)


def dx_kernel(*refs):
    n = len(refs) // 2
    total = mm(refs[0][...], refs[n][...], ((1,), (1,)))
    for k in range(1, n):
        total += mm(refs[k][...], refs[n + k][...], ((1,), (1,)))
    refs[-1][...] = total.astype(BF)


def call(kernel, scalars, ins, outs, grid, scratch, flops, operands):
    moved = sum(a.size * a.dtype.itemsize for a in operands)
    return pl.pallas_call(
        kernel,
        out_shape=[s for s, _ in outs],
        grid_spec=pltpu.PrefetchScalarGridSpec(
            num_scalar_prefetch=scalars,
            grid=grid,
            in_specs=ins,
            out_specs=[b for _, b in outs],
            scratch_shapes=scratch,
        ),
        cost_estimate=pl.CostEstimate(flops=flops, bytes_accessed=moved, transcendentals=0),
    )(*operands)


def per_device(tokens, grad_out, route_ids, route_probs, w_gate, w_up, w_down):
    n_src = lax.axis_size("ep")
    n_tp = lax.axis_size("tp")
    me = lax.axis_index("tp")
    spot = me.astype(jnp.int32).reshape(1)
    tok_rows, quarter = tokens.shape
    top = route_ids.shape[1]
    cap = max(2, 2 * tok_rows * top // n_src)
    rows = n_src * cap
    tile = rows // TILES
    hid = w_gate.shape[2]
    shifts = range(1, n_tp)

    def fetch(a, k):
        return lax.ppermute(a, "tp", [((i + k) % n_tp, i) for i in range(n_tp)])

    def give(a, k):
        return lax.ppermute(a, "tp", [(i, (i + k) % n_tp) for i in range(n_tp)])

    def exchange(a):
        return lax.all_to_all(
            a.reshape(n_src, cap, quarter), "ep", split_axis=0, concat_axis=0, tiled=True
        ).reshape(rows, quarter)

    def by_rows(width):
        return pl.BlockSpec((tile, width), lambda i, *_: (i, 0))

    def whole(shape):
        return pl.BlockSpec(shape, lambda *_: (0,) * len(shape))

    def array(shape, kind):
        return jax.ShapeDtypeStruct(shape, kind)

    ids = route_ids.T
    probs = route_probs.T
    experts = lax.broadcasted_iota(jnp.int32, (n_src, tok_rows), 0)
    hot = [experts == ids[k : k + 1] for k in range(top)]
    named = sum(h.astype(BF) for h in hot)
    before = (
        lax.broadcasted_iota(jnp.int32, (tok_rows, tok_rows), 0)
        < lax.broadcasted_iota(jnp.int32, (tok_rows, tok_rows), 1)
    ).astype(BF)
    earlier = rows_by_columns(named, before)
    row_index = lax.broadcasted_iota(jnp.int32, (rows, tok_rows), 0)
    found = []
    for k in range(top):
        rank = jnp.sum(jnp.where(hot[k], earlier, 0.0), axis=0, keepdims=True).astype(jnp.int32)
        found.append(row_index == ids[k : k + 1] * cap + rank)
    pick = sum(f.astype(BF) for f in found)

    x_own = exchange(rows_by_columns(pick, tokens).astype(BF))
    weight = sum(
        jnp.sum(jnp.where(found[k], probs[k : k + 1], 0.0), axis=1, keepdims=True)
        for k in range(top)
    )
    s_own = exchange((rows_by_columns(pick, grad_out) * weight).astype(BF))

    gate_q = w_gate[0].reshape(n_tp, quarter, hid)
    up_q = w_up[0].reshape(n_tp, quarter, hid)
    down = w_down[0]
    packed_shape = (quarter, 3 * hid)
    packed = call(
        pack_kernel,
        1,
        [whole(gate_q.shape), whole(up_q.shape), whole(down.shape)],
        [(array(packed_shape, BF), whole(packed_shape))] * n_tp,
        (1,),
        [],
        0,
        (spot, gate_q, up_q, down),
    )
    packed = [packed[0]] + [fetch(packed[k], k) for k in shifts]

    half = rows // 2
    x_next, x_last = fetch(x_own, 1), fetch(x_own, n_tp - 1)
    far_a = fetch(x_next[:half], 1)
    far_b = fetch(x_last[half:], n_tp - 1)
    (partial,) = call(
        partial_kernel,
        1,
        [by_rows(quarter)] * 3 + [whole(gate_q.shape), whole(up_q.shape)],
        [(array((rows, 2 * hid), F32), by_rows(2 * hid))],
        (TILES,),
        [],
        12 * rows * quarter * hid,
        (spot, x_own, x_next, x_last, gate_q, up_q),
    )

    terms = call(
        back_kernel,
        0,
        [by_rows(quarter)] + [pl.BlockSpec((quarter, hid), lambda i: (0, 2))] * n_tp,
        [(array((rows, hid), BF if k else F32), by_rows(hid)) for k in range(n_tp)],
        (TILES,),
        [],
        2 * n_tp * rows * quarter * hid,
        (s_own, *packed),
    )
    terms = [terms[0]] + [give(terms[k], k) for k in shifts]
    mid = TILES // 2
    opposite = pl.BlockSpec((1, quarter, hid), lambda i, m: (lax.rem(m[0] + 2, n_tp), 0, 0))
    hidden, d_own = call(
        acts_kernel,
        1,
        [
            pl.BlockSpec((tile, quarter), lambda i, m: (jnp.minimum(i, mid - 1), 0)),
            pl.BlockSpec((tile, quarter), lambda i, m: (jnp.maximum(i - mid, 0), 0)),
            by_rows(2 * hid),
            opposite,
            opposite,
        ]
        + [by_rows(hid)] * n_tp,
        [(array((rows, hid), BF), by_rows(hid)), (array((rows, 2 * hid), BF), by_rows(2 * hid))],
        (TILES,),
        [pltpu.VMEM((tile, quarter), BF)],
        4 * rows * quarter * hid,
        (spot, far_a, far_b, partial, gate_q, up_q, *terms),
    )
    d_all = [d_own] + [fetch(d_own, k) for k in shifts]
    (dx,) = call(
        dx_kernel,
        0,
        [by_rows(2 * hid)] * n_tp
        + [pl.BlockSpec((quarter, 2 * hid), lambda i: (0, 0))] * n_tp,
        [(array((rows, quarter), BF), by_rows(quarter))],
        (TILES,),
        [],
        4 * n_tp * rows * quarter * hid,
        (*d_all, *packed),
    )
    dx = exchange(dx)
    grad_tokens = mm(pick, dx, ((0,), (0,))).astype(BF)

    x_full = jnp.zeros((rows, n_tp * quarter), BF)
    x_far = jnp.concatenate([far_a, far_b], axis=0)
    for k, piece in ((0, x_own), (1, x_next), (2, x_far), (n_tp - 1, x_last)):
        start = lax.rem(me + k, n_tp) * quarter
        x_full = lax.dynamic_update_slice_in_dim(x_full, piece, start, axis=1)
    g_gate = mm(x_full, d_own[:, :hid], ((0,), (0,))).astype(BF)
    g_up = mm(x_full, d_own[:, hid:], ((0,), (0,))).astype(BF)

    h_all = [hidden] + [fetch(hidden, k) for k in shifts]
    g_down = jnp.zeros(down.shape, BF)
    for k in range(n_tp):
        piece = mm(h_all[k], s_own, ((0,), (0,))).astype(BF)
        if k:
            piece = give(piece, k)
        start = lax.rem(me + n_tp - k, n_tp) * quarter
        g_down = lax.dynamic_update_slice_in_dim(g_down, piece, start, axis=1)

    return grad_tokens, g_gate[None], g_up[None], g_down[None]


def solution(mesh):
    placed = (
        P("ep", "tp"),
        P("ep", "tp"),
        P("ep", None),
        P("ep", None),
        P("ep", None, "tp"),
        P("ep", None, "tp"),
        P("ep", "tp", None),
    )

    return jax.shard_map(
        per_device,
        mesh=mesh,
        in_specs=placed,
        out_specs=(P("ep", "tp"), P("ep", None, "tp"), P("ep", None, "tp"), P("ep", "tp", None)),
        check_vma=False,
    )
```

profile of v0, /device:TPU:2, one launch (start us, length us, event | category | flops | bytes accessed | tf_op | source)
XLA Modules:
  0.0 345.7 jit_solution(8508635918586733968)
XLA Ops:
  0.6 0.8 fusion.27
  1.6 0.8 multiply_add_fusion.1
  2.4 1.9 convolution_convert_fusion.2
  4.3 12.1 %all-to-all-start = ((bf16[64,16,896]{2,1,0:T(8,128)(2,1)}), bf16[64,16,896]{2,1,0:T(8,128)(2,1)S(1)}, u32[]{:S(2)}, u32[]{:S(2)}) async-start(bf16[64,16,896]{2,1,0:T(8,128)(2,1)} %bitcast.65), calls=%async_computation | async-start | bytes 3670016 | tf_op jit(solution)/shard_map/all_to_all | solution.py:121
  16.5 0.3 select_reduce_fusion
  16.9 2.0 multiply_convert_fusion
  18.8 43.3 %all-to-all-done = bf16[64,16,896]{2,1,0:T(8,128)(2,1)S(1)} async-done(((bf16[64,16,896]{2,1,0:T(8,128)(2,1)}), bf16[64,16,896]{2,1,0:T(8,128)(2,1)S(1)}, u32[]{:S(2)}, u32[]{:S(2)}) %all-to-all-start) | async-done | bytes 1835040 | tf_op jit(solution)/shard_map/all_to_all | solution.py:121
  62.1 1.2 copy-done.3
  63.3 5.4 %all-to-all-start.1 = ((bf16[64,16,896]{2,1,0:T(8,128)(2,1)}), bf16[64,16,896]{2,1,0:T(8,128)(2,1)S(1)}, u32[]{:S(2)}, u32[]{:S(2)}) async-start(bf16[64,16,896]{2,1,0:T(8,128)(2,1)} %bitcast.64), calls=%async_computation.1 | async-start | bytes 3670016 | tf_op jit(solution)/shard_map/all_to_all | solution.py:121
  68.8 1.7 collective-permute-start.2
  70.4 1.7 collective-permute-start
  72.1 7.2 %shard_map.103 = (bf16[896,768]{1,0:T(8,128)(2,1)}, bf16[896,768]{1,0:T(8,128)(2,1)}, bf16[896,768]{1,0:T(8,128)(2,1)}, bf16[896,768]{1,0:T(8,128)(2,1)}) custom-call(s32[1]{0:T(128)} %bitcast.7.me, bf16[4,896,256]{2,1,0:T(8,128)(2,1)} %bitcast.52, bf16[4,896,256]{2,1,0:T(8,128)(2,1)} %bitcast.55, bf16[256,3584]{1,0:T(8,128)(2,1)} %bitcast.66), custom_call_target="tpu_custom_call" | custom-call | bytes 5505028 | tf_op jit(solution)/shard_map/pallas_call | solution.py:87
  79.3 1.8 collective-permute-start.4
  81.1 0.6 collective-permute-start.5
  81.7 1.0 collective-permute-start.6
  82.7 31.0 %collective-permute-done.2.last = bf16[1024,896]{1,0:T(8,128)(2,1)} collective-permute-done((bf16[1024,896]{1,0:T(8,128)(2,1)}, bf16[1024,896]{1,0:T(8,128)(2,1)}, u32[]{:S(2)}, u32[]{:S(2)}) %collective-permute-start.2) | collective-permute-done | bytes 1835040 | tf_op jit(solution)/shard_map/ppermute | solution.py:115
  113.7 2.2 slice.37
  115.9 28.1 %collective-permute-start.3 = (bf16[512,896]{1,0:T(8,128)(2,1)}, bf16[512,896]{1,0:T(8,128)(2,1)S(1)}, u32[]{:S(2)}, u32[]{:S(2)}) collective-permute-start(bf16[512,896]{1,0:T(8,128)(2,1)} %slice.37), channel_id=1, source_target_pairs={{3,0},{0,1},{1,2},{2,3},{7,4},{4,5},{5,6},{6,7},{11,8},{8,9},{9,10... | collective-permute-start | bytes 2752520 | tf_op jit(solution)/shard_map/ppermute | solution.py:115
  144.0 2.2 slice.36
  146.2 25.3 %collective-permute-done.4.refs_1_.refs_5_ = bf16[896,768]{1,0:T(8,128)(2,1)S(1)} collective-permute-done((bf16[896,768]{1,0:T(8,128)(2,1)}, bf16[896,768]{1,0:T(8,128)(2,1)S(1)}, u32[]{:S(2)}, u32[]{:S(2)}) %collective-permute-start.4) | collective-permute-done | bytes 1376288 | tf_op jit(solution)/shard_map/ppermute | solution.py:115
  171.5 1.1 copy-done.7
  172.6 1.1 copy-done.8
  173.7 1.2 copy-done.1
  174.9 5.6 %shard_map.104 = (f32[1024,256]{1,0:T(8,128)}, bf16[1024,256]{1,0:T(8,128)(2,1)}, bf16[1024,256]{1,0:T(8,128)(2,1)}, bf16[1024,256]{1,0:T(8,128)(2,1)}) custom-call(bf16[1024,896]{1,0:T(8,128)(2,1)} %bitcast.47, bf16[896,768]{1,0:T(8,128)(2,1)} %get-tuple-element.14.refs_0_.refs_4_, bf16[896,768]{1,0:T(8,128)(2,1)} %copy-done.7, bf16[896,768]{1,0:T(8,128)(2,1)} %copy-done.8, ...), custom_call_target="tpu_custom_call" | custom-call | flops 1879048192 | bytes 7340032 | tf_op jit(solution)/shard_map/pallas_call | solution.py:87
  180.5 2.3 collective-permute-start.7
  182.8 3.1 collective-permute-start.8
  185.9 8.0 %shard_map.102.partial = f32[1024,512]{1,0:T(8,128)} custom-call(s32[1]{0:T(128)} %bitcast.7.me, bf16[1024,896]{1,0:T(8,128)(2,1)} %bitcast.60, bf16[1024,896]{1,0:T(8,128)(2,1)} %collective-permute-done.after, bf16[1024,896]{1,0:T(8,128)(2,1)} %collective-permute-done.2.last, bf16[4,896,256]{2,1,0:T(8,128)(2,1)} %bitcast.53, bf16[4,896,256]{2,1,0:T(8,128)(2,1)} %bitcast.56), custom_call_target="tpu_custom_call" | custom-call | flops 2818572288 | bytes 9175044 | tf_op jit(solution)/shard_map/pallas_call | solution.py:87
  193.9 8.3 %collective-permute-done.7.refs_1_ = bf16[1024,256]{1,0:T(8,128)(2,1)S(1)} collective-permute-done((bf16[1024,256]{1,0:T(8,128)(2,1)}, bf16[1024,256]{1,0:T(8,128)(2,1)S(1)}, u32[]{:S(2)}, u32[]{:S(2)}) %collective-permute-start.7) | collective-permute-done | bytes 524320 | tf_op jit(solution)/shard_map/ppermute | solution.py:118
  202.3 12.5 %collective-permute-done.8.refs_2_ = bf16[1024,256]{1,0:T(8,128)(2,1)S(1)} collective-permute-done((bf16[1024,256]{1,0:T(8,128)(2,1)}, bf16[1024,256]{1,0:T(8,128)(2,1)S(1)}, u32[]{:S(2)}, u32[]{:S(2)}) %collective-permute-start.8) | collective-permute-done | bytes 524320 | tf_op jit(solution)/shard_map/ppermute | solution.py:118
  214.8 0.7 copy-done.10
  215.7 0.3 copy-done.5
  216.0 6.0 %shard_map.105 = (bf16[1024,256]{1,0:T(8,128)(2,1)}, bf16[1024,512]{1,0:T(8,128)(2,1)}) custom-call(s32[1]{0:T(128)} %bitcast.7.me, bf16[512,896]{1,0:T(8,128)(2,1)} %collective-permute-done.1.far_a, bf16[512,896]{1,0:T(8,128)(2,1)} %copy-done.5, f32[1024,512]{1,0:T(8,128)} %shard_map.102.partial, bf16[4,896,256]{2,1,0:T(8,128)(2,1)} %bitcast.54, ...), custom_call_target="tpu_custom_call" | custom-call | flops 939524096 | bytes 10223620 | tf_op jit(solution)/shard_map/pallas_call | solution.py:87
  222.3 2.9 collective-permute-start.11
  225.2 1.1 collective-permute-start.10
  226.3 3.4 broadcast_in_dim.58
  229.7 1.4 constant_dynamic-update-slice_fusion.2
  231.1 2.9 constant_dynamic-update-slice_fusion.1
  234.0 0.9 collective-permute-start.17
  234.9 1.0 collective-permute-start.15
  235.9 36.1 %collective-permute-done.12.refs_3_ = bf16[1024,512]{1,0:T(8,128)(2,1)S(1)} collective-permute-done((bf16[1024,512]{1,0:T(8,128)(2,1)}, bf16[1024,512]{1,0:T(8,128)(2,1)S(1)}, u32[]{:S(2)}, u32[]{:S(2)}) %collective-permute-start.12) | collective-permute-done | bytes 1048608 | tf_op jit(solution)/shard_map/ppermute | solution.py:115
  272.0 0.9 collective-permute-done.10.refs_1_
  273.0 0.3 copy-done.15
  273.3 8.5 %shard_map.106 = bf16[1024,896]{1,0:T(8,128)(2,1)} custom-call(bf16[1024,512]{1,0:T(8,128)(2,1)} %get-tuple-element.22.refs_0_, bf16[1024,512]{1,0:T(8,128)(2,1)} %collective-permute-done.10.refs_1_, bf16[1024,512]{1,0:T(8,128)(2,1)} %copy-done.15, bf16[1024,512]{1,0:T(8,128)(2,1)} %copy-done.14, bf16[896,768]{1,0:T(8,128)(2,1)} %get-tuple-element.14.refs_0_.refs_4_, ...), custom_call_target="tpu_custom_call" | custom-call | flops 3758096384 | bytes 9699328 | tf_op jit(solution)/shard_map/pallas_call | solution.py:87
  281.8 10.4 %all-to-all-start.2 = ((bf16[64,16,896]{2,1,0:T(8,128)(2,1)}), bf16[64,16,896]{2,1,0:T(8,128)(2,1)S(1)}, u32[]{:S(2)}, u32[]{:S(2)}) async-start(bf16[64,16,896]{2,1,0:T(8,128)(2,1)} %bitcast.62), calls=%async_computation.2 | async-start | bytes 3670016 | tf_op jit(solution)/shard_map/all_to_all | solution.py:121
  292.3 2.6 maximum_dynamic-update-slice_fusion
  294.8 3.0 constant_dynamic-update-slice_fusion
  297.8 6.5 %fusion.1 = bf16[1,3584,256]{2,1,0:T(8,128)(2,1)} fusion(bf16[1024,3584]{1,0:T(8,128)(2,1)} %constant_dynamic-update-slice_fusion, bf16[1024,512]{1,0:T(8,128)(2,1)S(1)} %copy-done.13), kind=kOutput, calls=%fused_computation.3 | convolution fusion | flops 1879965696 | bytes 9699328 | tf_op jit(solution)/shard_map/dot_general | solution.py:15
  304.3 6.4 %fusion = bf16[1,3584,256]{2,1,0:T(8,128)(2,1)} fusion(bf16[1024,3584]{1,0:T(8,128)(2,1)} %constant_dynamic-update-slice_fusion, bf16[1024,512]{1,0:T(8,128)(2,1)S(1)} %copy-done.13), kind=kOutput, calls=%fused_computation.2 | convolution fusion | flops 1879965696 | bytes 9699328 | tf_op jit(solution)/shard_map/dot_general | solution.py:15
  310.7 1.3 broadcast_in_dim.61
  312.1 0.8 copy-done.2
  312.9 2.5 fusion.3
  315.4 1.8 convolution_convert_fusion.5
  317.2 1.8 collective-permute-start.14
  319.0 1.8 convolution_convert_fusion.4
  320.8 2.3 collective-permute-start.16
  323.1 1.8 convolution_convert_fusion.3
  324.9 0.6 collective-permute-start.18
  325.4 5.8 %collective-permute-done.14 = bf16[256,896]{1,0:T(8,128)(2,1)S(1)} collective-permute-done((bf16[256,896]{1,0:T(8,128)(2,1)S(1)}, bf16[256,896]{1,0:T(8,128)(2,1)S(1)}, u32[]{:S(2)}, u32[]{:S(2)}) %collective-permute-start.14) | collective-permute-done | bytes 458784 | tf_op jit(solution)/shard_map/ppermute | solution.py:118
  331.2 0.8 bitcast_dynamic-update-slice_fusion.2
  332.0 9.5 %collective-permute-done.16 = bf16[256,896]{1,0:T(8,128)(2,1)S(1)} collective-permute-done((bf16[256,896]{1,0:T(8,128)(2,1)S(1)}, bf16[256,896]{1,0:T(8,128)(2,1)S(1)}, u32[]{:S(2)}, u32[]{:S(2)}) %collective-permute-start.16) | collective-permute-done | bytes 458784 | tf_op jit(solution)/shard_map/ppermute | solution.py:118
  341.6 0.8 bitcast_dynamic-update-slice_fusion.1
  342.4 1.0 collective-permute-done.18
  343.4 0.8 bitcast_dynamic-update-slice_fusion
  344.2 1.5 convolution_convert_fusion.7
  (47 shorter events, 0.7 us)
Async XLA Ops:
  0.6 1.7 copy-start
  4.3 12.2 %copy-start.12 = (f32[256,2]{0,1:T(2,128)S(1)}, f32[256,2]{0,1:T(2,128)}, u32[]{:S(2)}) copy-start(f32[256,2]{0,1:T(2,128)} %param.10) | copy-start | bytes 6148
  4.3 12.5 %copy-start.16 = (bf16[256,896]{1,0:T(8,128)(2,1)S(1)}, bf16[256,896]{1,0:T(8,128)(2,1)}, u32[]{:S(2)}) copy-start(bf16[256,896]{1,0:T(8,128)(2,1)} %param.8) | copy-start | bytes 1376260
  4.3 57.8 %all-to-all-start = ((bf16[64,16,896]{2,1,0:T(8,128)(2,1)}), bf16[64,16,896]{2,1,0:T(8,128)(2,1)S(1)}, u32[]{:S(2)}, u32[]{:S(2)}) async-start(bf16[64,16,896]{2,1,0:T(8,128)(2,1)} %bitcast.65), calls=%async_computation | async-start | bytes 3670016 | tf_op jit(solution)/shard_map/all_to_all | solution.py:121
  62.1 1.2 copy-start.3
  63.3 110.3 %all-to-all-start.1 = ((bf16[64,16,896]{2,1,0:T(8,128)(2,1)}), bf16[64,16,896]{2,1,0:T(8,128)(2,1)S(1)}, u32[]{:S(2)}, u32[]{:S(2)}) async-start(bf16[64,16,896]{2,1,0:T(8,128)(2,1)} %bitcast.64), calls=%async_computation.1 | async-start | bytes 3670016 | tf_op jit(solution)/shard_map/all_to_all | solution.py:121
  68.8 44.9 %collective-permute-start.2 = (bf16[1024,896]{1,0:T(8,128)(2,1)}, bf16[1024,896]{1,0:T(8,128)(2,1)}, u32[]{:S(2)}, u32[]{:S(2)}) collective-permute-start(bf16[1024,896]{1,0:T(8,128)(2,1)} %bitcast.58), channel_id=1, source_target_pairs={{3,0},{0,1},{1,2},{2,3},{7,4},{4,5},{5,6},{6,7},{11,8},{8,9},{9,10... | collective-permute-start | bytes 5505032 | tf_op jit(solution)/shard_map/ppermute | solution.py:115
  70.4 73.5 %collective-permute-start = (bf16[1024,896]{1,0:T(8,128)(2,1)}, bf16[1024,896]{1,0:T(8,128)(2,1)}, u32[]{:S(2)}, u32[]{:S(2)}) collective-permute-start(bf16[1024,896]{1,0:T(8,128)(2,1)} %bitcast.59), channel_id=1, source_target_pairs={{1,0},{2,1},{3,2},{0,3},{5,4},{6,5},{7,6},{4,7},{9,8},{10,9},{11,1... | collective-permute-start | bytes 5505032 | tf_op jit(solution)/shard_map/ppermute | solution.py:115
  79.3 92.2 %collective-permute-start.4 = (bf16[896,768]{1,0:T(8,128)(2,1)}, bf16[896,768]{1,0:T(8,128)(2,1)S(1)}, u32[]{:S(2)}, u32[]{:S(2)}) collective-permute-start(bf16[896,768]{1,0:T(8,128)(2,1)} %get-tuple-element.15), channel_id=1, source_target_pairs={{1,0},{2,1},{3,2},{0,3},{5,4},{6,5},{7,6},{4,7},{9,8},{10,9},{11,1... | collective-permute-start | bytes 4128776 | tf_op jit(solution)/shard_map/ppermute | solution.py:115
  81.1 90.4 %collective-permute-start.5 = (bf16[896,768]{1,0:T(8,128)(2,1)}, bf16[896,768]{1,0:T(8,128)(2,1)S(1)}, u32[]{:S(2)}, u32[]{:S(2)}) collective-permute-start(bf16[896,768]{1,0:T(8,128)(2,1)} %get-tuple-element.16), channel_id=1, source_target_pairs={{2,0},{3,1},{0,2},{1,3},{6,4},{7,5},{4,6},{5,7},{10,8},{11,9},{8,1... | collective-permute-start | bytes 4128776 | tf_op jit(solution)/shard_map/ppermute | solution.py:115
  81.7 91.9 %collective-permute-start.6 = (bf16[896,768]{1,0:T(8,128)(2,1)}, bf16[896,768]{1,0:T(8,128)(2,1)}, u32[]{:S(2)}, u32[]{:S(2)}) collective-permute-start(bf16[896,768]{1,0:T(8,128)(2,1)} %get-tuple-element.17), channel_id=1, source_target_pairs={{3,0},{0,1},{1,2},{2,3},{7,4},{4,5},{5,6},{6,7},{11,8},{8,9},{9,10... | collective-permute-start | bytes 4128776 | tf_op jit(solution)/shard_map/ppermute | solution.py:115
  115.9 98.8 %collective-permute-start.3 = (bf16[512,896]{1,0:T(8,128)(2,1)}, bf16[512,896]{1,0:T(8,128)(2,1)S(1)}, u32[]{:S(2)}, u32[]{:S(2)}) collective-permute-start(bf16[512,896]{1,0:T(8,128)(2,1)} %slice.37), channel_id=1, source_target_pairs={{3,0},{0,1},{1,2},{2,3},{7,4},{4,5},{5,6},{6,7},{11,8},{8,9},{9,10... | collective-permute-start | bytes 2752520 | tf_op jit(solution)/shard_map/ppermute | solution.py:115
  146.2 68.6 %collective-permute-start.1 = (bf16[512,896]{1,0:T(8,128)(2,1)}, bf16[512,896]{1,0:T(8,128)(2,1)}, u32[]{:S(2)}, u32[]{:S(2)}) collective-permute-start(bf16[512,896]{1,0:T(8,128)(2,1)} %slice.36), channel_id=1, source_target_pairs={{1,0},{2,1},{3,2},{0,3},{5,4},{6,5},{7,6},{4,7},{9,8},{10,9},{11,1... | collective-permute-start | bytes 2752520 | tf_op jit(solution)/shard_map/ppermute | solution.py:115
  171.4 1.1 copy-start.7
  172.6 1.1 copy-start.8
  173.7 1.2 copy-start.1
  180.5 21.7 %collective-permute-start.7 = (bf16[1024,256]{1,0:T(8,128)(2,1)}, bf16[1024,256]{1,0:T(8,128)(2,1)S(1)}, u32[]{:S(2)}, u32[]{:S(2)}) collective-permute-start(bf16[1024,256]{1,0:T(8,128)(2,1)} %get-tuple-element.19), channel_id=1, source_target_pairs={{0,1},{1,2},{2,3},{3,0},{4,5},{5,6},{6,7},{7,4},{8,9},{9,10},{10,1... | collective-permute-start | bytes 1572872 | tf_op jit(solution)/shard_map/ppermute | solution.py:118
  182.8 31.9 %collective-permute-start.8 = (bf16[1024,256]{1,0:T(8,128)(2,1)}, bf16[1024,256]{1,0:T(8,128)(2,1)S(1)}, u32[]{:S(2)}, u32[]{:S(2)}) collective-permute-start(bf16[1024,256]{1,0:T(8,128)(2,1)} %get-tuple-element.20), channel_id=1, source_target_pairs={{0,2},{1,3},{2,0},{3,1},{4,6},{5,7},{6,4},{7,5},{8,10},{9,11},{10,... | collective-permute-start | bytes 1572872 | tf_op jit(solution)/shard_map/ppermute | solution.py:118
  185.9 28.8 %collective-permute-start.9 = (bf16[1024,256]{1,0:T(8,128)(2,1)}, bf16[1024,256]{1,0:T(8,128)(2,1)S(1)}, u32[]{:S(2)}, u32[]{:S(2)}) collective-permute-start(bf16[1024,256]{1,0:T(8,128)(2,1)} %get-tuple-element.21), channel_id=1, source_target_pairs={{0,3},{1,0},{2,1},{3,2},{4,7},{5,4},{6,5},{7,6},{8,11},{9,8},{10,9... | collective-permute-start | bytes 1572872 | tf_op jit(solution)/shard_map/ppermute | solution.py:118
  202.3 12.5 %copy-start.9 = (bf16[1024,256]{1,0:T(8,128)(2,1)}, bf16[1024,256]{1,0:T(8,128)(2,1)S(1)}, u32[]{:S(2)}) copy-start(bf16[1024,256]{1,0:T(8,128)(2,1)S(1)} %collective-permute-done.7.refs_1_) | copy-start | bytes 1572868
  214.7 0.8 copy-start.10
  214.7 1.0 copy-start.11
  214.7 1.3 copy-start.5
  222.0 49.9 %collective-permute-start.12 = (bf16[1024,512]{1,0:T(8,128)(2,1)}, bf16[1024,512]{1,0:T(8,128)(2,1)S(1)}, u32[]{:S(2)}, u32[]{:S(2)}) collective-permute-start(bf16[1024,512]{1,0:T(8,128)(2,1)} %get-tuple-element.22.refs_0_), channel_id=1, source_target_pairs={{3,0},{0,1},{1,2},{2,3},{7,4},{4,5},{5,6},{6,7},{11,8},{8,9},{9,10... | collective-permute-start | bytes 3145736 | tf_op jit(solution)/shard_map/ppermute | solution.py:115
  222.3 49.7 %collective-permute-start.11 = (bf16[1024,512]{1,0:T(8,128)(2,1)}, bf16[1024,512]{1,0:T(8,128)(2,1)S(1)}, u32[]{:S(2)}, u32[]{:S(2)}) collective-permute-start(bf16[1024,512]{1,0:T(8,128)(2,1)} %get-tuple-element.22.refs_0_), channel_id=1, source_target_pairs={{2,0},{3,1},{0,2},{1,3},{6,4},{7,5},{4,6},{5,7},{10,8},{11,9},{8,1... | collective-permute-start | bytes 3145736 | tf_op jit(solution)/shard_map/ppermute | solution.py:115
  225.2 47.8 %collective-permute-start.10 = (bf16[1024,512]{1,0:T(8,128)(2,1)}, bf16[1024,512]{1,0:T(8,128)(2,1)}, u32[]{:S(2)}, u32[]{:S(2)}) collective-permute-start(bf16[1024,512]{1,0:T(8,128)(2,1)} %get-tuple-element.22.refs_0_), channel_id=1, source_target_pairs={{1,0},{2,1},{3,2},{0,3},{5,4},{6,5},{7,6},{4,7},{9,8},{10,9},{11,1... | collective-permute-start | bytes 3145736 | tf_op jit(solution)/shard_map/ppermute | solution.py:115
  226.3 3.4 copy-start.4
  234.0 89.0 %collective-permute-start.17 = (bf16[1024,256]{1,0:T(8,128)(2,1)}, bf16[1024,256]{1,0:T(8,128)(2,1)}, u32[]{:S(2)}, u32[]{:S(2)}) collective-permute-start(bf16[1024,256]{1,0:T(8,128)(2,1)} %get-tuple-element.23), channel_id=1, source_target_pairs={{3,0},{0,1},{1,2},{2,3},{7,4},{4,5},{5,6},{6,7},{11,8},{8,9},{9,10... | collective-permute-start | bytes 1572872 | tf_op jit(solution)/shard_map/ppermute | solution.py:115
  234.9 84.1 %collective-permute-start.15 = (bf16[1024,256]{1,0:T(8,128)(2,1)}, bf16[1024,256]{1,0:T(8,128)(2,1)}, u32[]{:S(2)}, u32[]{:S(2)}) collective-permute-start(bf16[1024,256]{1,0:T(8,128)(2,1)} %get-tuple-element.23), channel_id=1, source_target_pairs={{2,0},{3,1},{0,2},{1,3},{6,4},{7,5},{4,6},{5,7},{10,8},{11,9},{8,1... | collective-permute-start | bytes 1572872 | tf_op jit(solution)/shard_map/ppermute | solution.py:115
  272.0 1.0 copy-start.14
  272.0 43.5 %collective-permute-start.13 = (bf16[1024,256]{1,0:T(8,128)(2,1)}, bf16[1024,256]{1,0:T(8,128)(2,1)}, u32[]{:S(2)}, u32[]{:S(2)}) collective-permute-start(bf16[1024,256]{1,0:T(8,128)(2,1)} %get-tuple-element.23), channel_id=1, source_target_pairs={{1,0},{2,1},{3,2},{0,3},{5,4},{6,5},{7,6},{4,7},{9,8},{10,9},{11,1... | collective-permute-start | bytes 1572872 | tf_op jit(solution)/shard_map/ppermute | solution.py:115
  272.0 1.3 copy-start.15
  281.8 10.5 %copy-start.6 = (bf16[512,896]{1,0:T(8,128)(2,1)S(1)}, bf16[512,896]{1,0:T(8,128)(2,1)}, u32[]{:S(2)}) copy-start(bf16[512,896]{1,0:T(8,128)(2,1)} %copy-done.5) | copy-start | bytes 2752516
  281.8 62.4 %all-to-all-start.2 = ((bf16[64,16,896]{2,1,0:T(8,128)(2,1)}), bf16[64,16,896]{2,1,0:T(8,128)(2,1)S(1)}, u32[]{:S(2)}, u32[]{:S(2)}) async-start(bf16[64,16,896]{2,1,0:T(8,128)(2,1)} %bitcast.62), calls=%async_computation.2 | async-start | bytes 3670016 | tf_op jit(solution)/shard_map/all_to_all | solution.py:121
  294.8 3.0 copy-start.13
  310.7 2.2 copy-start.2
  317.2 14.0 %collective-permute-start.14 = (bf16[256,896]{1,0:T(8,128)(2,1)S(1)}, bf16[256,896]{1,0:T(8,128)(2,1)S(1)}, u32[]{:S(2)}, u32[]{:S(2)}) collective-permute-start(bf16[256,896]{1,0:T(8,128)(2,1)S(1)} %convolution_convert_fusion.5), channel_id=1, source_target_pairs={{0,1},{1,2},{2,3},{3,0},{4,5},{5,6},{6,7},{7,4},{8,9},{9,10},{10,1... | collective-permute-start | bytes 1376264 | tf_op jit(solution)/shard_map/ppermute | solution.py:118
  320.8 20.8 %collective-permute-start.16 = (bf16[256,896]{1,0:T(8,128)(2,1)S(1)}, bf16[256,896]{1,0:T(8,128)(2,1)S(1)}, u32[]{:S(2)}, u32[]{:S(2)}) collective-permute-start(bf16[256,896]{1,0:T(8,128)(2,1)S(1)} %convolution_convert_fusion.4), channel_id=1, source_target_pairs={{0,2},{1,3},{2,0},{3,1},{4,6},{5,7},{6,4},{7,5},{8,10},{9,11},{10,... | collective-permute-start | bytes 1376264 | tf_op jit(solution)/shard_map/ppermute | solution.py:118
  324.9 18.5 %collective-permute-start.18 = (bf16[256,896]{1,0:T(8,128)(2,1)S(1)}, bf16[256,896]{1,0:T(8,128)(2,1)S(1)}, u32[]{:S(2)}, u32[]{:S(2)}) collective-permute-start(bf16[256,896]{1,0:T(8,128)(2,1)S(1)} %convolution_convert_fusion.3), channel_id=1, source_target_pairs={{0,3},{1,0},{2,1},{3,2},{4,7},{5,4},{6,5},{7,6},{8,11},{9,8},{10,9... | collective-permute-start | bytes 1376264 | tf_op jit(solution)/shard_map/ppermute | solution.py:118
where the time goes:
time: 347 us; the launch traced here: 346 us
  waiting for transfers between devices  174 us (50%)
  starting transfers between devices  79 us (23%)
  Pallas kernels  35.4 us (10%)
  local copies, waits for them, and re-layouts  26.7 us (8%)
  matrix products  26.4 us (8%)
  other arithmetic  3.72 us (1%)
    ppermute x13, waiting for transfers between devices, fetch(): return lax.ppermute(a, 'tp', [((i + k) % n_tp, i) for i in range(n_tp)])  93.4 us
    all_to_all x3, waiting for transfers between devices, exchange(): lax.all_to_all(a.reshape(n_src, cap, quarter), 'ep', split_axis=0, concat...  43.3 us
    ppermute x13, starting transfers between devices, fetch(): return lax.ppermute(a, 'tp', [((i + k) % n_tp, i) for i in range(n_tp)])  40.9 us
    ppermute x6, waiting for transfers between devices, give(): return lax.ppermute(a, 'tp', [(i, (i + k) % n_tp) for i in range(n_tp)])  37.1 us
    pallas_call x5, Pallas kernels, call(): pl.pallas_call(kernel, out_shape=[s for s, _ in outs], grid_spec=pltpu.Pr...  35.4 us
    all_to_all x3, starting transfers between devices, exchange(): lax.all_to_all(a.reshape(n_src, cap, quarter), 'ep', split_axis=0, concat...  28 us
    dot_general x10, matrix products, mm(): lax.dot_general(left, right, (dims, ((), ())), preferred_element_type=F32)  26.4 us
    ppermute x6, starting transfers between devices, give(): return lax.ppermute(a, 'tp', [(i, (i + k) % n_tp) for i in range(n_tp)])  10 us
  transfers between devices with their start and end apart: 22, of which 10 were waited for; matrix products, arithmetic and copies ran while one was open for 13% of the time, Pallas kernels for 8%

commit v1 on v0

--- a/solution.py
+++ b/solution.py
@@ -7,6 +7,7 @@
 
 
 TILES = 4
+CHUNKS = 2
 BF = jnp.bfloat16
 F32 = jnp.float32
 
@@ -21,18 +22,15 @@
 
 def pack_kernel(me, gate, up, down, *packed):
     n = len(packed)
-    quarter, hid = gate.shape[1:]
+    step = pl.program_id(0)
+    span, hid = gate.shape[1:]
+    width = down.shape[1] // n
     for k in range(n):
-        out = packed[k]
         q = lax.rem(me[0] + n - k, n)
-
-        @pl.loop(0, quarter // 128)
-        def _(t):
-            span = pl.ds(pl.multiple_of(t * 128, 128), 128)
-            out[span, 0:hid] = gate[q, span, :]
-            out[span, hid : 2 * hid] = up[q, span, :]
-            start = pl.multiple_of(q * quarter + t * 128, 128)
-            out[span, 2 * hid : 3 * hid] = down[:, pl.ds(start, 128)].T
+        packed[k][:, 0:hid] = gate[q]
+        packed[k][:, hid : 2 * hid] = up[q]
+        start = pl.multiple_of(q * width + step * span, 128)
+        packed[k][:, 2 * hid : 3 * hid] = down[:, pl.ds(start, span)].T
 
 
 def partial_kernel(me, own, after, last, gate, up, out):
@@ -119,8 +117,8 @@
 
     def exchange(a):
         return lax.all_to_all(
-            a.reshape(n_src, cap, quarter), "ep", split_axis=0, concat_axis=0, tiled=True
-        ).reshape(rows, quarter)
+            a.reshape(n_src, -1, quarter), "ep", split_axis=0, concat_axis=0, tiled=True
+        ).reshape(-1, quarter)
 
     def by_rows(width):
         return pl.BlockSpec((tile, width), lambda i, *_: (i, 0))
@@ -141,11 +139,20 @@
         < lax.broadcasted_iota(jnp.int32, (tok_rows, tok_rows), 1)
     ).astype(BF)
     earlier = rows_by_columns(named, before)
-    row_index = lax.broadcasted_iota(jnp.int32, (rows, tok_rows), 0)
-    found = []
-    for k in range(top):
-        rank = jnp.sum(jnp.where(hot[k], earlier, 0.0), axis=0, keepdims=True).astype(jnp.int32)
-        found.append(row_index == ids[k : k + 1] * cap + rank)
+    ranks = [
+        jnp.sum(jnp.where(h, earlier, 0.0), axis=0, keepdims=True).astype(jnp.int32) for h in hot
+    ]
+
+    def places(first, count):
+        row_index = lax.broadcasted_iota(jnp.int32, (n_src * count, tok_rows), 0)
+        at = []
+        for k in range(top):
+            rank = ranks[k] - first
+            inside = (rank >= 0) & (rank < count)
+            at.append(row_index == jnp.where(inside, ids[k : k + 1] * count + rank, -1))
+        return at
+
+    found = places(0, cap)
     pick = sum(f.astype(BF) for f in found)
 
     x_own = exchange(rows_by_columns(pick, tokens).astype(BF))
@@ -158,13 +165,14 @@
     gate_q = w_gate[0].reshape(n_tp, quarter, hid)
     up_q = w_up[0].reshape(n_tp, quarter, hid)
     down = w_down[0]
-    packed_shape = (quarter, 3 * hid)
+    by_span = pl.BlockSpec((n_tp, 128, hid), lambda i, m: (0, i, 0))
     packed = call(
         pack_kernel,
         1,
-        [whole(gate_q.shape), whole(up_q.shape), whole(down.shape)],
-        [(array(packed_shape, BF), whole(packed_shape))] * n_tp,
-        (1,),
+        [by_span, by_span, whole(down.shape)],
+        [(array((quarter, 3 * hid), BF), pl.BlockSpec((128, 3 * hid), lambda i, m: (i, 0)))]
+        * n_tp,
+        (quarter // 128,),
         [],
         0,
         (spot, gate_q, up_q, down),
@@ -216,20 +224,27 @@
         4 * rows * quarter * hid,
         (spot, far_a, far_b, partial, gate_q, up_q, *terms),
     )
-    d_all = [d_own] + [fetch(d_own, k) for k in shifts]
-    (dx,) = call(
-        dx_kernel,
-        0,
-        [by_rows(2 * hid)] * n_tp
-        + [pl.BlockSpec((quarter, 2 * hid), lambda i: (0, 0))] * n_tp,
-        [(array((rows, quarter), BF), by_rows(quarter))],
-        (TILES,),
-        [],
-        4 * n_tp * rows * quarter * hid,
-        (*d_all, *packed),
-    )
-    dx = exchange(dx)
-    grad_tokens = mm(pick, dx, ((0,), (0,))).astype(BF)
+    part = cap // CHUNKS
+    grad_tokens = 0.0
+    for c in range(CHUNKS):
+        d_part = d_own.reshape(n_src, cap, 2 * hid)[:, c * part : (c + 1) * part]
+        d_part = d_part.reshape(n_src * part, 2 * hid)
+        d_all = [d_part] + [fetch(d_part, k) for k in shifts]
+        (dx,) = call(
+            dx_kernel,
+            0,
+            [by_rows(2 * hid)] * n_tp
+            + [pl.BlockSpec((quarter, 2 * hid), lambda i: (0, 0))] * n_tp,
+            [(array((n_src * part, quarter), BF), by_rows(quarter))],
+            (TILES // CHUNKS,),
+            [],
+            4 * n_tp * n_src * part * quarter * hid,
+            (*d_all, *packed),
+        )
+        dx = exchange(dx)
+        spots = sum(f.astype(BF) for f in places(c * part, part))
+        grad_tokens += mm(spots, dx, ((0,), (0,)))
+    grad_tokens = grad_tokens.astype(BF)
 
     x_full = jnp.zeros((rows, n_tp * quarter), BF)
     x_far = jnp.concatenate([far_a, far_b], axis=0)

time: 347 us -> 348 us (level)
  waiting for transfers between devices: 174 us -> 153 us
  starting transfers between devices: 79 us -> 94.5 us
    ppermute x13 -> x16, waiting for transfers between devices: 93.4 us -> 70.8 us  [fetch(): return lax.ppermute(a, 'tp', [((i + k) % n_tp, i) for i in range(n_tp)])]
    all_to_all x3 -> x4, starting transfers between devices: 28 us -> 37.5 us  [exchange(): lax.all_to_all(a.reshape(n_src, -1, quarter), 'ep', split_axis=0, concat_...]
    ppermute x13 -> x16, starting transfers between devices: 40.9 us -> 47.4 us  [fetch(): return lax.ppermute(a, 'tp', [((i + k) % n_tp, i) for i in range(n_tp)])]
    pallas_call x5 -> x6, Pallas kernels: 35.4 us -> 38.5 us  [call(): pl.pallas_call(kernel, out_shape=[s for s, _ in outs], grid_spec=pltpu.Pr...]
    dot_general x10 -> x11, matrix products: 26.4 us -> 27.8 us  [mm(): lax.dot_general(left, right, (dims, ((), ())), preferred_element_type=F32)]
    all_to_all x3 -> x4, waiting for transfers between devices: 43.3 us -> 44.3 us  [exchange(): lax.all_to_all(a.reshape(n_src, -1, quarter), 'ep', split_axis=0, concat_...]
    unnamed x34 -> x38, local copies, waits for them, and re-layouts: 7.09 us -> 6.8 us
  transfers between devices with their start and end apart: 22 -> 26, of which waited for: 10 -> 10; matrix products, arithmetic and copies ran while one was open for 13% -> 13% of each run, Pallas kernels for 8% -> 9%
where the time goes in v1:
time: 348 us; the launch traced here: 347 us
  waiting for transfers between devices  153 us (44%)
  starting transfers between devices  94.5 us (27%)
  Pallas kernels  38.5 us (11%)
  local copies, waits for them, and re-layouts  28.6 us (8%)
  matrix products  27.8 us (8%)
  other arithmetic  3.74 us (1%)
    ppermute x16, waiting for transfers between devices, fetch(): return lax.ppermute(a, 'tp', [((i + k) % n_tp, i) for i in range(n_tp)])  70.8 us
    ppermute x16, starting transfers between devices, fetch(): return lax.ppermute(a, 'tp', [((i + k) % n_tp, i) for i in range(n_tp)])  47.4 us
    all_to_all x4, waiting for transfers between devices, exchange(): lax.all_to_all(a.reshape(n_src, -1, quarter), 'ep', split_axis=0, concat_...  44.3 us
    pallas_call x6, Pallas kernels, call(): pl.pallas_call(kernel, out_shape=[s for s, _ in outs], grid_spec=pltpu.Pr...  38.5 us
    ppermute x6, waiting for transfers between devices, give(): return lax.ppermute(a, 'tp', [(i, (i + k) % n_tp) for i in range(n_tp)])  37.5 us
    all_to_all x4, starting transfers between devices, exchange(): lax.all_to_all(a.reshape(n_src, -1, quarter), 'ep', split_axis=0, concat_...  37.5 us
    dot_general x11, matrix products, mm(): lax.dot_general(left, right, (dims, ((), ())), preferred_element_type=F32)  27.8 us
    ppermute x6, starting transfers between devices, give(): return lax.ppermute(a, 'tp', [(i, (i + k) % n_tp) for i in range(n_tp)])  9.6 us
  transfers between devices with their start and end apart: 26, of which 10 were waited for; matrix products, arithmetic and copies ran while one was open for 13% of the time, Pallas kernels for 9%

profile of v1, /device:TPU:2, one launch (start us, length us, event | category | flops | bytes accessed | tf_op | source)
XLA Modules:
  0.0 346.5 jit_solution(8358687389933902238)
XLA Ops:
  1.6 0.8 and_select_fusion.5
  2.4 2.0 convolution_convert_fusion.2
  4.4 12.1 %all-to-all-start = ((bf16[64,16,896]{2,1,0:T(8,128)(2,1)}), bf16[64,16,896]{2,1,0:T(8,128)(2,1)S(1)}, u32[]{:S(2)}, u32[]{:S(2)}) async-start(bf16[64,16,896]{2,1,0:T(8,128)(2,1)} %bitcast.79), calls=%async_computation | async-start | bytes 3670016 | tf_op jit(solution)/shard_map/all_to_all | solution.py:119
  16.9 2.0 multiply_convert_fusion
  18.9 43.3 %all-to-all-done = bf16[64,16,896]{2,1,0:T(8,128)(2,1)S(1)} async-done(((bf16[64,16,896]{2,1,0:T(8,128)(2,1)}), bf16[64,16,896]{2,1,0:T(8,128)(2,1)S(1)}, u32[]{:S(2)}, u32[]{:S(2)}) %all-to-all-start) | async-done | bytes 1835040 | tf_op jit(solution)/shard_map/all_to_all | solution.py:119
  62.1 1.2 copy-done.3
  63.4 5.4 %all-to-all-start.1 = ((bf16[64,16,896]{2,1,0:T(8,128)(2,1)}), bf16[64,16,896]{2,1,0:T(8,128)(2,1)S(1)}, u32[]{:S(2)}, u32[]{:S(2)}) async-start(bf16[64,16,896]{2,1,0:T(8,128)(2,1)} %bitcast.78), calls=%async_computation.1 | async-start | bytes 3670016 | tf_op jit(solution)/shard_map/all_to_all | solution.py:119
  68.8 1.7 collective-permute-start.2
  70.5 1.7 collective-permute-start
  72.1 7.1 %shard_map.103 = (bf16[896,768]{1,0:T(8,128)(2,1)}, bf16[896,768]{1,0:T(8,128)(2,1)}, bf16[896,768]{1,0:T(8,128)(2,1)}, bf16[896,768]{1,0:T(8,128)(2,1)}) custom-call(s32[1]{0:T(128)} %bitcast.7.me, bf16[4,896,256]{2,1,0:T(8,128)(2,1)} %bitcast.66, bf16[4,896,256]{2,1,0:T(8,128)(2,1)} %bitcast.69, bf16[256,3584]{1,0:T(8,128)(2,1)} %bitcast.80), custom_call_target="tpu_custom_call" | custom-call | bytes 5505028 | tf_op jit(solution)/shard_map/pallas_call | solution.py:85
  79.2 1.8 collective-permute-start.4
  81.7 1.0 collective-permute-start.6
  82.7 31.1 %collective-permute-done.2.last = bf16[1024,896]{1,0:T(8,128)(2,1)} collective-permute-done((bf16[1024,896]{1,0:T(8,128)(2,1)}, bf16[1024,896]{1,0:T(8,128)(2,1)}, u32[]{:S(2)}, u32[]{:S(2)}) %collective-permute-start.2) | collective-permute-done | bytes 1835040 | tf_op jit(solution)/shard_map/ppermute | solution.py:113
  113.7 2.2 slice.49
  115.9 28.1 %collective-permute-start.3 = (bf16[512,896]{1,0:T(8,128)(2,1)}, bf16[512,896]{1,0:T(8,128)(2,1)S(1)}, u32[]{:S(2)}, u32[]{:S(2)}) collective-permute-start(bf16[512,896]{1,0:T(8,128)(2,1)} %slice.49), channel_id=1, source_target_pairs={{3,0},{0,1},{1,2},{2,3},{7,4},{4,5},{5,6},{6,7},{11,8},{8,9},{9,10... | collective-permute-start | bytes 2752520 | tf_op jit(solution)/shard_map/ppermute | solution.py:113
  144.0 2.2 slice.48
  146.2 25.3 %collective-permute-done.4.refs_1_.refs_5_ = bf16[896,768]{1,0:T(8,128)(2,1)S(1)} collective-permute-done((bf16[896,768]{1,0:T(8,128)(2,1)}, bf16[896,768]{1,0:T(8,128)(2,1)S(1)}, u32[]{:S(2)}, u32[]{:S(2)}) %collective-permute-start.4) | collective-permute-done | bytes 1376288 | tf_op jit(solution)/shard_map/ppermute | solution.py:113
  171.5 1.1 copy-done.5
  172.6 1.1 copy-done.6
  173.7 1.2 copy-done.1
  174.9 5.6 %shard_map.104 = (f32[1024,256]{1,0:T(8,128)}, bf16[1024,256]{1,0:T(8,128)(2,1)}, bf16[1024,256]{1,0:T(8,128)(2,1)}, bf16[1024,256]{1,0:T(8,128)(2,1)}) custom-call(bf16[1024,896]{1,0:T(8,128)(2,1)} %bitcast.61, bf16[896,768]{1,0:T(8,128)(2,1)} %get-tuple-element.14.refs_0_.refs_4_, bf16[896,768]{1,0:T(8,128)(2,1)} %copy-done.5, bf16[896,768]{1,0:T(8,128)(2,1)} %copy-done.6, ...), custom_call_target="tpu_custom_call" | custom-call | flops 1879048192 | bytes 7340032 | tf_op jit(solution)/shard_map/pallas_call | solution.py:85
  180.6 2.3 collective-permute-start.7
  182.9 3.1 collective-permute-start.8
  186.0 8.0 %shard_map.102.partial = f32[1024,512]{1,0:T(8,128)} custom-call(s32[1]{0:T(128)} %bitcast.7.me, bf16[1024,896]{1,0:T(8,128)(2,1)} %bitcast.74, bf16[1024,896]{1,0:T(8,128)(2,1)} %collective-permute-done.after, bf16[1024,896]{1,0:T(8,128)(2,1)} %collective-permute-done.2.last, bf16[4,896,256]{2,1,0:T(8,128)(2,1)} %bitcast.67, bf16[4,896,256]{2,1,0:T(8,128)(2,1)} %bitcast.70), custom_call_target="tpu_custom_call" | custom-call | flops 2818572288 | bytes 9175044 | tf_op jit(solution)/shard_map/pallas_call | solution.py:85
  194.0 8.3 %collective-permute-done.7.refs_1_ = bf16[1024,256]{1,0:T(8,128)(2,1)S(1)} collective-permute-done((bf16[1024,256]{1,0:T(8,128)(2,1)}, bf16[1024,256]{1,0:T(8,128)(2,1)S(1)}, u32[]{:S(2)}, u32[]{:S(2)}) %collective-permute-start.7) | collective-permute-done | bytes 524320 | tf_op jit(solution)/shard_map/ppermute | solution.py:116
  202.3 12.5 %collective-permute-done.8.refs_2_ = bf16[1024,256]{1,0:T(8,128)(2,1)S(1)} collective-permute-done((bf16[1024,256]{1,0:T(8,128)(2,1)}, bf16[1024,256]{1,0:T(8,128)(2,1)S(1)}, u32[]{:S(2)}, u32[]{:S(2)}) %collective-permute-start.8) | collective-permute-done | bytes 524320 | tf_op jit(solution)/shard_map/ppermute | solution.py:116
  214.8 0.8 copy-done.12
  216.0 6.0 %shard_map.105 = (bf16[1024,256]{1,0:T(8,128)(2,1)}, bf16[1024,512]{1,0:T(8,128)(2,1)}) custom-call(s32[1]{0:T(128)} %bitcast.7.me, bf16[512,896]{1,0:T(8,128)(2,1)} %collective-permute-done.1.far_a, bf16[512,896]{1,0:T(8,128)(2,1)} %copy-done.7, f32[1024,512]{1,0:T(8,128)} %shard_map.102.partial, bf16[4,896,256]{2,1,0:T(8,128)(2,1)} %bitcast.68, ...), custom_call_target="tpu_custom_call" | custom-call | flops 939524096 | bytes 10223620 | tf_op jit(solution)/shard_map/pallas_call | solution.py:85
  222.1 2.1 slice_bitcast_fusion.1
  224.4 2.9 collective-permute-start.14
  227.3 1.1 collective-permute-start.13
  228.4 3.4 broadcast_in_dim.68
  231.8 1.4 constant_dynamic-update-slice_fusion.2
  233.2 3.0 constant_dynamic-update-slice_fusion.1
  236.2 1.9 collective-permute-start.18
  238.2 1.6 collective-permute-start.16
  239.8 2.6 maximum_dynamic-update-slice_fusion
  242.4 3.0 constant_dynamic-update-slice_fusion
  245.3 14.4 %collective-permute-done.15.refs_3_ = bf16[512,512]{1,0:T(8,128)(2,1)S(1)} collective-permute-done((bf16[512,512]{1,0:T(8,128)(2,1)S(1)}, bf16[512,512]{1,0:T(8,128)(2,1)S(1)}, u32[]{:S(2)}, u32[]{:S(2)}) %collective-permute-start.15) | collective-permute-done | bytes 524320 | tf_op jit(solution)/shard_map/ppermute | solution.py:113
  260.3 2.8 collective-permute-start.10
  263.1 5.9 %shard_map.107 = bf16[512,896]{1,0:T(8,128)(2,1)} custom-call(bf16[512,512]{1,0:T(8,128)(2,1)} %copy-done.9, bf16[512,512]{1,0:T(8,128)(2,1)} %copy-done.16, bf16[512,512]{1,0:T(8,128)(2,1)} %copy-done.15, bf16[512,512]{1,0:T(8,128)(2,1)} %copy-done.14, bf16[896,768]{1,0:T(8,128)(2,1)} %get-tuple-element.14.refs_0_.refs_4_, bf16[896,768]{1,0:T(8,128)(2,1)} %copy-done.5, ...), custom_call_target="tpu_custom_call" | custom-call | flops 1879048192 | bytes 7602176 | tf_op jit(solution)/shard_map/pallas_call | solution.py:85
  268.9 10.5 %all-to-all-start.3 = ((bf16[64,8,896]{2,1,0:T(8,128)(2,1)}), bf16[64,8,896]{2,1,0:T(8,128)(2,1)S(1)}, u32[]{:S(2)}, u32[]{:S(2)}) async-start(bf16[64,8,896]{2,1,0:T(8,128)(2,1)} %bitcast.77), calls=%async_computation.3 | async-start | bytes 1835008 | tf_op jit(solution)/shard_map/all_to_all | solution.py:119
  279.4 6.4 %fusion.1 = bf16[1,3584,256]{2,1,0:T(8,128)(2,1)} fusion(bf16[1024,3584]{1,0:T(8,128)(2,1)} %constant_dynamic-update-slice_fusion, bf16[1024,512]{1,0:T(8,128)(2,1)S(1)} %copy-done.10), kind=kOutput, calls=%fused_computation.3 | convolution fusion | flops 1879965696 | bytes 9699328 | tf_op jit(solution)/shard_map/dot_general | solution.py:16
  285.9 6.4 %fusion = bf16[1,3584,256]{2,1,0:T(8,128)(2,1)} fusion(bf16[1024,3584]{1,0:T(8,128)(2,1)} %constant_dynamic-update-slice_fusion, bf16[1024,512]{1,0:T(8,128)(2,1)S(1)} %copy-done.10), kind=kOutput, calls=%fused_computation.2 | convolution fusion | flops 1879965696 | bytes 9699328 | tf_op jit(solution)/shard_map/dot_general | solution.py:16
  292.3 1.3 broadcast_in_dim.71
  293.7 0.8 copy-done.2
  294.5 2.5 fusion.4
  297.0 1.5 collective-permute-start.20
  298.5 5.8 %shard_map.106 = bf16[512,896]{1,0:T(8,128)(2,1)} custom-call(bf16[512,512]{1,0:T(8,128)(2,1)} %get-tuple-element.26.refs_0_, bf16[512,512]{1,0:T(8,128)(2,1)} %collective-permute-done.10.refs_1_, bf16[512,512]{1,0:T(8,128)(2,1)} %collective-permute-done.11.refs_2_, bf16[512,512]{1,0:T(8,128)(2,1)} %collective-permute-done.12.refs_3_, ...), custom_call_target="tpu_custom_call" | custom-call | flops 1879048192 | bytes 7602176 | tf_op jit(solution)/shard_map/pallas_call | solution.py:85
  304.3 1.0 all-to-all-done.3
  305.4 9.5 %all-to-all-start.2 = ((bf16[64,8,896]{2,1,0:T(8,128)(2,1)}), bf16[64,8,896]{2,1,0:T(8,128)(2,1)}, u32[]{:S(2)}, u32[]{:S(2)}) async-start(bf16[64,8,896]{2,1,0:T(8,128)(2,1)} %bitcast.76), calls=%async_computation.2 | async-start | bytes 1835008 | tf_op jit(solution)/shard_map/all_to_all | solution.py:119
  314.8 1.8 convolution_convert_fusion.5
  316.6 1.3 collective-permute-start.17
  318.0 1.8 convolution_convert_fusion.4
  319.7 2.0 collective-permute-start.19
  321.7 1.8 convolution_convert_fusion.3
  323.5 0.9 collective-permute-start.21
  324.4 6.9 %collective-permute-done.17 = bf16[256,896]{1,0:T(8,128)(2,1)S(1)} collective-permute-done((bf16[256,896]{1,0:T(8,128)(2,1)S(1)}, bf16[256,896]{1,0:T(8,128)(2,1)S(1)}, u32[]{:S(2)}, u32[]{:S(2)}) %collective-permute-start.17) | collective-permute-done | bytes 458784 | tf_op jit(solution)/shard_map/ppermute | solution.py:116
  331.3 0.8 bitcast_dynamic-update-slice_fusion.2
  332.1 8.2 %collective-permute-done.19 = bf16[256,896]{1,0:T(8,128)(2,1)S(1)} collective-permute-done((bf16[256,896]{1,0:T(8,128)(2,1)S(1)}, bf16[256,896]{1,0:T(8,128)(2,1)S(1)}, u32[]{:S(2)}, u32[]{:S(2)}) %collective-permute-start.19) | collective-permute-done | bytes 458784 | tf_op jit(solution)/shard_map/ppermute | solution.py:116
  340.3 0.8 bitcast_dynamic-update-slice_fusion.1
  341.1 1.7 collective-permute-done.21
  342.8 0.8 bitcast_dynamic-update-slice_fusion
  344.1 2.4 fusion.2
  (62 shorter events, 3.7 us)
Async XLA Ops:
  0.6 1.8 copy-start
  4.4 12.2 %copy-start.17 = (f32[256,2]{0,1:T(2,128)S(1)}, f32[256,2]{0,1:T(2,128)}, u32[]{:S(2)}) copy-start(f32[256,2]{0,1:T(2,128)} %param.10) | copy-start | bytes 6148
  4.4 12.5 %copy-start.18 = (bf16[256,896]{1,0:T(8,128)(2,1)S(1)}, bf16[256,896]{1,0:T(8,128)(2,1)}, u32[]{:S(2)}) copy-start(bf16[256,896]{1,0:T(8,128)(2,1)} %param.8) | copy-start | bytes 1376260
  4.4 57.8 %all-to-all-start = ((bf16[64,16,896]{2,1,0:T(8,128)(2,1)}), bf16[64,16,896]{2,1,0:T(8,128)(2,1)S(1)}, u32[]{:S(2)}, u32[]{:S(2)}) async-start(bf16[64,16,896]{2,1,0:T(8,128)(2,1)} %bitcast.79), calls=%async_computation | async-start | bytes 3670016 | tf_op jit(solution)/shard_map/all_to_all | solution.py:119
  62.1 1.2 copy-start.3
  63.4 110.3 %all-to-all-start.1 = ((bf16[64,16,896]{2,1,0:T(8,128)(2,1)}), bf16[64,16,896]{2,1,0:T(8,128)(2,1)S(1)}, u32[]{:S(2)}, u32[]{:S(2)}) async-start(bf16[64,16,896]{2,1,0:T(8,128)(2,1)} %bitcast.78), calls=%async_computation.1 | async-start | bytes 3670016 | tf_op jit(solution)/shard_map/all_to_all | solution.py:119
  68.8 44.9 %collective-permute-start.2 = (bf16[1024,896]{1,0:T(8,128)(2,1)}, bf16[1024,896]{1,0:T(8,128)(2,1)}, u32[]{:S(2)}, u32[]{:S(2)}) collective-permute-start(bf16[1024,896]{1,0:T(8,128)(2,1)} %bitcast.72), channel_id=1, source_target_pairs={{3,0},{0,1},{1,2},{2,3},{7,4},{4,5},{5,6},{6,7},{11,8},{8,9},{9,10... | collective-permute-start | bytes 5505032 | tf_op jit(solution)/shard_map/ppermute | solution.py:113
  70.5 73.5 %collective-permute-start = (bf16[1024,896]{1,0:T(8,128)(2,1)}, bf16[1024,896]{1,0:T(8,128)(2,1)}, u32[]{:S(2)}, u32[]{:S(2)}) collective-permute-start(bf16[1024,896]{1,0:T(8,128)(2,1)} %bitcast.73), channel_id=1, source_target_pairs={{1,0},{2,1},{3,2},{0,3},{5,4},{6,5},{7,6},{4,7},{9,8},{10,9},{11,1... | collective-permute-start | bytes 5505032 | tf_op jit(solution)/shard_map/ppermute | solution.py:113
  79.2 92.2 %collective-permute-start.4 = (bf16[896,768]{1,0:T(8,128)(2,1)}, bf16[896,768]{1,0:T(8,128)(2,1)S(1)}, u32[]{:S(2)}, u32[]{:S(2)}) collective-permute-start(bf16[896,768]{1,0:T(8,128)(2,1)} %get-tuple-element.15), channel_id=1, source_target_pairs={{1,0},{2,1},{3,2},{0,3},{5,4},{6,5},{7,6},{4,7},{9,8},{10,9},{11,1... | collective-permute-start | bytes 4128776 | tf_op jit(solution)/shard_map/ppermute | solution.py:113
  81.1 90.4 %collective-permute-start.5 = (bf16[896,768]{1,0:T(8,128)(2,1)}, bf16[896,768]{1,0:T(8,128)(2,1)S(1)}, u32[]{:S(2)}, u32[]{:S(2)}) collective-permute-start(bf16[896,768]{1,0:T(8,128)(2,1)} %get-tuple-element.16), channel_id=1, source_target_pairs={{2,0},{3,1},{0,2},{1,3},{6,4},{7,5},{4,6},{5,7},{10,8},{11,9},{8,1... | collective-permute-start | bytes 4128776 | tf_op jit(solution)/shard_map/ppermute | solution.py:113
  81.7 92.0 %collective-permute-start.6 = (bf16[896,768]{1,0:T(8,128)(2,1)}, bf16[896,768]{1,0:T(8,128)(2,1)}, u32[]{:S(2)}, u32[]{:S(2)}) collective-permute-start(bf16[896,768]{1,0:T(8,128)(2,1)} %get-tuple-element.17), channel_id=1, source_target_pairs={{3,0},{0,1},{1,2},{2,3},{7,4},{4,5},{5,6},{6,7},{11,8},{8,9},{9,10... | collective-permute-start | bytes 4128776 | tf_op jit(solution)/shard_map/ppermute | solution.py:113
  115.9 98.8 %collective-permute-start.3 = (bf16[512,896]{1,0:T(8,128)(2,1)}, bf16[512,896]{1,0:T(8,128)(2,1)S(1)}, u32[]{:S(2)}, u32[]{:S(2)}) collective-permute-start(bf16[512,896]{1,0:T(8,128)(2,1)} %slice.49), channel_id=1, source_target_pairs={{3,0},{0,1},{1,2},{2,3},{7,4},{4,5},{5,6},{6,7},{11,8},{8,9},{9,10... | collective-permute-start | bytes 2752520 | tf_op jit(solution)/shard_map/ppermute | solution.py:113
  146.2 68.6 %collective-permute-start.1 = (bf16[512,896]{1,0:T(8,128)(2,1)}, bf16[512,896]{1,0:T(8,128)(2,1)}, u32[]{:S(2)}, u32[]{:S(2)}) collective-permute-start(bf16[512,896]{1,0:T(8,128)(2,1)} %slice.48), channel_id=1, source_target_pairs={{1,0},{2,1},{3,2},{0,3},{5,4},{6,5},{7,6},{4,7},{9,8},{10,9},{11,1... | collective-permute-start | bytes 2752520 | tf_op jit(solution)/shard_map/ppermute | solution.py:113
  171.5 1.1 copy-start.5
  172.6 1.1 copy-start.6
  173.7 1.2 copy-start.1
  180.6 21.7 %collective-permute-start.7 = (bf16[1024,256]{1,0:T(8,128)(2,1)}, bf16[1024,256]{1,0:T(8,128)(2,1)S(1)}, u32[]{:S(2)}, u32[]{:S(2)}) collective-permute-start(bf16[1024,256]{1,0:T(8,128)(2,1)} %get-tuple-element.19), channel_id=1, source_target_pairs={{0,1},{1,2},{2,3},{3,0},{4,5},{5,6},{6,7},{7,4},{8,9},{9,10},{10,1... | collective-permute-start | bytes 1572872 | tf_op jit(solution)/shard_map/ppermute | solution.py:116
  182.9 31.9 %collective-permute-start.8 = (bf16[1024,256]{1,0:T(8,128)(2,1)}, bf16[1024,256]{1,0:T(8,128)(2,1)S(1)}, u32[]{:S(2)}, u32[]{:S(2)}) collective-permute-start(bf16[1024,256]{1,0:T(8,128)(2,1)} %get-tuple-element.20), channel_id=1, source_target_pairs={{0,2},{1,3},{2,0},{3,1},{4,6},{5,7},{6,4},{7,5},{8,10},{9,11},{10,... | collective-permute-start | bytes 1572872 | tf_op jit(solution)/shard_map/ppermute | solution.py:116
  185.9 28.8 %collective-permute-start.9 = (bf16[1024,256]{1,0:T(8,128)(2,1)}, bf16[1024,256]{1,0:T(8,128)(2,1)S(1)}, u32[]{:S(2)}, u32[]{:S(2)}) collective-permute-start(bf16[1024,256]{1,0:T(8,128)(2,1)} %get-tuple-element.21), channel_id=1, source_target_pairs={{0,3},{1,0},{2,1},{3,2},{4,7},{5,4},{6,5},{7,6},{8,11},{9,8},{10,9... | collective-permute-start | bytes 1572872 | tf_op jit(solution)/shard_map/ppermute | solution.py:116
  202.3 12.5 %copy-start.11 = (bf16[1024,256]{1,0:T(8,128)(2,1)}, bf16[1024,256]{1,0:T(8,128)(2,1)S(1)}, u32[]{:S(2)}) copy-start(bf16[1024,256]{1,0:T(8,128)(2,1)S(1)} %collective-permute-done.7.refs_1_) | copy-start | bytes 1572868
  214.7 0.8 copy-start.12
  214.7 1.0 copy-start.13
  214.7 1.3 copy-start.7
  224.2 7.6 %copy-start.9 = (bf16[512,512]{1,0:T(8,128)(2,1)}, bf16[512,512]{1,0:T(8,128)(2,1)S(1)}, u32[]{:S(2)}) copy-start(bf16[512,512]{1,0:T(8,128)(2,1)S(1)} %get-tuple-element.27.refs_0_) | copy-start | bytes 1572868
  224.2 7.6 %copy-start.4 = (bf16[64,16,896]{2,1,0:T(8,128)(2,1)S(1)}, bf16[64,16,896]{2,1,0:T(8,128)(2,1)}, u32[]{:S(2)}) copy-start(bf16[64,16,896]{2,1,0:T(8,128)(2,1)} %copy-done.3) | copy-start | bytes 5505028
  224.2 35.5 %collective-permute-start.15 = (bf16[512,512]{1,0:T(8,128)(2,1)S(1)}, bf16[512,512]{1,0:T(8,128)(2,1)S(1)}, u32[]{:S(2)}, u32[]{:S(2)}) collective-permute-start(bf16[512,512]{1,0:T(8,128)(2,1)S(1)} %get-tuple-element.27.refs_0_), channel_id=1, source_target_pairs={{3,0},{0,1},{1,2},{2,3},{7,4},{4,5},{5,6},{6,7},{11,8},{8,9},{9,10... | collective-permute-start | bytes 1572872 | tf_op jit(solution)/shard_map/ppermute | solution.py:113
  224.4 35.4 %collective-permute-start.14 = (bf16[512,512]{1,0:T(8,128)(2,1)S(1)}, bf16[512,512]{1,0:T(8,128)(2,1)S(1)}, u32[]{:S(2)}, u32[]{:S(2)}) collective-permute-start(bf16[512,512]{1,0:T(8,128)(2,1)S(1)} %get-tuple-element.27.refs_0_), channel_id=1, source_target_pairs={{2,0},{3,1},{0,2},{1,3},{6,4},{7,5},{4,6},{5,7},{10,8},{11,9},{8,1... | collective-permute-start | bytes 1572872 | tf_op jit(solution)/shard_map/ppermute | solution.py:113
  227.3 33.0 %collective-permute-start.13 = (bf16[512,512]{1,0:T(8,128)(2,1)S(1)}, bf16[512,512]{1,0:T(8,128)(2,1)S(1)}, u32[]{:S(2)}, u32[]{:S(2)}) collective-permute-start(bf16[512,512]{1,0:T(8,128)(2,1)S(1)} %get-tuple-element.27.refs_0_), channel_id=1, source_target_pairs={{1,0},{2,1},{3,2},{0,3},{5,4},{6,5},{7,6},{4,7},{9,8},{10,9},{11,1... | collective-permute-start | bytes 1572872 | tf_op jit(solution)/shard_map/ppermute | solution.py:113
  233.2 6.5 %copy-start.8 = (bf16[512,896]{1,0:T(8,128)(2,1)S(1)}, bf16[512,896]{1,0:T(8,128)(2,1)}, u32[]{:S(2)}) copy-start(bf16[512,896]{1,0:T(8,128)(2,1)} %copy-done.7) | copy-start | bytes 2752516
  236.2 81.7 %collective-permute-start.18 = (bf16[1024,256]{1,0:T(8,128)(2,1)}, bf16[1024,256]{1,0:T(8,128)(2,1)}, u32[]{:S(2)}, u32[]{:S(2)}) collective-permute-start(bf16[1024,256]{1,0:T(8,128)(2,1)} %get-tuple-element.23), channel_id=1, source_target_pairs={{2,0},{3,1},{0,2},{1,3},{6,4},{7,5},{4,6},{5,7},{10,8},{11,9},{8,1... | collective-permute-start | bytes 1572872 | tf_op jit(solution)/shard_map/ppermute | solution.py:113
  238.2 76.6 %collective-permute-start.16 = (bf16[1024,256]{1,0:T(8,128)(2,1)}, bf16[1024,256]{1,0:T(8,128)(2,1)}, u32[]{:S(2)}, u32[]{:S(2)}) collective-permute-start(bf16[1024,256]{1,0:T(8,128)(2,1)} %get-tuple-element.23), channel_id=1, source_target_pairs={{1,0},{2,1},{3,2},{0,3},{5,4},{6,5},{7,6},{4,7},{9,8},{10,9},{11,1... | collective-permute-start | bytes 1572872 | tf_op jit(solution)/shard_map/ppermute | solution.py:113
  259.7 3.4 copy-start.14
  259.7 37.3 %collective-permute-start.12 = (bf16[512,512]{1,0:T(8,128)(2,1)}, bf16[512,512]{1,0:T(8,128)(2,1)}, u32[]{:S(2)}, u32[]{:S(2)}) collective-permute-start(bf16[512,512]{1,0:T(8,128)(2,1)} %get-tuple-element.26.refs_0_), channel_id=1, source_target_pairs={{3,0},{0,1},{1,2},{2,3},{7,4},{4,5},{5,6},{6,7},{11,8},{8,9},{9,10... | collective-permute-start | bytes 1572872 | tf_op jit(solution)/shard_map/ppermute | solution.py:113
  259.7 3.3 copy-start.15
  259.7 38.8 %collective-permute-start.11 = (bf16[512,512]{1,0:T(8,128)(2,1)}, bf16[512,512]{1,0:T(8,128)(2,1)}, u32[]{:S(2)}, u32[]{:S(2)}) collective-permute-start(bf16[512,512]{1,0:T(8,128)(2,1)} %get-tuple-element.26.refs_0_), channel_id=1, source_target_pairs={{2,0},{3,1},{0,2},{1,3},{6,4},{7,5},{4,6},{5,7},{10,8},{11,9},{8,1... | collective-permute-start | bytes 1572872 | tf_op jit(solution)/shard_map/ppermute | solution.py:113
  260.2 2.8 copy-start.16
  260.3 38.3 %collective-permute-start.10 = (bf16[512,512]{1,0:T(8,128)(2,1)}, bf16[512,512]{1,0:T(8,128)(2,1)}, u32[]{:S(2)}, u32[]{:S(2)}) collective-permute-start(bf16[512,512]{1,0:T(8,128)(2,1)} %get-tuple-element.26.refs_0_), channel_id=1, source_target_pairs={{1,0},{2,1},{3,2},{0,3},{5,4},{6,5},{7,6},{4,7},{9,8},{10,9},{11,1... | collective-permute-start | bytes 1572872 | tf_op jit(solution)/shard_map/ppermute | solution.py:113
  268.9 10.5 %copy-start.10 = (bf16[1024,512]{1,0:T(8,128)(2,1)S(1)}, bf16[1024,512]{1,0:T(8,128)(2,1)}, u32[]{:S(2)}) copy-start(bf16[1024,512]{1,0:T(8,128)(2,1)} %get-tuple-element.22) | copy-start | bytes 3145732
  268.9 36.4 %all-to-all-start.3 = ((bf16[64,8,896]{2,1,0:T(8,128)(2,1)}), bf16[64,8,896]{2,1,0:T(8,128)(2,1)S(1)}, u32[]{:S(2)}, u32[]{:S(2)}) async-start(bf16[64,8,896]{2,1,0:T(8,128)(2,1)} %bitcast.77), calls=%async_computation.3 | async-start | bytes 1835008 | tf_op jit(solution)/shard_map/all_to_all | solution.py:119
  292.3 2.2 copy-start.2
  297.0 24.7 %collective-permute-start.20 = (bf16[1024,256]{1,0:T(8,128)(2,1)}, bf16[1024,256]{1,0:T(8,128)(2,1)}, u32[]{:S(2)}, u32[]{:S(2)}) collective-permute-start(bf16[1024,256]{1,0:T(8,128)(2,1)} %get-tuple-element.23), channel_id=1, source_target_pairs={{3,0},{0,1},{1,2},{2,3},{7,4},{4,5},{5,6},{6,7},{11,8},{8,9},{9,10... | collective-permute-start | bytes 1572872 | tf_op jit(solution)/shard_map/ppermute | solution.py:113
  305.4 38.7 %all-to-all-start.2 = ((bf16[64,8,896]{2,1,0:T(8,128)(2,1)}), bf16[64,8,896]{2,1,0:T(8,128)(2,1)}, u32[]{:S(2)}, u32[]{:S(2)}) async-start(bf16[64,8,896]{2,1,0:T(8,128)(2,1)} %bitcast.76), calls=%async_computation.2 | async-start | bytes 1835008 | tf_op jit(solution)/shard_map/all_to_all | solution.py:119
  316.6 14.7 %collective-permute-start.17 = (bf16[256,896]{1,0:T(8,128)(2,1)S(1)}, bf16[256,896]{1,0:T(8,128)(2,1)S(1)}, u32[]{:S(2)}, u32[]{:S(2)}) collective-permute-start(bf16[256,896]{1,0:T(8,128)(2,1)S(1)} %convolution_convert_fusion.5), channel_id=1, source_target_pairs={{0,1},{1,2},{2,3},{3,0},{4,5},{5,6},{6,7},{7,4},{8,9},{9,10},{10,1... | collective-permute-start | bytes 1376264 | tf_op jit(solution)/shard_map/ppermute | solution.py:116
  319.7 20.5 %collective-permute-start.19 = (bf16[256,896]{1,0:T(8,128)(2,1)S(1)}, bf16[256,896]{1,0:T(8,128)(2,1)S(1)}, u32[]{:S(2)}, u32[]{:S(2)}) collective-permute-start(bf16[256,896]{1,0:T(8,128)(2,1)S(1)} %convolution_convert_fusion.4), channel_id=1, source_target_pairs={{0,2},{1,3},{2,0},{3,1},{4,6},{5,7},{6,4},{7,5},{8,10},{9,11},{10,... | collective-permute-start | bytes 1376264 | tf_op jit(solution)/shard_map/ppermute | solution.py:116
  323.5 19.2 %collective-permute-start.21 = (bf16[256,896]{1,0:T(8,128)(2,1)S(1)}, bf16[256,896]{1,0:T(8,128)(2,1)S(1)}, u32[]{:S(2)}, u32[]{:S(2)}) collective-permute-start(bf16[256,896]{1,0:T(8,128)(2,1)S(1)} %convolution_convert_fusion.3), channel_id=1, source_target_pairs={{0,3},{1,0},{2,1},{3,2},{4,7},{5,4},{6,5},{7,6},{8,11},{9,8},{10,9... | collective-permute-start | bytes 1376264 | tf_op jit(solution)/shard_map/ppermute | solution.py:116

commit v2 on v0

--- a/solution.py
+++ b/solution.py
@@ -1,3 +1,5 @@
+import functools
+
 import jax
 import jax.numpy as jnp
 from jax import lax
@@ -19,20 +21,16 @@
     return mm(left, right, ((1,), (0,)))
 
 
-def pack_kernel(me, gate, up, down, *packed):
-    n = len(packed)
-    quarter, hid = gate.shape[1:]
-    for k in range(n):
-        out = packed[k]
+def pack_kernel(places, me, gate, up, down, *packed):
+    step = pl.program_id(0)
+    n, span, hid = gate.shape
+    width = down.shape[1] // n
+    for k, out in zip(places, packed):
         q = lax.rem(me[0] + n - k, n)
-
-        @pl.loop(0, quarter // 128)
-        def _(t):
-            span = pl.ds(pl.multiple_of(t * 128, 128), 128)
-            out[span, 0:hid] = gate[q, span, :]
-            out[span, hid : 2 * hid] = up[q, span, :]
-            start = pl.multiple_of(q * quarter + t * 128, 128)
-            out[span, 2 * hid : 3 * hid] = down[:, pl.ds(start, 128)].T
+        out[:, 0:hid] = gate[q]
+        out[:, hid : 2 * hid] = up[q]
+        start = pl.multiple_of(q * width + step * span, 128)
+        out[:, 2 * hid : 3 * hid] = down[:, pl.ds(start, span)].T
 
 
 def partial_kernel(me, own, after, last, gate, up, out):
@@ -52,7 +50,7 @@
 
 
 def acts_kernel(me, far_a, far_b, partial, gate_w, up_w, *refs):
-    hidden, grads, x = refs[-3:]
+    hidden, grads_a, grads_b, x = refs[-4:]
     step = pl.program_id(0)
 
     @pl.when(step < TILES // 2)
@@ -66,20 +64,43 @@
     hid = gate_w.shape[2]
     gate = partial[:, :hid] + rows_by_columns(x[...], gate_w[0])
     upper = partial[:, hid:] + rows_by_columns(x[...], up_w[0])
-    back = sum(r[...].astype(F32) for r in refs[:-3])
+    back = sum(r[...].astype(F32) for r in refs[:-4])
     sigma = jax.nn.sigmoid(gate)
     active = gate * sigma
     hidden[...] = (active * upper).astype(BF)
-    grads[:, :hid] = (back * upper * sigma * (1.0 + gate * (1.0 - sigma))).astype(BF)
-    grads[:, hid:] = (back * active).astype(BF)
+    d_gate = (back * upper * sigma * (1.0 + gate * (1.0 - sigma))).astype(BF)
+    d_up = (back * active).astype(BF)
+
+    @pl.when(step < TILES // 2)
+    def _():
+        grads_a[:, :hid] = d_gate
+        grads_a[:, hid:] = d_up
+
+    @pl.when(step >= TILES // 2)
+    def _():
+        grads_b[:, :hid] = d_gate
+        grads_b[:, hid:] = d_up
 
 
 def dx_kernel(*refs):
-    n = len(refs) // 2
-    total = mm(refs[0][...], refs[n][...], ((1,), (1,)))
-    for k in range(1, n):
-        total += mm(refs[k][...], refs[n + k][...], ((1,), (1,)))
-    refs[-1][...] = total.astype(BF)
+    out, d = refs[-2:]
+    n = (len(refs) - 2) // 3
+    width = refs[0].shape[1]
+    step = pl.program_id(0)
+
+    @pl.when(step < TILES // 2)
+    def _():
+        for k in range(n):
+            d[:, k * width : (k + 1) * width] = refs[k][...]
+
+    @pl.when(step >= TILES // 2)
+    def _():
+        for k in range(n):
+            d[:, k * width : (k + 1) * width] = refs[n + k][...]
+
+    out[...] = sum(
+        mm(d[:, k * width : (k + 1) * width], refs[2 * n + k][...], ((1,), (1,))) for k in range(n)
+    ).astype(BF)
 
 
 def call(kernel, scalars, ins, outs, grid, scratch, flops, operands):
@@ -119,8 +140,8 @@
 
     def exchange(a):
         return lax.all_to_all(
-            a.reshape(n_src, cap, quarter), "ep", split_axis=0, concat_axis=0, tiled=True
-        ).reshape(rows, quarter)
+            a.reshape(n_src, -1, quarter), "ep", split_axis=0, concat_axis=0, tiled=True
+        ).reshape(-1, quarter)
 
     def by_rows(width):
         return pl.BlockSpec((tile, width), lambda i, *_: (i, 0))
@@ -141,11 +162,12 @@
         < lax.broadcasted_iota(jnp.int32, (tok_rows, tok_rows), 1)
     ).astype(BF)
     earlier = rows_by_columns(named, before)
+    ranks = [
+        jnp.sum(jnp.where(h, earlier, 0.0), axis=0, keepdims=True).astype(jnp.int32) for h in hot
+    ]
+
     row_index = lax.broadcasted_iota(jnp.int32, (rows, tok_rows), 0)
-    found = []
-    for k in range(top):
-        rank = jnp.sum(jnp.where(hot[k], earlier, 0.0), axis=0, keepdims=True).astype(jnp.int32)
-        found.append(row_index == ids[k : k + 1] * cap + rank)
+    found = [row_index == ids[k : k + 1] * cap + ranks[k] for k in range(top)]
     pick = sum(f.astype(BF) for f in found)
 
     x_own = exchange(rows_by_columns(pick, tokens).astype(BF))
@@ -158,18 +180,23 @@
     gate_q = w_gate[0].reshape(n_tp, quarter, hid)
     up_q = w_up[0].reshape(n_tp, quarter, hid)
     down = w_down[0]
-    packed_shape = (quarter, 3 * hid)
-    packed = call(
-        pack_kernel,
-        1,
-        [whole(gate_q.shape), whole(up_q.shape), whole(down.shape)],
-        [(array(packed_shape, BF), whole(packed_shape))] * n_tp,
-        (1,),
-        [],
-        0,
-        (spot, gate_q, up_q, down),
-    )
-    packed = [packed[0]] + [fetch(packed[k], k) for k in shifts]
+    by_span = pl.BlockSpec((n_tp, 128, hid), lambda i, m: (0, i, 0))
+
+    def pack(places):
+        return call(
+            functools.partial(pack_kernel, places),
+            1,
+            [by_span, by_span, whole(down.shape)],
+            [(array((quarter, 3 * hid), BF), pl.BlockSpec((128, 3 * hid), lambda i, m: (i, 0)))]
+            * len(places),
+            (quarter // 128,),
+            [],
+            0,
+            (spot, gate_q, up_q, down),
+        )
+
+    sent = pack(tuple(shifts))
+    packed = list(pack((0,))) + [fetch(sent[k - 1], k) for k in shifts]
 
     half = rows // 2
     x_next, x_last = fetch(x_own, 1), fetch(x_own, n_tp - 1)
@@ -198,35 +225,51 @@
     )
     terms = [terms[0]] + [give(terms[k], k) for k in shifts]
     mid = TILES // 2
+
+    def upper_rows(width):
+        return pl.BlockSpec((tile, width), lambda i, *_: (jnp.minimum(i, mid - 1), 0))
+
+    def lower_rows(width):
+        return pl.BlockSpec((tile, width), lambda i, *_: (jnp.maximum(i - mid, 0), 0))
+
     opposite = pl.BlockSpec((1, quarter, hid), lambda i, m: (lax.rem(m[0] + 2, n_tp), 0, 0))
-    hidden, d_own = call(
+    hidden, d_a, d_b = call(
         acts_kernel,
         1,
         [
-            pl.BlockSpec((tile, quarter), lambda i, m: (jnp.minimum(i, mid - 1), 0)),
-            pl.BlockSpec((tile, quarter), lambda i, m: (jnp.maximum(i - mid, 0), 0)),
+            upper_rows(quarter),
+            lower_rows(quarter),
             by_rows(2 * hid),
             opposite,
             opposite,
         ]
         + [by_rows(hid)] * n_tp,
-        [(array((rows, hid), BF), by_rows(hid)), (array((rows, 2 * hid), BF), by_rows(2 * hid))],
+        [
+            (array((rows, hid), BF), by_rows(hid)),
+            (array((half, 2 * hid), BF), upper_rows(2 * hid)),
+            (array((half, 2 * hid), BF), lower_rows(2 * hid)),
+        ],
         (TILES,),
         [pltpu.VMEM((tile, quarter), BF)],
         4 * rows * quarter * hid,
         (spot, far_a, far_b, partial, gate_q, up_q, *terms),
     )
-    d_all = [d_own] + [fetch(d_own, k) for k in shifts]
+    back_one = n_tp - 1
+    next_a, last_b = fetch(d_a, 1), fetch(d_b, back_one)
+    next_b, last_a = fetch(d_b, 1), fetch(d_a, back_one)
+    passed_a, passed_b = fetch(next_a, 1), fetch(last_b, back_one)
+    halves = (d_a, next_a, passed_a, last_a, d_b, next_b, passed_b, last_b)
     (dx,) = call(
         dx_kernel,
         0,
-        [by_rows(2 * hid)] * n_tp
+        [upper_rows(2 * hid)] * n_tp
+        + [lower_rows(2 * hid)] * n_tp
         + [pl.BlockSpec((quarter, 2 * hid), lambda i: (0, 0))] * n_tp,
         [(array((rows, quarter), BF), by_rows(quarter))],
         (TILES,),
-        [],
+        [pltpu.VMEM((tile, 2 * hid * n_tp), BF)],
         4 * n_tp * rows * quarter * hid,
-        (*d_all, *packed),
+        (*halves, *packed),
     )
     dx = exchange(dx)
     grad_tokens = mm(pick, dx, ((0,), (0,))).astype(BF)
@@ -236,6 +279,7 @@
     for k, piece in ((0, x_own), (1, x_next), (2, x_far), (n_tp - 1, x_last)):
         start = lax.rem(me + k, n_tp) * quarter
         x_full = lax.dynamic_update_slice_in_dim(x_full, piece, start, axis=1)
+    d_own = jnp.concatenate([d_a, d_b], axis=0)
     g_gate = mm(x_full, d_own[:, :hid], ((0,), (0,))).astype(BF)
     g_up = mm(x_full, d_own[:, hid:], ((0,), (0,))).astype(BF)
 

time: 347 us -> 344 us (level)
  waiting for transfers between devices: 174 us -> 158 us
  starting transfers between devices: 79 us -> 86.2 us
  Pallas kernels: 35.4 us -> 42.1 us
    ppermute x13 -> x16, waiting for transfers between devices: 93.4 us -> 76.1 us  [fetch(): return lax.ppermute(a, 'tp', [((i + k) % n_tp, i) for i in range(n_tp)])]
    pallas_call x5 -> x6, Pallas kernels: 35.4 us -> 42.1 us  [call(): pl.pallas_call(kernel, out_shape=[s for s, _ in outs], grid_spec=pltpu.Pr...]
    ppermute x13 -> x16, starting transfers between devices: 40.9 us -> 46.9 us  [fetch(): return lax.ppermute(a, 'tp', [((i + k) % n_tp, i) for i in range(n_tp)])]
    unnamed x34 -> x39, local copies, waits for them, and re-layouts: 7.09 us -> 5.35 us
  transfers between devices with their start and end apart: 22 -> 25, of which waited for: 10 -> 12; matrix products, arithmetic and copies ran while one was open for 13% -> 13% of each run, Pallas kernels for 8% -> 11%
where the time goes in v2:
time: 344 us; the launch traced here: 342 us
  waiting for transfers between devices  158 us (46%)
  starting transfers between devices  86.2 us (25%)
  Pallas kernels  42.1 us (12%)
  matrix products  26.4 us (8%)
  local copies, waits for them, and re-layouts  25.1 us (7%)
  other arithmetic  3.81 us (1%)
    ppermute x16, waiting for transfers between devices, fetch(): return lax.ppermute(a, 'tp', [((i + k) % n_tp, i) for i in range(n_tp)])  76.1 us
    ppermute x16, starting transfers between devices, fetch(): return lax.ppermute(a, 'tp', [((i + k) % n_tp, i) for i in range(n_tp)])  46.9 us
    all_to_all x3, waiting for transfers between devices, exchange(): lax.all_to_all(a.reshape(n_src, -1, quarter), 'ep', split_axis=0, concat_...  43.3 us
    pallas_call x6, Pallas kernels, call(): pl.pallas_call(kernel, out_shape=[s for s, _ in outs], grid_spec=pltpu.Pr...  42.1 us
    ppermute x6, waiting for transfers between devices, give(): return lax.ppermute(a, 'tp', [(i, (i + k) % n_tp) for i in range(n_tp)])  38.5 us
    all_to_all x3, starting transfers between devices, exchange(): lax.all_to_all(a.reshape(n_src, -1, quarter), 'ep', split_axis=0, concat_...  28 us
    dot_general x10, matrix products, mm(): lax.dot_general(left, right, (dims, ((), ())), preferred_element_type=F32)  26.4 us
    ppermute x6, starting transfers between devices, give(): return lax.ppermute(a, 'tp', [(i, (i + k) % n_tp) for i in range(n_tp)])  11.3 us
  transfers between devices with their start and end apart: 25, of which 12 were waited for; matrix products, arithmetic and copies ran while one was open for 13% of the time, Pallas kernels for 11%

profile of v2, /device:TPU:2, one launch (start us, length us, event | category | flops | bytes accessed | tf_op | source)
XLA Modules:
  0.0 342.3 jit_solution(3657070103733971280)
XLA Ops:
  0.6 0.8 fusion.27
  1.6 0.8 multiply_add_fusion.1
  2.4 1.9 convolution_convert_fusion.2
  4.3 12.1 %all-to-all-start = ((bf16[64,16,896]{2,1,0:T(8,128)(2,1)}), bf16[64,16,896]{2,1,0:T(8,128)(2,1)S(1)}, u32[]{:S(2)}, u32[]{:S(2)}) async-start(bf16[64,16,896]{2,1,0:T(8,128)(2,1)} %bitcast.69), calls=%async_computation | async-start | bytes 3670016 | tf_op jit(solution)/shard_map/all_to_all | solution.py:142
  16.9 2.0 multiply_convert_fusion
  18.8 43.3 %all-to-all-done = bf16[64,16,896]{2,1,0:T(8,128)(2,1)S(1)} async-done(((bf16[64,16,896]{2,1,0:T(8,128)(2,1)}), bf16[64,16,896]{2,1,0:T(8,128)(2,1)S(1)}, u32[]{:S(2)}, u32[]{:S(2)}) %all-to-all-start) | async-done | bytes 1835040 | tf_op jit(solution)/shard_map/all_to_all | solution.py:142
  62.1 1.2 copy-done.3
  63.3 5.4 %all-to-all-start.1 = ((bf16[64,16,896]{2,1,0:T(8,128)(2,1)}), bf16[64,16,896]{2,1,0:T(8,128)(2,1)S(1)}, u32[]{:S(2)}, u32[]{:S(2)}) async-start(bf16[64,16,896]{2,1,0:T(8,128)(2,1)} %bitcast.68), calls=%async_computation.1 | async-start | bytes 3670016 | tf_op jit(solution)/shard_map/all_to_all | solution.py:142
  68.8 1.7 collective-permute-start.2
  70.4 1.7 collective-permute-start
  72.1 6.9 %shard_map.104 = (bf16[896,768]{1,0:T(8,128)(2,1)}, bf16[896,768]{1,0:T(8,128)(2,1)}, bf16[896,768]{1,0:T(8,128)(2,1)}) custom-call(s32[1]{0:T(128)} %bitcast.7.me, bf16[4,896,256]{2,1,0:T(8,128)(2,1)} %bitcast.52, bf16[4,896,256]{2,1,0:T(8,128)(2,1)} %bitcast.56, bf16[256,3584]{1,0:T(8,128)(2,1)} %bitcast.64), custom_call_target="tpu_custom_call" | custom-call | bytes 5505028 | tf_op jit(solution)/shard_map/pallas_call | solution.py:108
  79.0 1.8 collective-permute-start.4
  80.8 0.6 collective-permute-start.5
  81.5 1.0 collective-permute-start.6
  82.4 31.3 %collective-permute-done.2.last = bf16[1024,896]{1,0:T(8,128)(2,1)} collective-permute-done((bf16[1024,896]{1,0:T(8,128)(2,1)}, bf16[1024,896]{1,0:T(8,128)(2,1)}, u32[]{:S(2)}, u32[]{:S(2)}) %collective-permute-start.2) | collective-permute-done | bytes 1835040 | tf_op jit(solution)/shard_map/ppermute | solution.py:136
  113.7 2.2 slice.37
  115.9 28.1 %collective-permute-start.3 = (bf16[512,896]{1,0:T(8,128)(2,1)}, bf16[512,896]{1,0:T(8,128)(2,1)S(1)}, u32[]{:S(2)}, u32[]{:S(2)}) collective-permute-start(bf16[512,896]{1,0:T(8,128)(2,1)} %slice.37), channel_id=1, source_target_pairs={{3,0},{0,1},{1,2},{2,3},{7,4},{4,5},{5,6},{6,7},{11,8},{8,9},{9,10... | collective-permute-start | bytes 2752520 | tf_op jit(solution)/shard_map/ppermute | solution.py:136
  144.0 2.2 slice.36
  146.2 6.2 %shard_map.103.refs_0_.refs_8_ = bf16[896,768]{1,0:T(8,128)(2,1)} custom-call(s32[1]{0:T(128)} %bitcast.7.me, bf16[4,896,256]{2,1,0:T(8,128)(2,1)} %bitcast.53, bf16[4,896,256]{2,1,0:T(8,128)(2,1)} %bitcast.57, bf16[256,3584]{1,0:T(8,128)(2,1)} %bitcast.65), custom_call_target="tpu_custom_call" | custom-call | bytes 5505028 | tf_op jit(solution)/shard_map/pallas_call | solution.py:108
  152.4 19.1 %collective-permute-done.4.refs_1_.refs_9_ = bf16[896,768]{1,0:T(8,128)(2,1)} collective-permute-done((bf16[896,768]{1,0:T(8,128)(2,1)}, bf16[896,768]{1,0:T(8,128)(2,1)}, u32[]{:S(2)}, u32[]{:S(2)}) %collective-permute-start.4) | collective-permute-done | bytes 1376288 | tf_op jit(solution)/shard_map/ppermute | solution.py:136
  171.5 0.8 collective-permute-done.6.refs_3_.refs_11_
  172.3 1.2 copy-done.1
  173.5 5.6 %shard_map.105 = (f32[1024,256]{1,0:T(8,128)}, bf16[1024,256]{1,0:T(8,128)(2,1)}, bf16[1024,256]{1,0:T(8,128)(2,1)}, bf16[1024,256]{1,0:T(8,128)(2,1)}) custom-call(bf16[1024,896]{1,0:T(8,128)(2,1)} %bitcast.47, bf16[896,768]{1,0:T(8,128)(2,1)} %shard_map.103.refs_0_.refs_8_, bf16[896,768]{1,0:T(8,128)(2,1)} %collective-permute-done.4.refs_1_.refs_9_, ...), custom_call_target="tpu_custom_call" | custom-call | flops 1879048192 | bytes 7340032 | tf_op jit(solution)/shard_map/pallas_call | solution.py:108
  179.1 2.7 collective-permute-start.7
  181.8 2.0 collective-permute-start.8
  183.8 0.8 collective-permute-start.9
  184.6 8.0 %shard_map.102.partial = f32[1024,512]{1,0:T(8,128)} custom-call(s32[1]{0:T(128)} %bitcast.7.me, bf16[1024,896]{1,0:T(8,128)(2,1)} %bitcast.62, bf16[1024,896]{1,0:T(8,128)(2,1)} %collective-permute-done.after, bf16[1024,896]{1,0:T(8,128)(2,1)} %collective-permute-done.2.last, bf16[4,896,256]{2,1,0:T(8,128)(2,1)} %bitcast.54, bf16[4,896,256]{2,1,0:T(8,128)(2,1)} %bitcast.58), custom_call_target="tpu_custom_call" | custom-call | flops 2818572288 | bytes 9175044 | tf_op jit(solution)/shard_map/pallas_call | solution.py:108
  192.6 9.7 %collective-permute-done.7.refs_1_ = bf16[1024,256]{1,0:T(8,128)(2,1)S(1)} collective-permute-done((bf16[1024,256]{1,0:T(8,128)(2,1)}, bf16[1024,256]{1,0:T(8,128)(2,1)S(1)}, u32[]{:S(2)}, u32[]{:S(2)}) %collective-permute-start.7) | collective-permute-done | bytes 524320 | tf_op jit(solution)/shard_map/ppermute | solution.py:139
  202.3 12.5 %collective-permute-done.8.refs_2_ = bf16[1024,256]{1,0:T(8,128)(2,1)S(1)} collective-permute-done((bf16[1024,256]{1,0:T(8,128)(2,1)}, bf16[1024,256]{1,0:T(8,128)(2,1)S(1)}, u32[]{:S(2)}, u32[]{:S(2)}) %collective-permute-start.8) | collective-permute-done | bytes 524320 | tf_op jit(solution)/shard_map/ppermute | solution.py:139
  214.8 0.8 copy-done.8
  216.0 6.1 %shard_map.106 = (bf16[1024,256]{1,0:T(8,128)(2,1)}, bf16[512,512]{1,0:T(8,128)(2,1)}, bf16[512,512]{1,0:T(8,128)(2,1)}) custom-call(s32[1]{0:T(128)} %bitcast.7.me, bf16[512,896]{1,0:T(8,128)(2,1)} %collective-permute-done.1.far_a, bf16[512,896]{1,0:T(8,128)(2,1)} %copy-done.5, f32[1024,512]{1,0:T(8,128)} %shard_map.102.partial, ...), custom_call_target="tpu_custom_call" | custom-call | flops 939524096 | bytes 10223620 | tf_op jit(solution)/shard_map/pallas_call | solution.py:108
  222.1 1.7 collective-permute-start.10
  223.8 0.4 collective-permute-start.14
  224.4 3.0 collective-permute-start.13
  227.4 9.7 %collective-permute-done.10.refs_1_ = bf16[512,512]{1,0:T(8,128)(2,1)S(1)} collective-permute-done((bf16[512,512]{1,0:T(8,128)(2,1)}, bf16[512,512]{1,0:T(8,128)(2,1)S(1)}, u32[]{:S(2)}, u32[]{:S(2)}) %collective-permute-start.10) | collective-permute-done | bytes 524320 | tf_op jit(solution)/shard_map/ppermute | solution.py:136
  237.2 2.9 collective-permute-start.11
  240.1 3.4 broadcast_in_dim.58
  243.5 1.4 constant_dynamic-update-slice_fusion.4
  244.9 3.0 constant_dynamic-update-slice_fusion.3
  247.9 2.7 maximum_dynamic-update-slice_fusion
  250.6 0.7 collective-permute-done.12.refs_3_
  251.2 3.9 %collective-permute-start.18 = (bf16[1024,256]{1,0:T(8,128)(2,1)}, bf16[1024,256]{1,0:T(8,128)(2,1)}, u32[]{:S(2)}, u32[]{:S(2)}) collective-permute-start(bf16[1024,256]{1,0:T(8,128)(2,1)} %get-tuple-element.23), channel_id=1, source_target_pairs={{2,0},{3,1},{0,2},{1,3},{6,4},{7,5},{4,6},{5,7},{10,8},{11,9},{8,1... | collective-permute-start | bytes 1572872 | tf_op jit(solution)/shard_map/ppermute | solution.py:136
  255.2 14.5 %collective-permute-done.11.refs_2_ = bf16[512,512]{1,0:T(8,128)(2,1)S(1)} collective-permute-done((bf16[512,512]{1,0:T(8,128)(2,1)S(1)}, bf16[512,512]{1,0:T(8,128)(2,1)S(1)}, u32[]{:S(2)}, u32[]{:S(2)}) %collective-permute-start.11) | collective-permute-done | bytes 524320 | tf_op jit(solution)/shard_map/ppermute | solution.py:136
  269.7 0.8 copy-done.17
  270.5 9.3 %shard_map.107 = bf16[1024,896]{1,0:T(8,128)(2,1)} custom-call(bf16[512,512]{1,0:T(8,128)(2,1)} %get-tuple-element.21.refs_0_, bf16[512,512]{1,0:T(8,128)(2,1)} %copy-done.13, bf16[512,512]{1,0:T(8,128)(2,1)} %copy-done.17, bf16[512,512]{1,0:T(8,128)(2,1)} %copy-done.15, bf16[512,512]{1,0:T(8,128)(2,1)} %get-tuple-element.22.refs_4_, ...), custom_call_target="tpu_custom_call" | custom-call | flops 3758096384 | bytes 9699328 | tf_op jit(solution)/shard_map/pallas_call | solution.py:108
  279.8 10.5 %all-to-all-start.2 = ((bf16[64,16,896]{2,1,0:T(8,128)(2,1)}), bf16[64,16,896]{2,1,0:T(8,128)(2,1)S(1)}, u32[]{:S(2)}, u32[]{:S(2)}) async-start(bf16[64,16,896]{2,1,0:T(8,128)(2,1)} %bitcast.66), calls=%async_computation.2 | async-start | bytes 3670016 | tf_op jit(solution)/shard_map/all_to_all | solution.py:142
  290.3 3.0 constant_dynamic-update-slice_fusion.2
  293.3 6.5 %fusion.1 = bf16[1,3584,256]{2,1,0:T(8,128)(2,1)} fusion(bf16[1024,3584]{1,0:T(8,128)(2,1)} %constant_dynamic-update-slice_fusion.2, bf16[1024,512]{1,0:T(8,128)(2,1)S(1)} %constant_dynamic-update-slice_fusion), kind=kOutput, calls=%fused_computation.3 | convolution fusion | flops 1879965696 | bytes 9699328 | tf_op jit(solution)/shard_map/dot_general | solution.py:17
  299.8 6.4 %fusion = bf16[1,3584,256]{2,1,0:T(8,128)(2,1)} fusion(bf16[1024,3584]{1,0:T(8,128)(2,1)} %constant_dynamic-update-slice_fusion.2, bf16[1024,512]{1,0:T(8,128)(2,1)S(1)} %constant_dynamic-update-slice_fusion), kind=kOutput, calls=%fused_computation.2 | convolution fusion | flops 1879965696 | bytes 9699328 | tf_op jit(solution)/shard_map/dot_general | solution.py:17
  306.2 1.3 broadcast_in_dim.61
  307.6 0.8 copy-done.2
  308.4 2.5 fusion.3
  310.9 1.8 convolution_convert_fusion.5
  312.7 0.5 collective-permute-start.17
  313.3 1.8 convolution_convert_fusion.4
  315.0 5.1 %collective-permute-start.19 = (bf16[256,896]{1,0:T(8,128)(2,1)S(1)}, bf16[256,896]{1,0:T(8,128)(2,1)S(1)}, u32[]{:S(2)}, u32[]{:S(2)}) collective-permute-start(bf16[256,896]{1,0:T(8,128)(2,1)S(1)} %convolution_convert_fusion.4), channel_id=1, source_target_pairs={{0,2},{1,3},{2,0},{3,1},{4,6},{5,7},{6,4},{7,5},{8,10},{9,11},{10,... | collective-permute-start | bytes 1376264 | tf_op jit(solution)/shard_map/ppermute | solution.py:139
  320.2 1.8 convolution_convert_fusion.3
  322.1 5.6 %collective-permute-done.17 = bf16[256,896]{1,0:T(8,128)(2,1)S(1)} collective-permute-done((bf16[256,896]{1,0:T(8,128)(2,1)S(1)}, bf16[256,896]{1,0:T(8,128)(2,1)S(1)}, u32[]{:S(2)}, u32[]{:S(2)}) %collective-permute-start.17) | collective-permute-done | bytes 458784 | tf_op jit(solution)/shard_map/ppermute | solution.py:139
  327.6 0.8 bitcast_dynamic-update-slice_fusion.2
  328.5 10.2 %collective-permute-done.19 = bf16[256,896]{1,0:T(8,128)(2,1)S(1)} collective-permute-done((bf16[256,896]{1,0:T(8,128)(2,1)S(1)}, bf16[256,896]{1,0:T(8,128)(2,1)S(1)}, u32[]{:S(2)}, u32[]{:S(2)}) %collective-permute-start.19) | collective-permute-done | bytes 458784 | tf_op jit(solution)/shard_map/ppermute | solution.py:139
  338.7 0.8 bitcast_dynamic-update-slice_fusion.1
  339.5 0.5 collective-permute-done.21
  340.0 0.8 bitcast_dynamic-update-slice_fusion
  340.8 1.5 convolution_convert_fusion.7
  (60 shorter events, 1.5 us)
Async XLA Ops:
  0.6 1.7 copy-start
  4.3 12.2 %copy-start.12 = (f32[256,2]{0,1:T(2,128)S(1)}, f32[256,2]{0,1:T(2,128)}, u32[]{:S(2)}) copy-start(f32[256,2]{0,1:T(2,128)} %param.10) | copy-start | bytes 6148
  4.3 12.5 %copy-start.18 = (bf16[256,896]{1,0:T(8,128)(2,1)S(1)}, bf16[256,896]{1,0:T(8,128)(2,1)}, u32[]{:S(2)}) copy-start(bf16[256,896]{1,0:T(8,128)(2,1)} %param.8) | copy-start | bytes 1376260
  4.3 57.8 %all-to-all-start = ((bf16[64,16,896]{2,1,0:T(8,128)(2,1)}), bf16[64,16,896]{2,1,0:T(8,128)(2,1)S(1)}, u32[]{:S(2)}, u32[]{:S(2)}) async-start(bf16[64,16,896]{2,1,0:T(8,128)(2,1)} %bitcast.69), calls=%async_computation | async-start | bytes 3670016 | tf_op jit(solution)/shard_map/all_to_all | solution.py:142
  62.1 1.2 copy-start.3
  63.3 108.9 %all-to-all-start.1 = ((bf16[64,16,896]{2,1,0:T(8,128)(2,1)}), bf16[64,16,896]{2,1,0:T(8,128)(2,1)S(1)}, u32[]{:S(2)}, u32[]{:S(2)}) async-start(bf16[64,16,896]{2,1,0:T(8,128)(2,1)} %bitcast.68), calls=%async_computation.1 | async-start | bytes 3670016 | tf_op jit(solution)/shard_map/all_to_all | solution.py:142
  68.8 44.9 %collective-permute-start.2 = (bf16[1024,896]{1,0:T(8,128)(2,1)}, bf16[1024,896]{1,0:T(8,128)(2,1)}, u32[]{:S(2)}, u32[]{:S(2)}) collective-permute-start(bf16[1024,896]{1,0:T(8,128)(2,1)} %bitcast.60), channel_id=1, source_target_pairs={{3,0},{0,1},{1,2},{2,3},{7,4},{4,5},{5,6},{6,7},{11,8},{8,9},{9,10... | collective-permute-start | bytes 5505032 | tf_op jit(solution)/shard_map/ppermute | solution.py:136
  70.4 73.5 %collective-permute-start = (bf16[1024,896]{1,0:T(8,128)(2,1)}, bf16[1024,896]{1,0:T(8,128)(2,1)}, u32[]{:S(2)}, u32[]{:S(2)}) collective-permute-start(bf16[1024,896]{1,0:T(8,128)(2,1)} %bitcast.61), channel_id=1, source_target_pairs={{1,0},{2,1},{3,2},{0,3},{5,4},{6,5},{7,6},{4,7},{9,8},{10,9},{11,1... | collective-permute-start | bytes 5505032 | tf_op jit(solution)/shard_map/ppermute | solution.py:136
  79.0 92.4 %collective-permute-start.4 = (bf16[896,768]{1,0:T(8,128)(2,1)}, bf16[896,768]{1,0:T(8,128)(2,1)}, u32[]{:S(2)}, u32[]{:S(2)}) collective-permute-start(bf16[896,768]{1,0:T(8,128)(2,1)} %get-tuple-element.14), channel_id=1, source_target_pairs={{1,0},{2,1},{3,2},{0,3},{5,4},{6,5},{7,6},{4,7},{9,8},{10,9},{11,1... | collective-permute-start | bytes 4128776 | tf_op jit(solution)/shard_map/ppermute | solution.py:136
  80.8 90.6 %collective-permute-start.5 = (bf16[896,768]{1,0:T(8,128)(2,1)}, bf16[896,768]{1,0:T(8,128)(2,1)}, u32[]{:S(2)}, u32[]{:S(2)}) collective-permute-start(bf16[896,768]{1,0:T(8,128)(2,1)} %get-tuple-element.15), channel_id=1, source_target_pairs={{2,0},{3,1},{0,2},{1,3},{6,4},{7,5},{4,6},{5,7},{10,8},{11,9},{8,1... | collective-permute-start | bytes 4128776 | tf_op jit(solution)/shard_map/ppermute | solution.py:136
  81.5 90.8 %collective-permute-start.6 = (bf16[896,768]{1,0:T(8,128)(2,1)}, bf16[896,768]{1,0:T(8,128)(2,1)}, u32[]{:S(2)}, u32[]{:S(2)}) collective-permute-start(bf16[896,768]{1,0:T(8,128)(2,1)} %get-tuple-element.16), channel_id=1, source_target_pairs={{3,0},{0,1},{1,2},{2,3},{7,4},{4,5},{5,6},{6,7},{11,8},{8,9},{9,10... | collective-permute-start | bytes 4128776 | tf_op jit(solution)/shard_map/ppermute | solution.py:136
  115.9 98.8 %collective-permute-start.3 = (bf16[512,896]{1,0:T(8,128)(2,1)}, bf16[512,896]{1,0:T(8,128)(2,1)S(1)}, u32[]{:S(2)}, u32[]{:S(2)}) collective-permute-start(bf16[512,896]{1,0:T(8,128)(2,1)} %slice.37), channel_id=1, source_target_pairs={{3,0},{0,1},{1,2},{2,3},{7,4},{4,5},{5,6},{6,7},{11,8},{8,9},{9,10... | collective-permute-start | bytes 2752520 | tf_op jit(solution)/shard_map/ppermute | solution.py:136
  146.2 68.6 %collective-permute-start.1 = (bf16[512,896]{1,0:T(8,128)(2,1)}, bf16[512,896]{1,0:T(8,128)(2,1)}, u32[]{:S(2)}, u32[]{:S(2)}) collective-permute-start(bf16[512,896]{1,0:T(8,128)(2,1)} %slice.36), channel_id=1, source_target_pairs={{1,0},{2,1},{3,2},{0,3},{5,4},{6,5},{7,6},{4,7},{9,8},{10,9},{11,1... | collective-permute-start | bytes 2752520 | tf_op jit(solution)/shard_map/ppermute | solution.py:136
  172.3 1.2 copy-start.1
  179.1 23.2 %collective-permute-start.7 = (bf16[1024,256]{1,0:T(8,128)(2,1)}, bf16[1024,256]{1,0:T(8,128)(2,1)S(1)}, u32[]{:S(2)}, u32[]{:S(2)}) collective-permute-start(bf16[1024,256]{1,0:T(8,128)(2,1)} %get-tuple-element.18), channel_id=1, source_target_pairs={{0,1},{1,2},{2,3},{3,0},{4,5},{5,6},{6,7},{7,4},{8,9},{9,10},{10,1... | collective-permute-start | bytes 1572872 | tf_op jit(solution)/shard_map/ppermute | solution.py:139
  181.8 32.9 %collective-permute-start.8 = (bf16[1024,256]{1,0:T(8,128)(2,1)}, bf16[1024,256]{1,0:T(8,128)(2,1)S(1)}, u32[]{:S(2)}, u32[]{:S(2)}) collective-permute-start(bf16[1024,256]{1,0:T(8,128)(2,1)} %get-tuple-element.19), channel_id=1, source_target_pairs={{0,2},{1,3},{2,0},{3,1},{4,6},{5,7},{6,4},{7,5},{8,10},{9,11},{10,... | collective-permute-start | bytes 1572872 | tf_op jit(solution)/shard_map/ppermute | solution.py:139
  183.8 30.9 %collective-permute-start.9 = (bf16[1024,256]{1,0:T(8,128)(2,1)}, bf16[1024,256]{1,0:T(8,128)(2,1)S(1)}, u32[]{:S(2)}, u32[]{:S(2)}) collective-permute-start(bf16[1024,256]{1,0:T(8,128)(2,1)} %get-tuple-element.20), channel_id=1, source_target_pairs={{0,3},{1,0},{2,1},{3,2},{4,7},{5,4},{6,5},{7,6},{8,11},{9,8},{10,9... | collective-permute-start | bytes 1572872 | tf_op jit(solution)/shard_map/ppermute | solution.py:139
  202.3 12.5 %copy-start.7 = (bf16[1024,256]{1,0:T(8,128)(2,1)}, bf16[1024,256]{1,0:T(8,128)(2,1)S(1)}, u32[]{:S(2)}) copy-start(bf16[1024,256]{1,0:T(8,128)(2,1)S(1)} %collective-permute-done.7.refs_1_) | copy-start | bytes 1572868
  214.7 0.8 copy-start.8
  214.7 1.0 copy-start.9
  214.7 1.2 copy-start.5
  222.1 15.0 %collective-permute-start.10 = (bf16[512,512]{1,0:T(8,128)(2,1)}, bf16[512,512]{1,0:T(8,128)(2,1)S(1)}, u32[]{:S(2)}, u32[]{:S(2)}) collective-permute-start(bf16[512,512]{1,0:T(8,128)(2,1)} %get-tuple-element.21.refs_0_), channel_id=1, source_target_pairs={{1,0},{2,1},{3,2},{0,3},{5,4},{6,5},{7,6},{4,7},{9,8},{10,9},{11,1... | collective-permute-start | bytes 1572872 | tf_op jit(solution)/shard_map/ppermute | solution.py:136
  223.8 16.2 %collective-permute-start.14 = (bf16[512,512]{1,0:T(8,128)(2,1)}, bf16[512,512]{1,0:T(8,128)(2,1)S(1)}, u32[]{:S(2)}, u32[]{:S(2)}) collective-permute-start(bf16[512,512]{1,0:T(8,128)(2,1)} %get-tuple-element.22.refs_4_), channel_id=1, source_target_pairs={{3,0},{0,1},{1,2},{2,3},{7,4},{4,5},{5,6},{6,7},{11,8},{8,9},{9,10... | collective-permute-start | bytes 1572872 | tf_op jit(solution)/shard_map/ppermute | solution.py:136
  224.2 27.1 %collective-permute-start.12 = (bf16[512,512]{1,0:T(8,128)(2,1)}, bf16[512,512]{1,0:T(8,128)(2,1)S(1)}, u32[]{:S(2)}, u32[]{:S(2)}) collective-permute-start(bf16[512,512]{1,0:T(8,128)(2,1)} %get-tuple-element.21.refs_0_), channel_id=1, source_target_pairs={{3,0},{0,1},{1,2},{2,3},{7,4},{4,5},{5,6},{6,7},{11,8},{8,9},{9,10... | collective-permute-start | bytes 1572872 | tf_op jit(solution)/shard_map/ppermute | solution.py:136
  224.4 30.8 %collective-permute-start.13 = (bf16[512,512]{1,0:T(8,128)(2,1)}, bf16[512,512]{1,0:T(8,128)(2,1)S(1)}, u32[]{:S(2)}, u32[]{:S(2)}) collective-permute-start(bf16[512,512]{1,0:T(8,128)(2,1)} %get-tuple-element.22.refs_4_), channel_id=1, source_target_pairs={{1,0},{2,1},{3,2},{0,3},{5,4},{6,5},{7,6},{4,7},{9,8},{10,9},{11,1... | collective-permute-start | bytes 1572872 | tf_op jit(solution)/shard_map/ppermute | solution.py:136
  237.2 6.3 %copy-start.13 = (bf16[512,512]{1,0:T(8,128)(2,1)}, bf16[512,512]{1,0:T(8,128)(2,1)S(1)}, u32[]{:S(2)}) copy-start(bf16[512,512]{1,0:T(8,128)(2,1)S(1)} %collective-permute-done.10.refs_1_) | copy-start | bytes 1572868
  237.2 32.5 %collective-permute-start.11 = (bf16[512,512]{1,0:T(8,128)(2,1)S(1)}, bf16[512,512]{1,0:T(8,128)(2,1)S(1)}, u32[]{:S(2)}, u32[]{:S(2)}) collective-permute-start(bf16[512,512]{1,0:T(8,128)(2,1)S(1)} %collective-permute-done.10.refs_1_), channel_id=1, source_target_pairs={{1,0},{2,1},{3,2},{0,3},{5,4},{6,5},{7,6},{4,7},{9,8},{10,9},{11,1... | collective-permute-start | bytes 1572872 | tf_op jit(solution)/shard_map/ppermute | solution.py:136
  240.0 3.4 %copy-start.14 = (bf16[512,512]{1,0:T(8,128)(2,1)}, bf16[512,512]{1,0:T(8,128)(2,1)S(1)}, u32[]{:S(2)}) copy-start(bf16[512,512]{1,0:T(8,128)(2,1)S(1)} %collective-permute-done.14.refs_7_) | copy-start | bytes 1572868
  240.0 29.6 %collective-permute-start.15 = (bf16[512,512]{1,0:T(8,128)(2,1)S(1)}, bf16[512,512]{1,0:T(8,128)(2,1)}, u32[]{:S(2)}, u32[]{:S(2)}) collective-permute-start(bf16[512,512]{1,0:T(8,128)(2,1)S(1)} %collective-permute-done.14.refs_7_), channel_id=1, source_target_pairs={{3,0},{0,1},{1,2},{2,3},{7,4},{4,5},{5,6},{6,7},{11,8},{8,9},{9,10... | collective-permute-start | bytes 1572872 | tf_op jit(solution)/shard_map/ppermute | solution.py:136
  240.1 3.4 copy-start.4
  244.9 3.0 copy-start.6
  247.9 72.3 %collective-permute-start.20 = (bf16[1024,256]{1,0:T(8,128)(2,1)}, bf16[1024,256]{1,0:T(8,128)(2,1)}, u32[]{:S(2)}, u32[]{:S(2)}) collective-permute-start(bf16[1024,256]{1,0:T(8,128)(2,1)} %get-tuple-element.23), channel_id=1, source_target_pairs={{3,0},{0,1},{1,2},{2,3},{7,4},{4,5},{5,6},{6,7},{11,8},{8,9},{9,10... | collective-permute-start | bytes 1572872 | tf_op jit(solution)/shard_map/ppermute | solution.py:136
  251.2 18.4 %copy-start.15 = (bf16[512,512]{1,0:T(8,128)(2,1)}, bf16[512,512]{1,0:T(8,128)(2,1)S(1)}, u32[]{:S(2)}) copy-start(bf16[512,512]{1,0:T(8,128)(2,1)S(1)} %collective-permute-done.12.refs_3_) | copy-start | bytes 1572868
  251.2 62.0 %collective-permute-start.18 = (bf16[1024,256]{1,0:T(8,128)(2,1)}, bf16[1024,256]{1,0:T(8,128)(2,1)}, u32[]{:S(2)}, u32[]{:S(2)}) collective-permute-start(bf16[1024,256]{1,0:T(8,128)(2,1)} %get-tuple-element.23), channel_id=1, source_target_pairs={{2,0},{3,1},{0,2},{1,3},{6,4},{7,5},{4,6},{5,7},{10,8},{11,9},{8,1... | collective-permute-start | bytes 1572872 | tf_op jit(solution)/shard_map/ppermute | solution.py:136
  255.2 14.5 %copy-start.16 = (bf16[512,512]{1,0:T(8,128)(2,1)}, bf16[512,512]{1,0:T(8,128)(2,1)S(1)}, u32[]{:S(2)}) copy-start(bf16[512,512]{1,0:T(8,128)(2,1)S(1)} %collective-permute-done.13.refs_5_) | copy-start | bytes 1572868
  255.2 55.7 %collective-permute-start.16 = (bf16[1024,256]{1,0:T(8,128)(2,1)}, bf16[1024,256]{1,0:T(8,128)(2,1)}, u32[]{:S(2)}, u32[]{:S(2)}) collective-permute-start(bf16[1024,256]{1,0:T(8,128)(2,1)} %get-tuple-element.23), channel_id=1, source_target_pairs={{1,0},{2,1},{3,2},{0,3},{5,4},{6,5},{7,6},{4,7},{9,8},{10,9},{11,1... | collective-permute-start | bytes 1572872 | tf_op jit(solution)/shard_map/ppermute | solution.py:136
  269.7 0.8 copy-start.17
  279.7 10.5 %copy-start.11 = (bf16[512,512]{1,0:T(8,128)(2,1)S(1)}, bf16[512,512]{1,0:T(8,128)(2,1)}, u32[]{:S(2)}) copy-start(bf16[512,512]{1,0:T(8,128)(2,1)} %get-tuple-element.21.refs_0_) | copy-start | bytes 1572868
  279.7 10.5 %copy-start.10 = (bf16[512,512]{1,0:T(8,128)(2,1)S(1)}, bf16[512,512]{1,0:T(8,128)(2,1)}, u32[]{:S(2)}) copy-start(bf16[512,512]{1,0:T(8,128)(2,1)} %get-tuple-element.22.refs_4_) | copy-start | bytes 1572868
  279.8 61.0 %all-to-all-start.2 = ((bf16[64,16,896]{2,1,0:T(8,128)(2,1)}), bf16[64,16,896]{2,1,0:T(8,128)(2,1)S(1)}, u32[]{:S(2)}, u32[]{:S(2)}) async-start(bf16[64,16,896]{2,1,0:T(8,128)(2,1)} %bitcast.66), calls=%async_computation.2 | async-start | bytes 3670016 | tf_op jit(solution)/shard_map/all_to_all | solution.py:142
  306.2 2.2 copy-start.2
  312.7 14.9 %collective-permute-start.17 = (bf16[256,896]{1,0:T(8,128)(2,1)S(1)}, bf16[256,896]{1,0:T(8,128)(2,1)S(1)}, u32[]{:S(2)}, u32[]{:S(2)}) collective-permute-start(bf16[256,896]{1,0:T(8,128)(2,1)S(1)} %convolution_convert_fusion.5), channel_id=1, source_target_pairs={{0,1},{1,2},{2,3},{3,0},{4,5},{5,6},{6,7},{7,4},{8,9},{9,10},{10,1... | collective-permute-start | bytes 1376264 | tf_op jit(solution)/shard_map/ppermute | solution.py:139
  315.0 23.6 %collective-permute-start.19 = (bf16[256,896]{1,0:T(8,128)(2,1)S(1)}, bf16[256,896]{1,0:T(8,128)(2,1)S(1)}, u32[]{:S(2)}, u32[]{:S(2)}) collective-permute-start(bf16[256,896]{1,0:T(8,128)(2,1)S(1)} %convolution_convert_fusion.4), channel_id=1, source_target_pairs={{0,2},{1,3},{2,0},{3,1},{4,6},{5,7},{6,4},{7,5},{8,10},{9,11},{10,... | collective-permute-start | bytes 1376264 | tf_op jit(solution)/shard_map/ppermute | solution.py:139
  322.0 18.0 %collective-permute-start.21 = (bf16[256,896]{1,0:T(8,128)(2,1)S(1)}, bf16[256,896]{1,0:T(8,128)(2,1)S(1)}, u32[]{:S(2)}, u32[]{:S(2)}) collective-permute-start(bf16[256,896]{1,0:T(8,128)(2,1)S(1)} %convolution_convert_fusion.3), channel_id=1, source_target_pairs={{0,3},{1,0},{2,1},{3,2},{4,7},{5,4},{6,5},{7,6},{8,11},{9,8},{10,9... | collective-permute-start | bytes 1376264 | tf_op jit(solution)/shard_map/ppermute | solution.py:139

commit v3 on v2

--- a/solution.py
+++ b/solution.py
@@ -25,12 +25,15 @@
     step = pl.program_id(0)
     n, span, hid = gate.shape
     width = down.shape[1] // n
+    rows, columns = (lax.broadcasted_iota(jnp.int32, (span, span), d) for d in (0, 1))
+    same = (rows == columns).astype(BF)
     for k, out in zip(places, packed):
         q = lax.rem(me[0] + n - k, n)
         out[:, 0:hid] = gate[q]
         out[:, hid : 2 * hid] = up[q]
         start = pl.multiple_of(q * width + step * span, 128)
-        out[:, 2 * hid : 3 * hid] = down[:, pl.ds(start, span)].T
+        turned = mm(same, down[:, pl.ds(start, span)], ((1,), (1,)))
+        out[:, 2 * hid : 3 * hid] = turned.astype(BF)
 
 
 def partial_kernel(me, own, after, last, gate, up, out):
@@ -82,9 +85,8 @@
         grads_b[:, hid:] = d_up
 
 
-def dx_kernel(*refs):
+def dx_kernel(n, *refs):
     out, d = refs[-2:]
-    n = (len(refs) - 2) // 3
     width = refs[0].shape[1]
     step = pl.program_id(0)
 
@@ -98,9 +100,12 @@
         for k in range(n):
             d[:, k * width : (k + 1) * width] = refs[n + k][...]
 
-    out[...] = sum(
+    total = sum(
         mm(d[:, k * width : (k + 1) * width], refs[2 * n + k][...], ((1,), (1,))) for k in range(n)
-    ).astype(BF)
+    )
+    for so_far in refs[3 * n : -2]:
+        total += so_far[...]
+    out[...] = total.astype(out.dtype)
 
 
 def call(kernel, scalars, ins, outs, grid, scratch, flops, operands):
@@ -258,19 +263,26 @@
     next_a, last_b = fetch(d_a, 1), fetch(d_b, back_one)
     next_b, last_a = fetch(d_b, 1), fetch(d_a, back_one)
     passed_a, passed_b = fetch(next_a, 1), fetch(last_b, back_one)
-    halves = (d_a, next_a, passed_a, last_a, d_b, next_b, passed_b, last_b)
-    (dx,) = call(
-        dx_kernel,
-        0,
-        [upper_rows(2 * hid)] * n_tp
-        + [lower_rows(2 * hid)] * n_tp
-        + [pl.BlockSpec((quarter, 2 * hid), lambda i: (0, 0))] * n_tp,
-        [(array((rows, quarter), BF), by_rows(quarter))],
-        (TILES,),
-        [pltpu.VMEM((tile, 2 * hid * n_tp), BF)],
-        4 * n_tp * rows * quarter * hid,
-        (*halves, *packed),
-    )
+
+    def add_up(upper, lower, weights, so_far, kind):
+        n = len(upper)
+        return call(
+            functools.partial(dx_kernel, n),
+            0,
+            [upper_rows(2 * hid)] * n
+            + [lower_rows(2 * hid)] * n
+            + [pl.BlockSpec((quarter, 2 * hid), lambda i: (0, 0))] * n
+            + [by_rows(quarter)] * len(so_far),
+            [(array((rows, quarter), kind), by_rows(quarter))],
+            (TILES,),
+            [pltpu.VMEM((tile, 2 * hid * n), BF)],
+            4 * n * rows * quarter * hid,
+            (*upper, *lower, *weights, *so_far),
+        )
+
+    near = (packed[0], packed[1], packed[back_one])
+    so_far = add_up((d_a, next_a, last_a), (d_b, next_b, last_b), near, (), F32)
+    (dx,) = add_up((passed_a,), (passed_b,), (packed[2],), so_far, BF)
     dx = exchange(dx)
     grad_tokens = mm(pick, dx, ((0,), (0,))).astype(BF)
 

time: 344 us -> 340 us (0.988)
  waiting for transfers between devices: 158 us -> 151 us
  Pallas kernels: 42.1 us -> 47.3 us
    ppermute x16, waiting for transfers between devices: 76.1 us -> 69.2 us  [fetch(): return lax.ppermute(a, 'tp', [((i + k) % n_tp, i) for i in range(n_tp)])]
    pallas_call x6 -> x7, Pallas kernels: 42.1 us -> 47.3 us  [call(): pl.pallas_call(kernel, out_shape=[s for s, _ in outs], grid_spec=pltpu.Pr...]
  transfers between devices with their start and end apart: 25 -> 25, of which waited for: 12 -> 12; matrix products, arithmetic and copies ran while one was open for 13% -> 13% of each run, Pallas kernels for 11% -> 12%
where the time goes in v3:
time: 340 us; the launch traced here: 338 us
  waiting for transfers between devices  151 us (44%)
  starting transfers between devices  84.1 us (25%)
  Pallas kernels  47.3 us (14%)
  matrix products  26.4 us (8%)
  local copies, waits for them, and re-layouts  25.2 us (7%)
  other arithmetic  3.74 us (1%)
    ppermute x16, waiting for transfers between devices, fetch(): return lax.ppermute(a, 'tp', [((i + k) % n_tp, i) for i in range(n_tp)])  69.2 us
    pallas_call x7, Pallas kernels, call(): pl.pallas_call(kernel, out_shape=[s for s, _ in outs], grid_spec=pltpu.Pr...  47.3 us
    ppermute x16, starting transfers between devices, fetch(): return lax.ppermute(a, 'tp', [((i + k) % n_tp, i) for i in range(n_tp)])  44.8 us
    all_to_all x3, waiting for transfers between devices, exchange(): lax.all_to_all(a.reshape(n_src, -1, quarter), 'ep', split_axis=0, concat_...  43.3 us
    ppermute x6, waiting for transfers between devices, give(): return lax.ppermute(a, 'tp', [(i, (i + k) % n_tp) for i in range(n_tp)])  38.4 us
    all_to_all x3, starting transfers between devices, exchange(): lax.all_to_all(a.reshape(n_src, -1, quarter), 'ep', split_axis=0, concat_...  28 us
    dot_general x10, matrix products, mm(): lax.dot_general(left, right, (dims, ((), ())), preferred_element_type=F32)  26.4 us
    ppermute x6, starting transfers between devices, give(): return lax.ppermute(a, 'tp', [(i, (i + k) % n_tp) for i in range(n_tp)])  11.3 us
  transfers between devices with their start and end apart: 25, of which 12 were waited for; matrix products, arithmetic and copies ran while one was open for 13% of the time, Pallas kernels for 12%

profile of v3, /device:TPU:2, one launch (start us, length us, event | category | flops | bytes accessed | tf_op | source)
XLA Modules:
  0.0 338.5 jit_solution(8980334471349371933)
XLA Ops:
  0.6 0.8 fusion.27
  1.6 0.8 multiply_add_fusion.1
  2.4 1.9 convolution_convert_fusion.2
  4.3 12.1 %all-to-all-start = ((bf16[64,16,896]{2,1,0:T(8,128)(2,1)}), bf16[64,16,896]{2,1,0:T(8,128)(2,1)S(1)}, u32[]{:S(2)}, u32[]{:S(2)}) async-start(bf16[64,16,896]{2,1,0:T(8,128)(2,1)} %bitcast.69), calls=%async_computation | async-start | bytes 3670016 | tf_op jit(solution)/shard_map/all_to_all | solution.py:147
  16.9 2.0 multiply_convert_fusion
  18.9 43.3 %all-to-all-done = bf16[64,16,896]{2,1,0:T(8,128)(2,1)S(1)} async-done(((bf16[64,16,896]{2,1,0:T(8,128)(2,1)}), bf16[64,16,896]{2,1,0:T(8,128)(2,1)S(1)}, u32[]{:S(2)}, u32[]{:S(2)}) %all-to-all-start) | async-done | bytes 1835040 | tf_op jit(solution)/shard_map/all_to_all | solution.py:147
  62.1 1.2 copy-done.4
  63.3 5.4 %all-to-all-start.1 = ((bf16[64,16,896]{2,1,0:T(8,128)(2,1)}), bf16[64,16,896]{2,1,0:T(8,128)(2,1)S(1)}, u32[]{:S(2)}, u32[]{:S(2)}) async-start(bf16[64,16,896]{2,1,0:T(8,128)(2,1)} %bitcast.68), calls=%async_computation.1 | async-start | bytes 3670016 | tf_op jit(solution)/shard_map/all_to_all | solution.py:147
  68.8 1.7 collective-permute-start.2
  70.4 1.7 collective-permute-start
  72.1 7.5 %shard_map.104 = (bf16[896,768]{1,0:T(8,128)(2,1)}, bf16[896,768]{1,0:T(8,128)(2,1)}, bf16[896,768]{1,0:T(8,128)(2,1)}) custom-call(s32[1]{0:T(128)} %bitcast.7.me, bf16[4,896,256]{2,1,0:T(8,128)(2,1)} %bitcast.52, bf16[4,896,256]{2,1,0:T(8,128)(2,1)} %bitcast.56, bf16[256,3584]{1,0:T(8,128)(2,1)} %bitcast.64), custom_call_target="tpu_custom_call" | custom-call | bytes 5505028 | tf_op jit(solution)/shard_map/pallas_call | solution.py:113
  79.6 1.8 collective-permute-start.4
  81.4 0.6 collective-permute-start.5
  82.0 1.0 collective-permute-start.6
  83.0 30.7 %collective-permute-done.2.last = bf16[1024,896]{1,0:T(8,128)(2,1)} collective-permute-done((bf16[1024,896]{1,0:T(8,128)(2,1)}, bf16[1024,896]{1,0:T(8,128)(2,1)}, u32[]{:S(2)}, u32[]{:S(2)}) %collective-permute-start.2) | collective-permute-done | bytes 1835040 | tf_op jit(solution)/shard_map/ppermute | solution.py:141
  113.7 2.2 slice.37
  115.9 28.1 %collective-permute-start.3 = (bf16[512,896]{1,0:T(8,128)(2,1)}, bf16[512,896]{1,0:T(8,128)(2,1)S(1)}, u32[]{:S(2)}, u32[]{:S(2)}) collective-permute-start(bf16[512,896]{1,0:T(8,128)(2,1)} %slice.37), channel_id=1, source_target_pairs={{3,0},{0,1},{1,2},{2,3},{7,4},{4,5},{5,6},{6,7},{11,8},{8,9},{9,10... | collective-permute-start | bytes 2752520 | tf_op jit(solution)/shard_map/ppermute | solution.py:141
  144.0 2.2 slice.36
  146.1 6.5 %shard_map.103.refs_0_.refs_6_ = bf16[896,768]{1,0:T(8,128)(2,1)} custom-call(s32[1]{0:T(128)} %bitcast.7.me, bf16[4,896,256]{2,1,0:T(8,128)(2,1)} %bitcast.53, bf16[4,896,256]{2,1,0:T(8,128)(2,1)} %bitcast.57, bf16[256,3584]{1,0:T(8,128)(2,1)} %bitcast.65), custom_call_target="tpu_custom_call" | custom-call | bytes 5505028 | tf_op jit(solution)/shard_map/pallas_call | solution.py:113
  152.7 18.8 %collective-permute-done.4.refs_1_.refs_7_ = bf16[896,768]{1,0:T(8,128)(2,1)} collective-permute-done((bf16[896,768]{1,0:T(8,128)(2,1)}, bf16[896,768]{1,0:T(8,128)(2,1)}, u32[]{:S(2)}, u32[]{:S(2)}) %collective-permute-start.4) | collective-permute-done | bytes 1376288 | tf_op jit(solution)/shard_map/ppermute | solution.py:141
  171.5 0.8 collective-permute-done.6.refs_3_.refs_8_
  172.3 1.2 copy-done.2
  173.5 5.6 %shard_map.105 = (f32[1024,256]{1,0:T(8,128)}, bf16[1024,256]{1,0:T(8,128)(2,1)}, bf16[1024,256]{1,0:T(8,128)(2,1)}, bf16[1024,256]{1,0:T(8,128)(2,1)}) custom-call(bf16[1024,896]{1,0:T(8,128)(2,1)} %bitcast.47, bf16[896,768]{1,0:T(8,128)(2,1)} %shard_map.103.refs_0_.refs_6_, bf16[896,768]{1,0:T(8,128)(2,1)} %collective-permute-done.4.refs_1_.refs_7_, ...), custom_call_target="tpu_custom_call" | custom-call | flops 1879048192 | bytes 7340032 | tf_op jit(solution)/shard_map/pallas_call | solution.py:113
  179.1 2.7 collective-permute-start.7
  181.8 2.0 collective-permute-start.8
  183.8 0.8 collective-permute-start.9
  184.6 8.0 %shard_map.102.partial = f32[1024,512]{1,0:T(8,128)} custom-call(s32[1]{0:T(128)} %bitcast.7.me, bf16[1024,896]{1,0:T(8,128)(2,1)} %bitcast.62, bf16[1024,896]{1,0:T(8,128)(2,1)} %collective-permute-done.after, bf16[1024,896]{1,0:T(8,128)(2,1)} %collective-permute-done.2.last, bf16[4,896,256]{2,1,0:T(8,128)(2,1)} %bitcast.54, bf16[4,896,256]{2,1,0:T(8,128)(2,1)} %bitcast.58), custom_call_target="tpu_custom_call" | custom-call | flops 2818572288 | bytes 9175044 | tf_op jit(solution)/shard_map/pallas_call | solution.py:113
  192.6 9.7 %collective-permute-done.7.refs_1_ = bf16[1024,256]{1,0:T(8,128)(2,1)S(1)} collective-permute-done((bf16[1024,256]{1,0:T(8,128)(2,1)}, bf16[1024,256]{1,0:T(8,128)(2,1)S(1)}, u32[]{:S(2)}, u32[]{:S(2)}) %collective-permute-start.7) | collective-permute-done | bytes 524320 | tf_op jit(solution)/shard_map/ppermute | solution.py:144
  202.3 12.5 %collective-permute-done.8.refs_2_ = bf16[1024,256]{1,0:T(8,128)(2,1)S(1)} collective-permute-done((bf16[1024,256]{1,0:T(8,128)(2,1)}, bf16[1024,256]{1,0:T(8,128)(2,1)S(1)}, u32[]{:S(2)}, u32[]{:S(2)}) %collective-permute-start.8) | collective-permute-done | bytes 524320 | tf_op jit(solution)/shard_map/ppermute | solution.py:144
  214.8 0.8 copy-done.11
  216.0 6.2 %shard_map.106 = (bf16[1024,256]{1,0:T(8,128)(2,1)}, bf16[512,512]{1,0:T(8,128)(2,1)}, bf16[512,512]{1,0:T(8,128)(2,1)}) custom-call(s32[1]{0:T(128)} %bitcast.7.me, bf16[512,896]{1,0:T(8,128)(2,1)} %collective-permute-done.1.far_a, bf16[512,896]{1,0:T(8,128)(2,1)} %copy-done.6, f32[1024,512]{1,0:T(8,128)} %shard_map.102.partial, ...), custom_call_target="tpu_custom_call" | custom-call | flops 939524096 | bytes 10223620 | tf_op jit(solution)/shard_map/pallas_call | solution.py:113
  222.2 1.6 collective-permute-start.10
  224.4 3.1 collective-permute-start.15
  227.5 3.4 broadcast_in_dim.58
  230.9 1.4 constant_dynamic-update-slice_fusion.4
  232.3 4.9 %collective-permute-done.10.refs_1_ = bf16[512,512]{1,0:T(8,128)(2,1)S(1)} collective-permute-done((bf16[512,512]{1,0:T(8,128)(2,1)}, bf16[512,512]{1,0:T(8,128)(2,1)S(1)}, u32[]{:S(2)}, u32[]{:S(2)}) %collective-permute-start.10) | collective-permute-done | bytes 524320 | tf_op jit(solution)/shard_map/ppermute | solution.py:141
  237.2 2.8 collective-permute-start.11
  240.1 3.2 constant_dynamic-update-slice_fusion.3
  243.2 2.6 maximum_dynamic-update-slice_fusion
  245.9 5.4 %collective-permute-done.14.refs_2_ = bf16[512,512]{1,0:T(8,128)(2,1)S(1)} collective-permute-done((bf16[512,512]{1,0:T(8,128)(2,1)}, bf16[512,512]{1,0:T(8,128)(2,1)S(1)}, u32[]{:S(2)}, u32[]{:S(2)}) %collective-permute-start.14) | collective-permute-done | bytes 524320 | tf_op jit(solution)/shard_map/ppermute | solution.py:141
  251.3 1.9 collective-permute-start.16
  253.2 8.0 %shard_map.107.refs_3_ = f32[1024,896]{1,0:T(8,128)} custom-call(bf16[512,512]{1,0:T(8,128)(2,1)} %get-tuple-element.21.refs_0_, bf16[512,512]{1,0:T(8,128)(2,1)} %copy-done.13, bf16[512,512]{1,0:T(8,128)(2,1)} %copy-done.15, bf16[512,512]{1,0:T(8,128)(2,1)} %get-tuple-element.22.refs_3_, bf16[512,512]{1,0:T(8,128)(2,1)} %copy-done.16, ...), custom_call_target="tpu_custom_call" | custom-call | flops 2818572288 | bytes 7274496 | tf_op jit(solution)/shard_map/pallas_call | solution.py:113
  261.1 8.5 %collective-permute-done.11.refs_0_ = bf16[512,512]{1,0:T(8,128)(2,1)S(1)} collective-permute-done((bf16[512,512]{1,0:T(8,128)(2,1)S(1)}, bf16[512,512]{1,0:T(8,128)(2,1)S(1)}, u32[]{:S(2)}, u32[]{:S(2)}) %collective-permute-start.11) | collective-permute-done | bytes 524320 | tf_op jit(solution)/shard_map/ppermute | solution.py:141
  269.7 0.8 copy-done.17
  270.5 5.5 %shard_map.108 = bf16[1024,896]{1,0:T(8,128)(2,1)} custom-call(bf16[512,512]{1,0:T(8,128)(2,1)} %copy-done.17, bf16[512,512]{1,0:T(8,128)(2,1)} %collective-permute-done.13.refs_1_, bf16[896,768]{1,0:T(8,128)(2,1)} %collective-permute-done.5.refs_2_, f32[1024,896]{1,0:T(8,128)} %shard_map.107.refs_3_), custom_call_target="tpu_custom_call" | custom-call | flops 939524096 | bytes 6094848 | tf_op jit(solution)/shard_map/pallas_call | solution.py:113
  275.9 10.4 %all-to-all-start.2 = ((bf16[64,16,896]{2,1,0:T(8,128)(2,1)}), bf16[64,16,896]{2,1,0:T(8,128)(2,1)S(1)}, u32[]{:S(2)}, u32[]{:S(2)}) async-start(bf16[64,16,896]{2,1,0:T(8,128)(2,1)} %bitcast.66), calls=%async_computation.2 | async-start | bytes 3670016 | tf_op jit(solution)/shard_map/all_to_all | solution.py:147
  286.5 2.9 constant_dynamic-update-slice_fusion.2
  289.4 6.5 %fusion.1 = bf16[1,3584,256]{2,1,0:T(8,128)(2,1)} fusion(bf16[1024,3584]{1,0:T(8,128)(2,1)} %constant_dynamic-update-slice_fusion.2, bf16[1024,512]{1,0:T(8,128)(2,1)S(1)} %constant_dynamic-update-slice_fusion), kind=kOutput, calls=%fused_computation.3 | convolution fusion | flops 1879965696 | bytes 9699328 | tf_op jit(solution)/shard_map/dot_general | solution.py:17
  295.9 6.4 %fusion = bf16[1,3584,256]{2,1,0:T(8,128)(2,1)} fusion(bf16[1024,3584]{1,0:T(8,128)(2,1)} %constant_dynamic-update-slice_fusion.2, bf16[1024,512]{1,0:T(8,128)(2,1)S(1)} %constant_dynamic-update-slice_fusion), kind=kOutput, calls=%fused_computation.2 | convolution fusion | flops 1879965696 | bytes 9699328 | tf_op jit(solution)/shard_map/dot_general | solution.py:17
  302.3 1.3 broadcast_in_dim.61
  303.6 0.8 copy-done.3
  304.5 2.5 fusion.3
  307.0 1.8 convolution_convert_fusion.5
  308.8 0.7 collective-permute-start.17
  309.5 1.8 convolution_convert_fusion.4
  311.2 5.1 %collective-permute-start.19 = (bf16[256,896]{1,0:T(8,128)(2,1)S(1)}, bf16[256,896]{1,0:T(8,128)(2,1)S(1)}, u32[]{:S(2)}, u32[]{:S(2)}) collective-permute-start(bf16[256,896]{1,0:T(8,128)(2,1)S(1)} %convolution_convert_fusion.4), channel_id=1, source_target_pairs={{0,2},{1,3},{2,0},{3,1},{4,6},{5,7},{6,4},{7,5},{8,10},{9,11},{10,... | collective-permute-start | bytes 1376264 | tf_op jit(solution)/shard_map/ppermute | solution.py:144
  316.3 1.8 convolution_convert_fusion.3
  318.2 5.6 %collective-permute-done.17 = bf16[256,896]{1,0:T(8,128)(2,1)S(1)} collective-permute-done((bf16[256,896]{1,0:T(8,128)(2,1)S(1)}, bf16[256,896]{1,0:T(8,128)(2,1)S(1)}, u32[]{:S(2)}, u32[]{:S(2)}) %collective-permute-start.17) | collective-permute-done | bytes 458784 | tf_op jit(solution)/shard_map/ppermute | solution.py:144
  323.8 0.8 bitcast_dynamic-update-slice_fusion.2
  324.6 10.2 %collective-permute-done.19 = bf16[256,896]{1,0:T(8,128)(2,1)S(1)} collective-permute-done((bf16[256,896]{1,0:T(8,128)(2,1)S(1)}, bf16[256,896]{1,0:T(8,128)(2,1)S(1)}, u32[]{:S(2)}, u32[]{:S(2)}) %collective-permute-start.19) | collective-permute-done | bytes 458784 | tf_op jit(solution)/shard_map/ppermute | solution.py:144
  334.8 0.8 bitcast_dynamic-update-slice_fusion.1
  335.6 0.5 collective-permute-done.21
  336.1 0.8 bitcast_dynamic-update-slice_fusion
  336.9 1.5 convolution_convert_fusion.7
  (63 shorter events, 1.9 us)
Async XLA Ops:
  0.6 1.8 copy-start
  4.3 12.2 %copy-start.18 = (f32[256,2]{0,1:T(2,128)S(1)}, f32[256,2]{0,1:T(2,128)}, u32[]{:S(2)}) copy-start(f32[256,2]{0,1:T(2,128)} %param.10) | copy-start | bytes 6148
  4.3 12.5 %copy-start.19 = (bf16[256,896]{1,0:T(8,128)(2,1)S(1)}, bf16[256,896]{1,0:T(8,128)(2,1)}, u32[]{:S(2)}) copy-start(bf16[256,896]{1,0:T(8,128)(2,1)} %param.8) | copy-start | bytes 1376260
  4.3 57.8 %all-to-all-start = ((bf16[64,16,896]{2,1,0:T(8,128)(2,1)}), bf16[64,16,896]{2,1,0:T(8,128)(2,1)S(1)}, u32[]{:S(2)}, u32[]{:S(2)}) async-start(bf16[64,16,896]{2,1,0:T(8,128)(2,1)} %bitcast.69), calls=%async_computation | async-start | bytes 3670016 | tf_op jit(solution)/shard_map/all_to_all | solution.py:147
  62.1 1.2 copy-start.4
  63.3 108.9 %all-to-all-start.1 = ((bf16[64,16,896]{2,1,0:T(8,128)(2,1)}), bf16[64,16,896]{2,1,0:T(8,128)(2,1)S(1)}, u32[]{:S(2)}, u32[]{:S(2)}) async-start(bf16[64,16,896]{2,1,0:T(8,128)(2,1)} %bitcast.68), calls=%async_computation.1 | async-start | bytes 3670016 | tf_op jit(solution)/shard_map/all_to_all | solution.py:147
  68.8 44.9 %collective-permute-start.2 = (bf16[1024,896]{1,0:T(8,128)(2,1)}, bf16[1024,896]{1,0:T(8,128)(2,1)}, u32[]{:S(2)}, u32[]{:S(2)}) collective-permute-start(bf16[1024,896]{1,0:T(8,128)(2,1)} %bitcast.60), channel_id=1, source_target_pairs={{3,0},{0,1},{1,2},{2,3},{7,4},{4,5},{5,6},{6,7},{11,8},{8,9},{9,10... | collective-permute-start | bytes 5505032 | tf_op jit(solution)/shard_map/ppermute | solution.py:141
  70.4 73.5 %collective-permute-start = (bf16[1024,896]{1,0:T(8,128)(2,1)}, bf16[1024,896]{1,0:T(8,128)(2,1)}, u32[]{:S(2)}, u32[]{:S(2)}) collective-permute-start(bf16[1024,896]{1,0:T(8,128)(2,1)} %bitcast.61), channel_id=1, source_target_pairs={{1,0},{2,1},{3,2},{0,3},{5,4},{6,5},{7,6},{4,7},{9,8},{10,9},{11,1... | collective-permute-start | bytes 5505032 | tf_op jit(solution)/shard_map/ppermute | solution.py:141
  79.6 91.9 %collective-permute-start.4 = (bf16[896,768]{1,0:T(8,128)(2,1)}, bf16[896,768]{1,0:T(8,128)(2,1)}, u32[]{:S(2)}, u32[]{:S(2)}) collective-permute-start(bf16[896,768]{1,0:T(8,128)(2,1)} %get-tuple-element.14), channel_id=1, source_target_pairs={{1,0},{2,1},{3,2},{0,3},{5,4},{6,5},{7,6},{4,7},{9,8},{10,9},{11,1... | collective-permute-start | bytes 4128776 | tf_op jit(solution)/shard_map/ppermute | solution.py:141
  81.4 90.1 %collective-permute-start.5 = (bf16[896,768]{1,0:T(8,128)(2,1)}, bf16[896,768]{1,0:T(8,128)(2,1)}, u32[]{:S(2)}, u32[]{:S(2)}) collective-permute-start(bf16[896,768]{1,0:T(8,128)(2,1)} %get-tuple-element.15), channel_id=1, source_target_pairs={{2,0},{3,1},{0,2},{1,3},{6,4},{7,5},{4,6},{5,7},{10,8},{11,9},{8,1... | collective-permute-start | bytes 4128776 | tf_op jit(solution)/shard_map/ppermute | solution.py:141
  82.0 90.2 %collective-permute-start.6 = (bf16[896,768]{1,0:T(8,128)(2,1)}, bf16[896,768]{1,0:T(8,128)(2,1)}, u32[]{:S(2)}, u32[]{:S(2)}) collective-permute-start(bf16[896,768]{1,0:T(8,128)(2,1)} %get-tuple-element.16), channel_id=1, source_target_pairs={{3,0},{0,1},{1,2},{2,3},{7,4},{4,5},{5,6},{6,7},{11,8},{8,9},{9,10... | collective-permute-start | bytes 4128776 | tf_op jit(solution)/shard_map/ppermute | solution.py:141
  115.9 98.8 %collective-permute-start.3 = (bf16[512,896]{1,0:T(8,128)(2,1)}, bf16[512,896]{1,0:T(8,128)(2,1)S(1)}, u32[]{:S(2)}, u32[]{:S(2)}) collective-permute-start(bf16[512,896]{1,0:T(8,128)(2,1)} %slice.37), channel_id=1, source_target_pairs={{3,0},{0,1},{1,2},{2,3},{7,4},{4,5},{5,6},{6,7},{11,8},{8,9},{9,10... | collective-permute-start | bytes 2752520 | tf_op jit(solution)/shard_map/ppermute | solution.py:141
  146.1 68.6 %collective-permute-start.1 = (bf16[512,896]{1,0:T(8,128)(2,1)}, bf16[512,896]{1,0:T(8,128)(2,1)}, u32[]{:S(2)}, u32[]{:S(2)}) collective-permute-start(bf16[512,896]{1,0:T(8,128)(2,1)} %slice.36), channel_id=1, source_target_pairs={{1,0},{2,1},{3,2},{0,3},{5,4},{6,5},{7,6},{4,7},{9,8},{10,9},{11,1... | collective-permute-start | bytes 2752520 | tf_op jit(solution)/shard_map/ppermute | solution.py:141
  172.3 1.2 copy-start.2
  179.1 23.2 %collective-permute-start.7 = (bf16[1024,256]{1,0:T(8,128)(2,1)}, bf16[1024,256]{1,0:T(8,128)(2,1)S(1)}, u32[]{:S(2)}, u32[]{:S(2)}) collective-permute-start(bf16[1024,256]{1,0:T(8,128)(2,1)} %get-tuple-element.18), channel_id=1, source_target_pairs={{0,1},{1,2},{2,3},{3,0},{4,5},{5,6},{6,7},{7,4},{8,9},{9,10},{10,1... | collective-permute-start | bytes 1572872 | tf_op jit(solution)/shard_map/ppermute | solution.py:144
  181.8 32.9 %collective-permute-start.8 = (bf16[1024,256]{1,0:T(8,128)(2,1)}, bf16[1024,256]{1,0:T(8,128)(2,1)S(1)}, u32[]{:S(2)}, u32[]{:S(2)}) collective-permute-start(bf16[1024,256]{1,0:T(8,128)(2,1)} %get-tuple-element.19), channel_id=1, source_target_pairs={{0,2},{1,3},{2,0},{3,1},{4,6},{5,7},{6,4},{7,5},{8,10},{9,11},{10,... | collective-permute-start | bytes 1572872 | tf_op jit(solution)/shard_map/ppermute | solution.py:144
  183.8 30.9 %collective-permute-start.9 = (bf16[1024,256]{1,0:T(8,128)(2,1)}, bf16[1024,256]{1,0:T(8,128)(2,1)S(1)}, u32[]{:S(2)}, u32[]{:S(2)}) collective-permute-start(bf16[1024,256]{1,0:T(8,128)(2,1)} %get-tuple-element.20), channel_id=1, source_target_pairs={{0,3},{1,0},{2,1},{3,2},{4,7},{5,4},{6,5},{7,6},{8,11},{9,8},{10,9... | collective-permute-start | bytes 1572872 | tf_op jit(solution)/shard_map/ppermute | solution.py:144
  202.3 12.5 %copy-start.10 = (bf16[1024,256]{1,0:T(8,128)(2,1)}, bf16[1024,256]{1,0:T(8,128)(2,1)S(1)}, u32[]{:S(2)}) copy-start(bf16[1024,256]{1,0:T(8,128)(2,1)S(1)} %collective-permute-done.7.refs_1_) | copy-start | bytes 1572868
  214.7 0.8 copy-start.11
  214.7 1.0 copy-start.12
  214.7 1.3 copy-start.6
  222.2 15.0 %collective-permute-start.10 = (bf16[512,512]{1,0:T(8,128)(2,1)}, bf16[512,512]{1,0:T(8,128)(2,1)S(1)}, u32[]{:S(2)}, u32[]{:S(2)}) collective-permute-start(bf16[512,512]{1,0:T(8,128)(2,1)} %get-tuple-element.21.refs_0_), channel_id=1, source_target_pairs={{1,0},{2,1},{3,2},{0,3},{5,4},{6,5},{7,6},{4,7},{9,8},{10,9},{11,1... | collective-permute-start | bytes 1572872 | tf_op jit(solution)/shard_map/ppermute | solution.py:141
  223.8 16.2 %collective-permute-start.12 = (bf16[512,512]{1,0:T(8,128)(2,1)}, bf16[512,512]{1,0:T(8,128)(2,1)S(1)}, u32[]{:S(2)}, u32[]{:S(2)}) collective-permute-start(bf16[512,512]{1,0:T(8,128)(2,1)} %get-tuple-element.22.refs_3_), channel_id=1, source_target_pairs={{3,0},{0,1},{1,2},{2,3},{7,4},{4,5},{5,6},{6,7},{11,8},{8,9},{9,10... | collective-permute-start | bytes 1572872 | tf_op jit(solution)/shard_map/ppermute | solution.py:141
  224.2 27.0 %collective-permute-start.14 = (bf16[512,512]{1,0:T(8,128)(2,1)}, bf16[512,512]{1,0:T(8,128)(2,1)S(1)}, u32[]{:S(2)}, u32[]{:S(2)}) collective-permute-start(bf16[512,512]{1,0:T(8,128)(2,1)} %get-tuple-element.21.refs_0_), channel_id=1, source_target_pairs={{3,0},{0,1},{1,2},{2,3},{7,4},{4,5},{5,6},{6,7},{11,8},{8,9},{9,10... | collective-permute-start | bytes 1572872 | tf_op jit(solution)/shard_map/ppermute | solution.py:141
  224.4 26.9 %collective-permute-start.15 = (bf16[512,512]{1,0:T(8,128)(2,1)}, bf16[512,512]{1,0:T(8,128)(2,1)S(1)}, u32[]{:S(2)}, u32[]{:S(2)}) collective-permute-start(bf16[512,512]{1,0:T(8,128)(2,1)} %get-tuple-element.22.refs_3_), channel_id=1, source_target_pairs={{1,0},{2,1},{3,2},{0,3},{5,4},{6,5},{7,6},{4,7},{9,8},{10,9},{11,1... | collective-permute-start | bytes 1572872 | tf_op jit(solution)/shard_map/ppermute | solution.py:141
  227.5 3.4 copy-start.5
  232.3 11.0 %copy-start.7 = (bf16[512,896]{1,0:T(8,128)(2,1)S(1)}, bf16[512,896]{1,0:T(8,128)(2,1)}, u32[]{:S(2)}) copy-start(bf16[512,896]{1,0:T(8,128)(2,1)} %copy-done.6) | copy-start | bytes 2752516
  237.2 6.0 %copy-start.13 = (bf16[512,512]{1,0:T(8,128)(2,1)}, bf16[512,512]{1,0:T(8,128)(2,1)S(1)}, u32[]{:S(2)}) copy-start(bf16[512,512]{1,0:T(8,128)(2,1)S(1)} %collective-permute-done.10.refs_1_) | copy-start | bytes 1572868
  237.2 32.5 %collective-permute-start.11 = (bf16[512,512]{1,0:T(8,128)(2,1)S(1)}, bf16[512,512]{1,0:T(8,128)(2,1)S(1)}, u32[]{:S(2)}, u32[]{:S(2)}) collective-permute-start(bf16[512,512]{1,0:T(8,128)(2,1)S(1)} %collective-permute-done.10.refs_1_), channel_id=1, source_target_pairs={{1,0},{2,1},{3,2},{0,3},{5,4},{6,5},{7,6},{4,7},{9,8},{10,9},{11,1... | collective-permute-start | bytes 1572872 | tf_op jit(solution)/shard_map/ppermute | solution.py:141
  240.1 3.2 copy-start.14
  240.1 29.6 %collective-permute-start.13 = (bf16[512,512]{1,0:T(8,128)(2,1)S(1)}, bf16[512,512]{1,0:T(8,128)(2,1)}, u32[]{:S(2)}, u32[]{:S(2)}) collective-permute-start(bf16[512,512]{1,0:T(8,128)(2,1)S(1)} %collective-permute-done.12.refs_5_), channel_id=1, source_target_pairs={{3,0},{0,1},{1,2},{2,3},{7,4},{4,5},{5,6},{6,7},{11,8},{8,9},{9,10... | collective-permute-start | bytes 1572872 | tf_op jit(solution)/shard_map/ppermute | solution.py:141
  243.2 73.1 %collective-permute-start.20 = (bf16[1024,256]{1,0:T(8,128)(2,1)}, bf16[1024,256]{1,0:T(8,128)(2,1)}, u32[]{:S(2)}, u32[]{:S(2)}) collective-permute-start(bf16[1024,256]{1,0:T(8,128)(2,1)} %get-tuple-element.23), channel_id=1, source_target_pairs={{3,0},{0,1},{1,2},{2,3},{7,4},{4,5},{5,6},{6,7},{11,8},{8,9},{9,10... | collective-permute-start | bytes 1572872 | tf_op jit(solution)/shard_map/ppermute | solution.py:141
  251.3 1.9 copy-start.15
  251.3 58.2 %collective-permute-start.18 = (bf16[1024,256]{1,0:T(8,128)(2,1)}, bf16[1024,256]{1,0:T(8,128)(2,1)}, u32[]{:S(2)}, u32[]{:S(2)}) collective-permute-start(bf16[1024,256]{1,0:T(8,128)(2,1)} %get-tuple-element.23), channel_id=1, source_target_pairs={{2,0},{3,1},{0,2},{1,3},{6,4},{7,5},{4,6},{5,7},{10,8},{11,9},{8,1... | collective-permute-start | bytes 1572872 | tf_op jit(solution)/shard_map/ppermute | solution.py:141
  251.3 1.9 copy-start.16
  251.3 55.7 %collective-permute-start.16 = (bf16[1024,256]{1,0:T(8,128)(2,1)}, bf16[1024,256]{1,0:T(8,128)(2,1)}, u32[]{:S(2)}, u32[]{:S(2)}) collective-permute-start(bf16[1024,256]{1,0:T(8,128)(2,1)} %get-tuple-element.23), channel_id=1, source_target_pairs={{1,0},{2,1},{3,2},{0,3},{5,4},{6,5},{7,6},{4,7},{9,8},{10,9},{11,1... | collective-permute-start | bytes 1572872 | tf_op jit(solution)/shard_map/ppermute | solution.py:141
  269.7 0.8 copy-start.17
  275.9 10.5 %copy-start.9 = (bf16[512,512]{1,0:T(8,128)(2,1)S(1)}, bf16[512,512]{1,0:T(8,128)(2,1)}, u32[]{:S(2)}) copy-start(bf16[512,512]{1,0:T(8,128)(2,1)} %get-tuple-element.21.refs_0_) | copy-start | bytes 1572868
  275.9 10.5 %copy-start.8 = (bf16[512,512]{1,0:T(8,128)(2,1)S(1)}, bf16[512,512]{1,0:T(8,128)(2,1)}, u32[]{:S(2)}) copy-start(bf16[512,512]{1,0:T(8,128)(2,1)} %get-tuple-element.22.refs_3_) | copy-start | bytes 1572868
  275.9 61.0 %all-to-all-start.2 = ((bf16[64,16,896]{2,1,0:T(8,128)(2,1)}), bf16[64,16,896]{2,1,0:T(8,128)(2,1)S(1)}, u32[]{:S(2)}, u32[]{:S(2)}) async-start(bf16[64,16,896]{2,1,0:T(8,128)(2,1)} %bitcast.66), calls=%async_computation.2 | async-start | bytes 3670016 | tf_op jit(solution)/shard_map/all_to_all | solution.py:147
  302.3 2.2 copy-start.3
  308.8 15.0 %collective-permute-start.17 = (bf16[256,896]{1,0:T(8,128)(2,1)S(1)}, bf16[256,896]{1,0:T(8,128)(2,1)S(1)}, u32[]{:S(2)}, u32[]{:S(2)}) collective-permute-start(bf16[256,896]{1,0:T(8,128)(2,1)S(1)} %convolution_convert_fusion.5), channel_id=1, source_target_pairs={{0,1},{1,2},{2,3},{3,0},{4,5},{5,6},{6,7},{7,4},{8,9},{9,10},{10,1... | collective-permute-start | bytes 1376264 | tf_op jit(solution)/shard_map/ppermute | solution.py:144
  311.2 23.5 %collective-permute-start.19 = (bf16[256,896]{1,0:T(8,128)(2,1)S(1)}, bf16[256,896]{1,0:T(8,128)(2,1)S(1)}, u32[]{:S(2)}, u32[]{:S(2)}) collective-permute-start(bf16[256,896]{1,0:T(8,128)(2,1)S(1)} %convolution_convert_fusion.4), channel_id=1, source_target_pairs={{0,2},{1,3},{2,0},{3,1},{4,6},{5,7},{6,4},{7,5},{8,10},{9,11},{10,... | collective-permute-start | bytes 1376264 | tf_op jit(solution)/shard_map/ppermute | solution.py:144
  318.1 18.0 %collective-permute-start.21 = (bf16[256,896]{1,0:T(8,128)(2,1)S(1)}, bf16[256,896]{1,0:T(8,128)(2,1)S(1)}, u32[]{:S(2)}, u32[]{:S(2)}) collective-permute-start(bf16[256,896]{1,0:T(8,128)(2,1)S(1)} %convolution_convert_fusion.3), channel_id=1, source_target_pairs={{0,3},{1,0},{2,1},{3,2},{4,7},{5,4},{6,5},{7,6},{8,11},{9,8},{10,9... | collective-permute-start | bytes 1376264 | tf_op jit(solution)/shard_map/ppermute | solution.py:144
  334.8 3.7 %copy-start.1 = (bf16[256,896]{1,0:T(8,128)(2,1)S(1)}, bf16[256,896]{1,0:T(8,128)(2,1)}, u32[]{:S(2)}) copy-start(bf16[256,896]{1,0:T(8,128)(2,1)} %param.7) | copy-start | bytes 1376260

commit v4 on v3

--- a/solution.py
+++ b/solution.py
@@ -25,15 +25,12 @@
     step = pl.program_id(0)
     n, span, hid = gate.shape
     width = down.shape[1] // n
-    rows, columns = (lax.broadcasted_iota(jnp.int32, (span, span), d) for d in (0, 1))
-    same = (rows == columns).astype(BF)
     for k, out in zip(places, packed):
         q = lax.rem(me[0] + n - k, n)
         out[:, 0:hid] = gate[q]
         out[:, hid : 2 * hid] = up[q]
         start = pl.multiple_of(q * width + step * span, 128)
-        turned = mm(same, down[:, pl.ds(start, span)], ((1,), (1,)))
-        out[:, 2 * hid : 3 * hid] = turned.astype(BF)
+        out[:, 2 * hid : 3 * hid] = down[:, pl.ds(start, span)].T
 
 
 def partial_kernel(me, own, after, last, gate, up, out):

time: 340 us -> 340 us (level)
  no operation moved by 1% of the time
where the time goes in v4:
time: 340 us; the launch traced here: 338 us
  waiting for transfers between devices  152 us (45%)
  starting transfers between devices  84.1 us (25%)
  Pallas kernels  46.3 us (14%)
  matrix products  26.4 us (8%)
  local copies, waits for them, and re-layouts  25.2 us (7%)
  other arithmetic  3.74 us (1%)
    ppermute x16, waiting for transfers between devices, fetch(): return lax.ppermute(a, 'tp', [((i + k) % n_tp, i) for i in range(n_tp)])  70.1 us
    pallas_call x7, Pallas kernels, call(): pl.pallas_call(kernel, out_shape=[s for s, _ in outs], grid_spec=pltpu.Pr...  46.3 us
    ppermute x16, starting transfers between devices, fetch(): return lax.ppermute(a, 'tp', [((i + k) % n_tp, i) for i in range(n_tp)])  44.8 us
    all_to_all x3, waiting for transfers between devices, exchange(): lax.all_to_all(a.reshape(n_src, -1, quarter), 'ep', split_axis=0, concat_...  43.3 us
    ppermute x6, waiting for transfers between devices, give(): return lax.ppermute(a, 'tp', [(i, (i + k) % n_tp) for i in range(n_tp)])  38.4 us
    all_to_all x3, starting transfers between devices, exchange(): lax.all_to_all(a.reshape(n_src, -1, quarter), 'ep', split_axis=0, concat_...  28 us
    dot_general x10, matrix products, mm(): lax.dot_general(left, right, (dims, ((), ())), preferred_element_type=F32)  26.4 us
    ppermute x6, starting transfers between devices, give(): return lax.ppermute(a, 'tp', [(i, (i + k) % n_tp) for i in range(n_tp)])  11.3 us
  transfers between devices with their start and end apart: 25, of which 12 were waited for; matrix products, arithmetic and copies ran while one was open for 13% of the time, Pallas kernels for 12%

profile of v4, /device:TPU:2, one launch (start us, length us, event | category | flops | bytes accessed | tf_op | source)
XLA Modules:
  0.0 338.5 jit_solution(18349762932605176193)
XLA Ops:
  0.6 0.8 fusion.27
  1.6 0.8 multiply_add_fusion.1
  2.4 1.9 convolution_convert_fusion.2
  4.3 12.1 %all-to-all-start = ((bf16[64,16,896]{2,1,0:T(8,128)(2,1)}), bf16[64,16,896]{2,1,0:T(8,128)(2,1)S(1)}, u32[]{:S(2)}, u32[]{:S(2)}) async-start(bf16[64,16,896]{2,1,0:T(8,128)(2,1)} %bitcast.69), calls=%async_computation | async-start | bytes 3670016 | tf_op jit(solution)/shard_map/all_to_all | solution.py:144
  16.9 2.0 multiply_convert_fusion
  18.9 43.3 %all-to-all-done = bf16[64,16,896]{2,1,0:T(8,128)(2,1)S(1)} async-done(((bf16[64,16,896]{2,1,0:T(8,128)(2,1)}), bf16[64,16,896]{2,1,0:T(8,128)(2,1)S(1)}, u32[]{:S(2)}, u32[]{:S(2)}) %all-to-all-start) | async-done | bytes 1835040 | tf_op jit(solution)/shard_map/all_to_all | solution.py:144
  62.1 1.2 copy-done.4
  63.3 5.4 %all-to-all-start.1 = ((bf16[64,16,896]{2,1,0:T(8,128)(2,1)}), bf16[64,16,896]{2,1,0:T(8,128)(2,1)S(1)}, u32[]{:S(2)}, u32[]{:S(2)}) async-start(bf16[64,16,896]{2,1,0:T(8,128)(2,1)} %bitcast.68), calls=%async_computation.1 | async-start | bytes 3670016 | tf_op jit(solution)/shard_map/all_to_all | solution.py:144
  68.8 1.7 collective-permute-start.2
  70.4 1.7 collective-permute-start
  72.1 7.0 %shard_map.104 = (bf16[896,768]{1,0:T(8,128)(2,1)}, bf16[896,768]{1,0:T(8,128)(2,1)}, bf16[896,768]{1,0:T(8,128)(2,1)}) custom-call(s32[1]{0:T(128)} %bitcast.7.me, bf16[4,896,256]{2,1,0:T(8,128)(2,1)} %bitcast.52, bf16[4,896,256]{2,1,0:T(8,128)(2,1)} %bitcast.56, bf16[256,3584]{1,0:T(8,128)(2,1)} %bitcast.64), custom_call_target="tpu_custom_call" | custom-call | bytes 5505028 | tf_op jit(solution)/shard_map/pallas_call | solution.py:110
  79.0 1.8 collective-permute-start.4
  80.9 0.6 collective-permute-start.5
  81.5 1.0 collective-permute-start.6
  82.5 31.3 %collective-permute-done.2.last = bf16[1024,896]{1,0:T(8,128)(2,1)} collective-permute-done((bf16[1024,896]{1,0:T(8,128)(2,1)}, bf16[1024,896]{1,0:T(8,128)(2,1)}, u32[]{:S(2)}, u32[]{:S(2)}) %collective-permute-start.2) | collective-permute-done | bytes 1835040 | tf_op jit(solution)/shard_map/ppermute | solution.py:138
  113.7 2.2 slice.37
  115.9 28.1 %collective-permute-start.3 = (bf16[512,896]{1,0:T(8,128)(2,1)}, bf16[512,896]{1,0:T(8,128)(2,1)S(1)}, u32[]{:S(2)}, u32[]{:S(2)}) collective-permute-start(bf16[512,896]{1,0:T(8,128)(2,1)} %slice.37), channel_id=1, source_target_pairs={{3,0},{0,1},{1,2},{2,3},{7,4},{4,5},{5,6},{6,7},{11,8},{8,9},{9,10... | collective-permute-start | bytes 2752520 | tf_op jit(solution)/shard_map/ppermute | solution.py:138
  144.0 2.2 slice.36
  146.1 6.2 %shard_map.103.refs_0_.refs_6_ = bf16[896,768]{1,0:T(8,128)(2,1)} custom-call(s32[1]{0:T(128)} %bitcast.7.me, bf16[4,896,256]{2,1,0:T(8,128)(2,1)} %bitcast.53, bf16[4,896,256]{2,1,0:T(8,128)(2,1)} %bitcast.57, bf16[256,3584]{1,0:T(8,128)(2,1)} %bitcast.65), custom_call_target="tpu_custom_call" | custom-call | bytes 5505028 | tf_op jit(solution)/shard_map/pallas_call | solution.py:110
  152.3 19.1 %collective-permute-done.4.refs_1_.refs_7_ = bf16[896,768]{1,0:T(8,128)(2,1)} collective-permute-done((bf16[896,768]{1,0:T(8,128)(2,1)}, bf16[896,768]{1,0:T(8,128)(2,1)}, u32[]{:S(2)}, u32[]{:S(2)}) %collective-permute-start.4) | collective-permute-done | bytes 1376288 | tf_op jit(solution)/shard_map/ppermute | solution.py:138
  171.5 0.8 collective-permute-done.6.refs_3_.refs_8_
  172.3 1.2 copy-done.2
  173.5 5.6 %shard_map.105 = (f32[1024,256]{1,0:T(8,128)}, bf16[1024,256]{1,0:T(8,128)(2,1)}, bf16[1024,256]{1,0:T(8,128)(2,1)}, bf16[1024,256]{1,0:T(8,128)(2,1)}) custom-call(bf16[1024,896]{1,0:T(8,128)(2,1)} %bitcast.47, bf16[896,768]{1,0:T(8,128)(2,1)} %shard_map.103.refs_0_.refs_6_, bf16[896,768]{1,0:T(8,128)(2,1)} %collective-permute-done.4.refs_1_.refs_7_, ...), custom_call_target="tpu_custom_call" | custom-call | flops 1879048192 | bytes 7340032 | tf_op jit(solution)/shard_map/pallas_call | solution.py:110
  179.1 2.7 collective-permute-start.7
  181.8 2.0 collective-permute-start.8
  183.8 0.8 collective-permute-start.9
  184.6 8.0 %shard_map.102.partial = f32[1024,512]{1,0:T(8,128)} custom-call(s32[1]{0:T(128)} %bitcast.7.me, bf16[1024,896]{1,0:T(8,128)(2,1)} %bitcast.62, bf16[1024,896]{1,0:T(8,128)(2,1)} %collective-permute-done.after, bf16[1024,896]{1,0:T(8,128)(2,1)} %collective-permute-done.2.last, bf16[4,896,256]{2,1,0:T(8,128)(2,1)} %bitcast.54, bf16[4,896,256]{2,1,0:T(8,128)(2,1)} %bitcast.58), custom_call_target="tpu_custom_call" | custom-call | flops 2818572288 | bytes 9175044 | tf_op jit(solution)/shard_map/pallas_call | solution.py:110
  192.6 9.7 %collective-permute-done.7.refs_1_ = bf16[1024,256]{1,0:T(8,128)(2,1)S(1)} collective-permute-done((bf16[1024,256]{1,0:T(8,128)(2,1)}, bf16[1024,256]{1,0:T(8,128)(2,1)S(1)}, u32[]{:S(2)}, u32[]{:S(2)}) %collective-permute-start.7) | collective-permute-done | bytes 524320 | tf_op jit(solution)/shard_map/ppermute | solution.py:141
  202.3 12.5 %collective-permute-done.8.refs_2_ = bf16[1024,256]{1,0:T(8,128)(2,1)S(1)} collective-permute-done((bf16[1024,256]{1,0:T(8,128)(2,1)}, bf16[1024,256]{1,0:T(8,128)(2,1)S(1)}, u32[]{:S(2)}, u32[]{:S(2)}) %collective-permute-start.8) | collective-permute-done | bytes 524320 | tf_op jit(solution)/shard_map/ppermute | solution.py:141
  214.8 0.8 copy-done.11
  216.0 6.2 %shard_map.106 = (bf16[1024,256]{1,0:T(8,128)(2,1)}, bf16[512,512]{1,0:T(8,128)(2,1)}, bf16[512,512]{1,0:T(8,128)(2,1)}) custom-call(s32[1]{0:T(128)} %bitcast.7.me, bf16[512,896]{1,0:T(8,128)(2,1)} %collective-permute-done.1.far_a, bf16[512,896]{1,0:T(8,128)(2,1)} %copy-done.6, f32[1024,512]{1,0:T(8,128)} %shard_map.102.partial, ...), custom_call_target="tpu_custom_call" | custom-call | flops 939524096 | bytes 10223620 | tf_op jit(solution)/shard_map/pallas_call | solution.py:110
  222.2 1.6 collective-permute-start.10
  224.4 3.1 collective-permute-start.15
  227.5 3.4 broadcast_in_dim.58
  230.9 1.4 constant_dynamic-update-slice_fusion.4
  232.3 4.9 %collective-permute-done.10.refs_1_ = bf16[512,512]{1,0:T(8,128)(2,1)S(1)} collective-permute-done((bf16[512,512]{1,0:T(8,128)(2,1)}, bf16[512,512]{1,0:T(8,128)(2,1)S(1)}, u32[]{:S(2)}, u32[]{:S(2)}) %collective-permute-start.10) | collective-permute-done | bytes 524320 | tf_op jit(solution)/shard_map/ppermute | solution.py:138
  237.2 2.8 collective-permute-start.11
  240.1 3.2 constant_dynamic-update-slice_fusion.3
  243.2 2.6 maximum_dynamic-update-slice_fusion
  245.9 5.4 %collective-permute-done.14.refs_2_ = bf16[512,512]{1,0:T(8,128)(2,1)S(1)} collective-permute-done((bf16[512,512]{1,0:T(8,128)(2,1)}, bf16[512,512]{1,0:T(8,128)(2,1)S(1)}, u32[]{:S(2)}, u32[]{:S(2)}) %collective-permute-start.14) | collective-permute-done | bytes 524320 | tf_op jit(solution)/shard_map/ppermute | solution.py:138
  251.3 1.9 collective-permute-start.16
  253.2 8.0 %shard_map.107.refs_3_ = f32[1024,896]{1,0:T(8,128)} custom-call(bf16[512,512]{1,0:T(8,128)(2,1)} %get-tuple-element.21.refs_0_, bf16[512,512]{1,0:T(8,128)(2,1)} %copy-done.13, bf16[512,512]{1,0:T(8,128)(2,1)} %copy-done.15, bf16[512,512]{1,0:T(8,128)(2,1)} %get-tuple-element.22.refs_3_, bf16[512,512]{1,0:T(8,128)(2,1)} %copy-done.16, ...), custom_call_target="tpu_custom_call" | custom-call | flops 2818572288 | bytes 7274496 | tf_op jit(solution)/shard_map/pallas_call | solution.py:110
  261.1 8.5 %collective-permute-done.11.refs_0_ = bf16[512,512]{1,0:T(8,128)(2,1)S(1)} collective-permute-done((bf16[512,512]{1,0:T(8,128)(2,1)S(1)}, bf16[512,512]{1,0:T(8,128)(2,1)S(1)}, u32[]{:S(2)}, u32[]{:S(2)}) %collective-permute-start.11) | collective-permute-done | bytes 524320 | tf_op jit(solution)/shard_map/ppermute | solution.py:138
  269.7 0.8 copy-done.17
  270.5 5.5 %shard_map.108 = bf16[1024,896]{1,0:T(8,128)(2,1)} custom-call(bf16[512,512]{1,0:T(8,128)(2,1)} %copy-done.17, bf16[512,512]{1,0:T(8,128)(2,1)} %collective-permute-done.13.refs_1_, bf16[896,768]{1,0:T(8,128)(2,1)} %collective-permute-done.5.refs_2_, f32[1024,896]{1,0:T(8,128)} %shard_map.107.refs_3_), custom_call_target="tpu_custom_call" | custom-call | flops 939524096 | bytes 6094848 | tf_op jit(solution)/shard_map/pallas_call | solution.py:110
  275.9 10.4 %all-to-all-start.2 = ((bf16[64,16,896]{2,1,0:T(8,128)(2,1)}), bf16[64,16,896]{2,1,0:T(8,128)(2,1)S(1)}, u32[]{:S(2)}, u32[]{:S(2)}) async-start(bf16[64,16,896]{2,1,0:T(8,128)(2,1)} %bitcast.66), calls=%async_computation.2 | async-start | bytes 3670016 | tf_op jit(solution)/shard_map/all_to_all | solution.py:144
  286.5 2.9 constant_dynamic-update-slice_fusion.2
  289.4 6.5 %fusion.1 = bf16[1,3584,256]{2,1,0:T(8,128)(2,1)} fusion(bf16[1024,3584]{1,0:T(8,128)(2,1)} %constant_dynamic-update-slice_fusion.2, bf16[1024,512]{1,0:T(8,128)(2,1)S(1)} %constant_dynamic-update-slice_fusion), kind=kOutput, calls=%fused_computation.3 | convolution fusion | flops 1879965696 | bytes 9699328 | tf_op jit(solution)/shard_map/dot_general | solution.py:17
  295.9 6.4 %fusion = bf16[1,3584,256]{2,1,0:T(8,128)(2,1)} fusion(bf16[1024,3584]{1,0:T(8,128)(2,1)} %constant_dynamic-update-slice_fusion.2, bf16[1024,512]{1,0:T(8,128)(2,1)S(1)} %constant_dynamic-update-slice_fusion), kind=kOutput, calls=%fused_computation.2 | convolution fusion | flops 1879965696 | bytes 9699328 | tf_op jit(solution)/shard_map/dot_general | solution.py:17
  302.3 1.3 broadcast_in_dim.61
  303.6 0.8 copy-done.3
  304.5 2.5 fusion.3
  307.0 1.8 convolution_convert_fusion.5
  308.8 0.7 collective-permute-start.17
  309.5 1.8 convolution_convert_fusion.4
  311.2 5.1 %collective-permute-start.19 = (bf16[256,896]{1,0:T(8,128)(2,1)S(1)}, bf16[256,896]{1,0:T(8,128)(2,1)S(1)}, u32[]{:S(2)}, u32[]{:S(2)}) collective-permute-start(bf16[256,896]{1,0:T(8,128)(2,1)S(1)} %convolution_convert_fusion.4), channel_id=1, source_target_pairs={{0,2},{1,3},{2,0},{3,1},{4,6},{5,7},{6,4},{7,5},{8,10},{9,11},{10,... | collective-permute-start | bytes 1376264 | tf_op jit(solution)/shard_map/ppermute | solution.py:141
  316.3 1.8 convolution_convert_fusion.3
  318.2 5.6 %collective-permute-done.17 = bf16[256,896]{1,0:T(8,128)(2,1)S(1)} collective-permute-done((bf16[256,896]{1,0:T(8,128)(2,1)S(1)}, bf16[256,896]{1,0:T(8,128)(2,1)S(1)}, u32[]{:S(2)}, u32[]{:S(2)}) %collective-permute-start.17) | collective-permute-done | bytes 458784 | tf_op jit(solution)/shard_map/ppermute | solution.py:141
  323.8 0.8 bitcast_dynamic-update-slice_fusion.2
  324.6 10.2 %collective-permute-done.19 = bf16[256,896]{1,0:T(8,128)(2,1)S(1)} collective-permute-done((bf16[256,896]{1,0:T(8,128)(2,1)S(1)}, bf16[256,896]{1,0:T(8,128)(2,1)S(1)}, u32[]{:S(2)}, u32[]{:S(2)}) %collective-permute-start.19) | collective-permute-done | bytes 458784 | tf_op jit(solution)/shard_map/ppermute | solution.py:141
  334.8 0.8 bitcast_dynamic-update-slice_fusion.1
  335.6 0.5 collective-permute-done.21
  336.1 0.8 bitcast_dynamic-update-slice_fusion
  336.9 1.5 convolution_convert_fusion.7
  (63 shorter events, 1.9 us)
Async XLA Ops:
  0.6 1.8 copy-start
  4.3 12.2 %copy-start.18 = (f32[256,2]{0,1:T(2,128)S(1)}, f32[256,2]{0,1:T(2,128)}, u32[]{:S(2)}) copy-start(f32[256,2]{0,1:T(2,128)} %param.10) | copy-start | bytes 6148
  4.3 12.5 %copy-start.19 = (bf16[256,896]{1,0:T(8,128)(2,1)S(1)}, bf16[256,896]{1,0:T(8,128)(2,1)}, u32[]{:S(2)}) copy-start(bf16[256,896]{1,0:T(8,128)(2,1)} %param.8) | copy-start | bytes 1376260
  4.3 57.8 %all-to-all-start = ((bf16[64,16,896]{2,1,0:T(8,128)(2,1)}), bf16[64,16,896]{2,1,0:T(8,128)(2,1)S(1)}, u32[]{:S(2)}, u32[]{:S(2)}) async-start(bf16[64,16,896]{2,1,0:T(8,128)(2,1)} %bitcast.69), calls=%async_computation | async-start | bytes 3670016 | tf_op jit(solution)/shard_map/all_to_all | solution.py:144
  62.1 1.2 copy-start.4
  63.3 108.9 %all-to-all-start.1 = ((bf16[64,16,896]{2,1,0:T(8,128)(2,1)}), bf16[64,16,896]{2,1,0:T(8,128)(2,1)S(1)}, u32[]{:S(2)}, u32[]{:S(2)}) async-start(bf16[64,16,896]{2,1,0:T(8,128)(2,1)} %bitcast.68), calls=%async_computation.1 | async-start | bytes 3670016 | tf_op jit(solution)/shard_map/all_to_all | solution.py:144
  68.8 44.9 %collective-permute-start.2 = (bf16[1024,896]{1,0:T(8,128)(2,1)}, bf16[1024,896]{1,0:T(8,128)(2,1)}, u32[]{:S(2)}, u32[]{:S(2)}) collective-permute-start(bf16[1024,896]{1,0:T(8,128)(2,1)} %bitcast.60), channel_id=1, source_target_pairs={{3,0},{0,1},{1,2},{2,3},{7,4},{4,5},{5,6},{6,7},{11,8},{8,9},{9,10... | collective-permute-start | bytes 5505032 | tf_op jit(solution)/shard_map/ppermute | solution.py:138
  70.4 73.5 %collective-permute-start = (bf16[1024,896]{1,0:T(8,128)(2,1)}, bf16[1024,896]{1,0:T(8,128)(2,1)}, u32[]{:S(2)}, u32[]{:S(2)}) collective-permute-start(bf16[1024,896]{1,0:T(8,128)(2,1)} %bitcast.61), channel_id=1, source_target_pairs={{1,0},{2,1},{3,2},{0,3},{5,4},{6,5},{7,6},{4,7},{9,8},{10,9},{11,1... | collective-permute-start | bytes 5505032 | tf_op jit(solution)/shard_map/ppermute | solution.py:138
  79.0 92.4 %collective-permute-start.4 = (bf16[896,768]{1,0:T(8,128)(2,1)}, bf16[896,768]{1,0:T(8,128)(2,1)}, u32[]{:S(2)}, u32[]{:S(2)}) collective-permute-start(bf16[896,768]{1,0:T(8,128)(2,1)} %get-tuple-element.14), channel_id=1, source_target_pairs={{1,0},{2,1},{3,2},{0,3},{5,4},{6,5},{7,6},{4,7},{9,8},{10,9},{11,1... | collective-permute-start | bytes 4128776 | tf_op jit(solution)/shard_map/ppermute | solution.py:138
  80.9 90.6 %collective-permute-start.5 = (bf16[896,768]{1,0:T(8,128)(2,1)}, bf16[896,768]{1,0:T(8,128)(2,1)}, u32[]{:S(2)}, u32[]{:S(2)}) collective-permute-start(bf16[896,768]{1,0:T(8,128)(2,1)} %get-tuple-element.15), channel_id=1, source_target_pairs={{2,0},{3,1},{0,2},{1,3},{6,4},{7,5},{4,6},{5,7},{10,8},{11,9},{8,1... | collective-permute-start | bytes 4128776 | tf_op jit(solution)/shard_map/ppermute | solution.py:138
  81.5 90.8 %collective-permute-start.6 = (bf16[896,768]{1,0:T(8,128)(2,1)}, bf16[896,768]{1,0:T(8,128)(2,1)}, u32[]{:S(2)}, u32[]{:S(2)}) collective-permute-start(bf16[896,768]{1,0:T(8,128)(2,1)} %get-tuple-element.16), channel_id=1, source_target_pairs={{3,0},{0,1},{1,2},{2,3},{7,4},{4,5},{5,6},{6,7},{11,8},{8,9},{9,10... | collective-permute-start | bytes 4128776 | tf_op jit(solution)/shard_map/ppermute | solution.py:138
  115.9 98.8 %collective-permute-start.3 = (bf16[512,896]{1,0:T(8,128)(2,1)}, bf16[512,896]{1,0:T(8,128)(2,1)S(1)}, u32[]{:S(2)}, u32[]{:S(2)}) collective-permute-start(bf16[512,896]{1,0:T(8,128)(2,1)} %slice.37), channel_id=1, source_target_pairs={{3,0},{0,1},{1,2},{2,3},{7,4},{4,5},{5,6},{6,7},{11,8},{8,9},{9,10... | collective-permute-start | bytes 2752520 | tf_op jit(solution)/shard_map/ppermute | solution.py:138
  146.1 68.6 %collective-permute-start.1 = (bf16[512,896]{1,0:T(8,128)(2,1)}, bf16[512,896]{1,0:T(8,128)(2,1)}, u32[]{:S(2)}, u32[]{:S(2)}) collective-permute-start(bf16[512,896]{1,0:T(8,128)(2,1)} %slice.36), channel_id=1, source_target_pairs={{1,0},{2,1},{3,2},{0,3},{5,4},{6,5},{7,6},{4,7},{9,8},{10,9},{11,1... | collective-permute-start | bytes 2752520 | tf_op jit(solution)/shard_map/ppermute | solution.py:138
  172.3 1.2 copy-start.2
  179.1 23.2 %collective-permute-start.7 = (bf16[1024,256]{1,0:T(8,128)(2,1)}, bf16[1024,256]{1,0:T(8,128)(2,1)S(1)}, u32[]{:S(2)}, u32[]{:S(2)}) collective-permute-start(bf16[1024,256]{1,0:T(8,128)(2,1)} %get-tuple-element.18), channel_id=1, source_target_pairs={{0,1},{1,2},{2,3},{3,0},{4,5},{5,6},{6,7},{7,4},{8,9},{9,10},{10,1... | collective-permute-start | bytes 1572872 | tf_op jit(solution)/shard_map/ppermute | solution.py:141
  181.8 32.9 %collective-permute-start.8 = (bf16[1024,256]{1,0:T(8,128)(2,1)}, bf16[1024,256]{1,0:T(8,128)(2,1)S(1)}, u32[]{:S(2)}, u32[]{:S(2)}) collective-permute-start(bf16[1024,256]{1,0:T(8,128)(2,1)} %get-tuple-element.19), channel_id=1, source_target_pairs={{0,2},{1,3},{2,0},{3,1},{4,6},{5,7},{6,4},{7,5},{8,10},{9,11},{10,... | collective-permute-start | bytes 1572872 | tf_op jit(solution)/shard_map/ppermute | solution.py:141
  183.8 30.9 %collective-permute-start.9 = (bf16[1024,256]{1,0:T(8,128)(2,1)}, bf16[1024,256]{1,0:T(8,128)(2,1)S(1)}, u32[]{:S(2)}, u32[]{:S(2)}) collective-permute-start(bf16[1024,256]{1,0:T(8,128)(2,1)} %get-tuple-element.20), channel_id=1, source_target_pairs={{0,3},{1,0},{2,1},{3,2},{4,7},{5,4},{6,5},{7,6},{8,11},{9,8},{10,9... | collective-permute-start | bytes 1572872 | tf_op jit(solution)/shard_map/ppermute | solution.py:141
  202.3 12.5 %copy-start.10 = (bf16[1024,256]{1,0:T(8,128)(2,1)}, bf16[1024,256]{1,0:T(8,128)(2,1)S(1)}, u32[]{:S(2)}) copy-start(bf16[1024,256]{1,0:T(8,128)(2,1)S(1)} %collective-permute-done.7.refs_1_) | copy-start | bytes 1572868
  214.7 0.8 copy-start.11
  214.7 1.0 copy-start.12
  214.7 1.3 copy-start.6
  222.2 15.0 %collective-permute-start.10 = (bf16[512,512]{1,0:T(8,128)(2,1)}, bf16[512,512]{1,0:T(8,128)(2,1)S(1)}, u32[]{:S(2)}, u32[]{:S(2)}) collective-permute-start(bf16[512,512]{1,0:T(8,128)(2,1)} %get-tuple-element.21.refs_0_), channel_id=1, source_target_pairs={{1,0},{2,1},{3,2},{0,3},{5,4},{6,5},{7,6},{4,7},{9,8},{10,9},{11,1... | collective-permute-start | bytes 1572872 | tf_op jit(solution)/shard_map/ppermute | solution.py:138
  223.8 16.2 %collective-permute-start.12 = (bf16[512,512]{1,0:T(8,128)(2,1)}, bf16[512,512]{1,0:T(8,128)(2,1)S(1)}, u32[]{:S(2)}, u32[]{:S(2)}) collective-permute-start(bf16[512,512]{1,0:T(8,128)(2,1)} %get-tuple-element.22.refs_3_), channel_id=1, source_target_pairs={{3,0},{0,1},{1,2},{2,3},{7,4},{4,5},{5,6},{6,7},{11,8},{8,9},{9,10... | collective-permute-start | bytes 1572872 | tf_op jit(solution)/shard_map/ppermute | solution.py:138
  224.2 27.0 %collective-permute-start.14 = (bf16[512,512]{1,0:T(8,128)(2,1)}, bf16[512,512]{1,0:T(8,128)(2,1)S(1)}, u32[]{:S(2)}, u32[]{:S(2)}) collective-permute-start(bf16[512,512]{1,0:T(8,128)(2,1)} %get-tuple-element.21.refs_0_), channel_id=1, source_target_pairs={{3,0},{0,1},{1,2},{2,3},{7,4},{4,5},{5,6},{6,7},{11,8},{8,9},{9,10... | collective-permute-start | bytes 1572872 | tf_op jit(solution)/shard_map/ppermute | solution.py:138
  224.4 26.9 %collective-permute-start.15 = (bf16[512,512]{1,0:T(8,128)(2,1)}, bf16[512,512]{1,0:T(8,128)(2,1)S(1)}, u32[]{:S(2)}, u32[]{:S(2)}) collective-permute-start(bf16[512,512]{1,0:T(8,128)(2,1)} %get-tuple-element.22.refs_3_), channel_id=1, source_target_pairs={{1,0},{2,1},{3,2},{0,3},{5,4},{6,5},{7,6},{4,7},{9,8},{10,9},{11,1... | collective-permute-start | bytes 1572872 | tf_op jit(solution)/shard_map/ppermute | solution.py:138
  227.5 3.4 copy-start.5
  232.3 11.0 %copy-start.7 = (bf16[512,896]{1,0:T(8,128)(2,1)S(1)}, bf16[512,896]{1,0:T(8,128)(2,1)}, u32[]{:S(2)}) copy-start(bf16[512,896]{1,0:T(8,128)(2,1)} %copy-done.6) | copy-start | bytes 2752516
  237.2 6.0 %copy-start.13 = (bf16[512,512]{1,0:T(8,128)(2,1)}, bf16[512,512]{1,0:T(8,128)(2,1)S(1)}, u32[]{:S(2)}) copy-start(bf16[512,512]{1,0:T(8,128)(2,1)S(1)} %collective-permute-done.10.refs_1_) | copy-start | bytes 1572868
  237.2 32.5 %collective-permute-start.11 = (bf16[512,512]{1,0:T(8,128)(2,1)S(1)}, bf16[512,512]{1,0:T(8,128)(2,1)S(1)}, u32[]{:S(2)}, u32[]{:S(2)}) collective-permute-start(bf16[512,512]{1,0:T(8,128)(2,1)S(1)} %collective-permute-done.10.refs_1_), channel_id=1, source_target_pairs={{1,0},{2,1},{3,2},{0,3},{5,4},{6,5},{7,6},{4,7},{9,8},{10,9},{11,1... | collective-permute-start | bytes 1572872 | tf_op jit(solution)/shard_map/ppermute | solution.py:138
  240.1 3.2 copy-start.14
  240.1 29.6 %collective-permute-start.13 = (bf16[512,512]{1,0:T(8,128)(2,1)S(1)}, bf16[512,512]{1,0:T(8,128)(2,1)}, u32[]{:S(2)}, u32[]{:S(2)}) collective-permute-start(bf16[512,512]{1,0:T(8,128)(2,1)S(1)} %collective-permute-done.12.refs_5_), channel_id=1, source_target_pairs={{3,0},{0,1},{1,2},{2,3},{7,4},{4,5},{5,6},{6,7},{11,8},{8,9},{9,10... | collective-permute-start | bytes 1572872 | tf_op jit(solution)/shard_map/ppermute | solution.py:138
  243.2 73.1 %collective-permute-start.20 = (bf16[1024,256]{1,0:T(8,128)(2,1)}, bf16[1024,256]{1,0:T(8,128)(2,1)}, u32[]{:S(2)}, u32[]{:S(2)}) collective-permute-start(bf16[1024,256]{1,0:T(8,128)(2,1)} %get-tuple-element.23), channel_id=1, source_target_pairs={{3,0},{0,1},{1,2},{2,3},{7,4},{4,5},{5,6},{6,7},{11,8},{8,9},{9,10... | collective-permute-start | bytes 1572872 | tf_op jit(solution)/shard_map/ppermute | solution.py:138
  251.3 1.9 copy-start.15
  251.3 58.2 %collective-permute-start.18 = (bf16[1024,256]{1,0:T(8,128)(2,1)}, bf16[1024,256]{1,0:T(8,128)(2,1)}, u32[]{:S(2)}, u32[]{:S(2)}) collective-permute-start(bf16[1024,256]{1,0:T(8,128)(2,1)} %get-tuple-element.23), channel_id=1, source_target_pairs={{2,0},{3,1},{0,2},{1,3},{6,4},{7,5},{4,6},{5,7},{10,8},{11,9},{8,1... | collective-permute-start | bytes 1572872 | tf_op jit(solution)/shard_map/ppermute | solution.py:138
  251.3 1.9 copy-start.16
  251.3 55.7 %collective-permute-start.16 = (bf16[1024,256]{1,0:T(8,128)(2,1)}, bf16[1024,256]{1,0:T(8,128)(2,1)}, u32[]{:S(2)}, u32[]{:S(2)}) collective-permute-start(bf16[1024,256]{1,0:T(8,128)(2,1)} %get-tuple-element.23), channel_id=1, source_target_pairs={{1,0},{2,1},{3,2},{0,3},{5,4},{6,5},{7,6},{4,7},{9,8},{10,9},{11,1... | collective-permute-start | bytes 1572872 | tf_op jit(solution)/shard_map/ppermute | solution.py:138
  269.7 0.8 copy-start.17
  275.9 10.5 %copy-start.9 = (bf16[512,512]{1,0:T(8,128)(2,1)S(1)}, bf16[512,512]{1,0:T(8,128)(2,1)}, u32[]{:S(2)}) copy-start(bf16[512,512]{1,0:T(8,128)(2,1)} %get-tuple-element.21.refs_0_) | copy-start | bytes 1572868
  275.9 10.5 %copy-start.8 = (bf16[512,512]{1,0:T(8,128)(2,1)S(1)}, bf16[512,512]{1,0:T(8,128)(2,1)}, u32[]{:S(2)}) copy-start(bf16[512,512]{1,0:T(8,128)(2,1)} %get-tuple-element.22.refs_3_) | copy-start | bytes 1572868
  275.9 61.0 %all-to-all-start.2 = ((bf16[64,16,896]{2,1,0:T(8,128)(2,1)}), bf16[64,16,896]{2,1,0:T(8,128)(2,1)S(1)}, u32[]{:S(2)}, u32[]{:S(2)}) async-start(bf16[64,16,896]{2,1,0:T(8,128)(2,1)} %bitcast.66), calls=%async_computation.2 | async-start | bytes 3670016 | tf_op jit(solution)/shard_map/all_to_all | solution.py:144
  302.3 2.2 copy-start.3
  308.8 15.0 %collective-permute-start.17 = (bf16[256,896]{1,0:T(8,128)(2,1)S(1)}, bf16[256,896]{1,0:T(8,128)(2,1)S(1)}, u32[]{:S(2)}, u32[]{:S(2)}) collective-permute-start(bf16[256,896]{1,0:T(8,128)(2,1)S(1)} %convolution_convert_fusion.5), channel_id=1, source_target_pairs={{0,1},{1,2},{2,3},{3,0},{4,5},{5,6},{6,7},{7,4},{8,9},{9,10},{10,1... | collective-permute-start | bytes 1376264 | tf_op jit(solution)/shard_map/ppermute | solution.py:141
  311.2 23.5 %collective-permute-start.19 = (bf16[256,896]{1,0:T(8,128)(2,1)S(1)}, bf16[256,896]{1,0:T(8,128)(2,1)S(1)}, u32[]{:S(2)}, u32[]{:S(2)}) collective-permute-start(bf16[256,896]{1,0:T(8,128)(2,1)S(1)} %convolution_convert_fusion.4), channel_id=1, source_target_pairs={{0,2},{1,3},{2,0},{3,1},{4,6},{5,7},{6,4},{7,5},{8,10},{9,11},{10,... | collective-permute-start | bytes 1376264 | tf_op jit(solution)/shard_map/ppermute | solution.py:141
  318.1 18.0 %collective-permute-start.21 = (bf16[256,896]{1,0:T(8,128)(2,1)S(1)}, bf16[256,896]{1,0:T(8,128)(2,1)S(1)}, u32[]{:S(2)}, u32[]{:S(2)}) collective-permute-start(bf16[256,896]{1,0:T(8,128)(2,1)S(1)} %convolution_convert_fusion.3), channel_id=1, source_target_pairs={{0,3},{1,0},{2,1},{3,2},{4,7},{5,4},{6,5},{7,6},{8,11},{9,8},{10,9... | collective-permute-start | bytes 1376264 | tf_op jit(solution)/shard_map/ppermute | solution.py:141
  334.8 3.7 %copy-start.1 = (bf16[256,896]{1,0:T(8,128)(2,1)S(1)}, bf16[256,896]{1,0:T(8,128)(2,1)}, u32[]{:S(2)}) copy-start(bf16[256,896]{1,0:T(8,128)(2,1)} %param.7) | copy-start | bytes 1376260
